TPU v7x, 32 devices: a whole 2x2x4 slice. The times are simulated.
32 devices in a mesh: expert: 16 (over z, y, x), tensor: 2 (over core).
Axes of the slice: x: 2, y: 2, z: 4, core: 2. Of those that a mesh axis runs over, the one named last changes fastest.
Arguments:
- tokens: bfloat16 [8192, 2048], P('expert'), may hold values from -6 to 6
- lengths: int32 [16], P('expert'), may hold values from 256 to 512, as said below
- routes: int32 [8192, 8], P('expert'), may hold values from 0 to 15, all different within a row; in each aligned block of 512 rows (0 to 511, 512 to 1023, ...) at most 288 rows name the same one
- attn_gain: float32 [2048], P('expert'), may hold values from 0.5 to 1.5
- w_query: float32 [2048, 2048], P('expert', 'tensor'), may hold values from -0.125 to 0.125
- w_key: float32 [2048, 2048], P('expert', 'tensor'), may hold values from -0.125 to 0.125
- w_value: float32 [2048, 2048], P('expert', 'tensor'), may hold values from -0.125 to 0.125
- query_gain: float32 [128], P('expert'), may hold values from 0.5 to 1.5
- key_gain: float32 [128], P('expert'), may hold values from 0.5 to 1.5
- w_out: float32 [2048, 2048], P('expert', 'tensor'), may hold values from -0.5 to 0.5
- ffn_gain: float32 [2048], P('expert'), may hold values from 0.5 to 1.5
- w_router: float32 [2048, 16], P('expert'), may hold values from -0.0625 to 0.0625
- w_gate: float32 [16, 2048, 1024], P('expert', None, 'tensor'), may hold values from -0.125 to 0.125
- w_up: float32 [16, 2048, 1024], P('expert', None, 'tensor'), may hold values from -0.125 to 0.125
- w_down: float32 [16, 1024, 2048], P('expert', 'tensor'), may hold values from -1 to 1
- cotangent: bfloat16 [8192, 2048], P('expert'), may hold values from -6 to 6
Outputs:
- output: bfloat16 [8192, 2048], P('expert')
- input_grad: bfloat16 [8192, 2048], P('expert')
- grad_attn_gain: float32 [2048], P('expert')
- grad_query: float32 [2048, 2048], P('expert', 'tensor')
- grad_key: float32 [2048, 2048], P('expert', 'tensor')
- grad_value: float32 [2048, 2048], P('expert', 'tensor')
- grad_query_gain: float32 [128], P('expert')
- grad_key_gain: float32 [128], P('expert')
- grad_out: float32 [2048, 2048], P('expert', 'tensor')
- grad_ffn_gain: float32 [2048], P('expert')
- grad_router: float32 [2048, 16], P('expert')
- grad_gate: float32 [16, 2048, 1024], P('expert', None, 'tensor')
- grad_up: float32 [16, 2048, 1024], P('expert', None, 'tensor')
- grad_down: float32 [16, 1024, 2048], P('expert', 'tensor')
Inputs may be any that keep to these rules, and one draw needn't show every extreme that they name: `lengths`: each index of expert holds one sequence; at least one sequence fills all 512 slots. `routes`: within the rows of one sequence no expert is named by more than 288 rows, a bound that some block reaches.
All inputs are finite; a program needn't handle non-finite values.
Results may differ from a plain program's by a relative error of at most 0.02.
Values may be sent and summed in bfloat16 or wider, within the bound.
A program may use at most 384 MiB of HBM per device.

v0:
```python
import math

import jax
import jax.numpy as jnp
from jax import lax
from jax.sharding import PartitionSpec as P

D = 2048
HD = 128
TOP = 8
SEQ = 512


EPSILON = 1e-06
ROPE_BASE = 10000.0
NEG_BIG = -1e30


def rope_tables(seq_len, head_dim):
    half_dim = head_dim // 2
    inverse = ROPE_BASE ** (-(jnp.arange(half_dim).astype(jnp.float32) * 2.0 / head_dim))
    angles = jnp.arange(seq_len).astype(jnp.float32)[:, None] * inverse[None, :]
    return (jnp.cos(angles), jnp.sin(angles))


def rotate(values, cosine, sine_tab):
    half_dim = values.shape[-1] // 2
    lower_half = values[..., :half_dim]
    upper_half = values[..., half_dim:]
    cos_b = cosine[:, None, :]
    sin_b = sine_tab[:, None, :]
    return jnp.concatenate(
        [lower_half * cos_b - upper_half * sin_b, upper_half * cos_b + lower_half * sin_b], axis=-1
    )


def rotate_back(grads_in, cosine, sine_tab):
    half_dim = grads_in.shape[-1] // 2
    lower_half = grads_in[..., :half_dim]
    upper_half = grads_in[..., half_dim:]
    cos_b = cosine[:, None, :]
    sin_b = sine_tab[:, None, :]
    return jnp.concatenate(
        [lower_half * cos_b + upper_half * sin_b, upper_half * cos_b - lower_half * sin_b], axis=-1
    )


def norm_stats(values):
    inverse = lax.rsqrt(jnp.mean(values * values, axis=-1, keepdims=True) + EPSILON)
    return (values * inverse, inverse)


def norm_back(grad_normed, normed, inverse):
    return inverse * (grad_normed - normed * jnp.mean(grad_normed * normed, axis=-1, keepdims=True))


def slot_tables(block_routes, experts, capacity):
    seq_len, top_count = block_routes.shape
    expert_ids = jnp.arange(experts)
    match_hot = block_routes[:, :, None] == expert_ids[None, None, :]
    hit_count = jnp.sum(match_hot.astype(jnp.int32), axis=1)
    before = jnp.cumsum(hit_count, axis=0) - hit_count
    slot_index = jnp.sum(jnp.where(match_hot, before[:, None, :], 0), axis=2)
    flat_slot = block_routes * capacity + slot_index
    route_ids = jnp.arange(seq_len * top_count)
    slot_owner = (
        jnp.full((experts * capacity,), seq_len * top_count, jnp.int32)
        .at[flat_slot.reshape(-1)]
        .set(route_ids)
    )
    return (match_hot, flat_slot, slot_owner)


def to_experts(arrived, sources, per_device):
    capacity, width = (arrived.shape[1], arrived.shape[2])
    return (
        arrived.reshape(sources, per_device, capacity, width)
        .transpose(1, 0, 2, 3)
        .reshape(per_device, sources * capacity, width)
    )


def to_sources(rows, sources, capacity):
    per_device, width = (rows.shape[0], rows.shape[2])
    return (
        rows.reshape(per_device, sources, capacity, width)
        .transpose(1, 0, 2, 3)
        .reshape(sources * per_device, capacity, width)
    )


def contract_rows(left_mat, right_mat):
    return lax.dot_general(
        left_mat, right_mat, (((0,), (0,)), ((), ())), preferred_element_type=jnp.float32
    )


def contract_cols(left_mat, right_mat):
    return lax.dot_general(
        left_mat, right_mat, (((1,), (1,)), ((), ())), preferred_element_type=jnp.float32
    )


def local(
    tokens,
    lengths,
    routes,
    attn_gain,
    w_query,
    w_key,
    w_value,
    query_gain,
    key_gain,
    w_out,
    ffn_gain,
    w_router,
    w_gate,
    w_up,
    w_down,
    cotangent,
):
    sources = lax.axis_size("expert")
    experts = w_router.shape[1]
    per_device = w_gate.shape[0]
    capacity = SEQ * TOP * 9 // (8 * experts)
    scale = 1.0 / math.sqrt(HD)
    gathered = (
        lax.all_gather(w_query.astype(jnp.bfloat16), "expert", axis=0, tiled=True),
        lax.all_gather(w_key.astype(jnp.bfloat16), "expert", axis=0, tiled=True),
        lax.all_gather(w_value.astype(jnp.bfloat16), "expert", axis=0, tiled=True),
        lax.all_gather(w_out.astype(jnp.bfloat16), "expert", axis=0, tiled=True),
        lax.all_gather(w_router.astype(jnp.bfloat16), "expert", axis=0, tiled=True),
        lax.all_gather(attn_gain.astype(jnp.bfloat16), "expert", axis=0, tiled=True),
        lax.all_gather(ffn_gain.astype(jnp.bfloat16), "expert", axis=0, tiled=True),
        lax.all_gather(query_gain.astype(jnp.bfloat16), "expert", axis=0, tiled=True),
        lax.all_gather(key_gain.astype(jnp.bfloat16), "expert", axis=0, tiled=True),
    )
    wq_full, wk_full, wv_full, wo_full, router_full = (
        gathered[0],
        gathered[1],
        gathered[2],
        gathered[3],
        gathered[4],
    )
    gain_one = gathered[5].astype(jnp.float32)
    gain_two = gathered[6].astype(jnp.float32)
    gain_query = gathered[7].astype(jnp.float32)
    gain_key = gathered[8].astype(jnp.float32)
    heads_here = wq_full.shape[1] // HD
    cosine, sine_tab = rope_tables(SEQ, HD)
    resid_zero = tokens.astype(jnp.float32)
    normed_one, inverse_one = norm_stats(resid_zero)
    attn_in = (normed_one * gain_one).astype(jnp.bfloat16)
    query_lin = jnp.dot(attn_in, wq_full, preferred_element_type=jnp.float32).reshape(
        SEQ, heads_here, HD
    )
    key_lin = jnp.dot(attn_in, wk_full, preferred_element_type=jnp.float32).reshape(
        SEQ, heads_here, HD
    )
    values_b = (
        jnp.dot(attn_in, wv_full, preferred_element_type=jnp.float32)
        .astype(jnp.bfloat16)
        .reshape(SEQ, heads_here, HD)
    )
    query_hat, query_inv = norm_stats(query_lin)
    key_hat, key_inv = norm_stats(key_lin)
    queries = rotate(query_hat * gain_query, cosine, sine_tab).astype(jnp.bfloat16)
    keys_rot = rotate(key_hat * gain_key, cosine, sine_tab).astype(jnp.bfloat16)
    allowed = jnp.arange(SEQ) < lengths[0]

    def masked_scores():
        scores = (
            jnp.einsum("qhd,khd->hqk", queries, keys_rot, preferred_element_type=jnp.float32)
            * scale
        )
        return jnp.where(allowed[None, None, :], scores, NEG_BIG)

    masked = masked_scores()
    top_score = jnp.max(masked, axis=-1, keepdims=True)
    expo_vals = jnp.exp(masked - top_score)
    totals = jnp.sum(expo_vals, axis=-1, keepdims=True)
    probs_low = (expo_vals / totals).astype(jnp.bfloat16)
    log_total = top_score + jnp.log(totals)
    mixed = (
        jnp.einsum("hqk,khd->qhd", probs_low, values_b, preferred_element_type=jnp.float32)
        .reshape(SEQ, heads_here * HD)
        .astype(jnp.bfloat16)
    )
    attn_part = contract_cols(mixed, wo_full)
    resid_one = resid_zero + lax.psum(attn_part, "tensor")
    normed_two, inverse_two = norm_stats(resid_one)
    ffn_in = (normed_two * gain_two).astype(jnp.bfloat16)
    logits = jnp.dot(ffn_in, router_full, preferred_element_type=jnp.float32)
    route_hot, flat_slot, slot_owner = slot_tables(routes, experts, capacity)
    chosen = jnp.sum(jnp.where(route_hot, logits[:, None, :], 0.0), axis=2)
    gates = jax.nn.softmax(chosen, axis=1)
    token_of = slot_owner // TOP
    padded_in = jnp.concatenate([ffn_in, jnp.zeros((1, D), jnp.bfloat16)], axis=0)
    send_rows = padded_in[token_of].reshape(experts, capacity, D)
    arrived = lax.all_to_all(send_rows, "expert", split_axis=0, concat_axis=0, tiled=True)
    expert_rows = to_experts(arrived, sources, per_device)
    wg_low = w_gate.astype(jnp.bfloat16)
    wu_low = w_up.astype(jnp.bfloat16)
    wd_low = w_down.astype(jnp.bfloat16)
    gate_lin = jnp.einsum("erd,edf->erf", expert_rows, wg_low, preferred_element_type=jnp.float32)
    up_lin = jnp.einsum("erd,edf->erf", expert_rows, wu_low, preferred_element_type=jnp.float32)
    sigmoid_gate = jax.nn.sigmoid(gate_lin)
    activated = gate_lin * sigmoid_gate
    hidden = (activated * up_lin).astype(jnp.bfloat16)
    partial_value = jnp.einsum("erf,efd->erd", hidden, wd_low, preferred_element_type=jnp.float32)
    partial_low = partial_value.astype(jnp.bfloat16).astype(jnp.float32)
    summed = lax.psum(partial_low.astype(jnp.bfloat16), "tensor")
    returned = lax.all_to_all(
        to_sources(summed, sources, capacity), "expert", split_axis=0, concat_axis=0, tiled=True
    )
    picked = returned.reshape(experts * capacity, D)[flat_slot]
    moe_out = jnp.zeros((SEQ, D), jnp.float32)
    for route_index in range(TOP):
        moe_out = moe_out + gates[:, route_index : route_index + 1] * picked[:, route_index].astype(
            jnp.float32
        )
    output = (resid_one + moe_out).astype(jnp.bfloat16)
    keep_rows = allowed.astype(jnp.float32)
    grad_two = cotangent.astype(jnp.float32) * keep_rows[:, None]
    grad_gate_sel = jnp.stack(
        [
            jnp.sum(grad_two * picked[:, route_index].astype(jnp.float32), axis=-1)
            for route_index in range(TOP)
        ],
        axis=1,
    )
    padded_grad = jnp.concatenate([grad_two, jnp.zeros((1, D), jnp.float32)], axis=0)
    padded_gates = jnp.concatenate([gates.reshape(-1), jnp.zeros((1,), jnp.float32)], axis=0)
    slot_gates = padded_gates[slot_owner][:, None]
    grad_send = (
        (padded_grad[token_of] * slot_gates).astype(jnp.bfloat16).reshape(experts, capacity, D)
    )
    grad_arrived = lax.all_to_all(grad_send, "expert", split_axis=0, concat_axis=0, tiled=True)
    grad_out_rows = to_experts(grad_arrived, sources, per_device)
    grad_hidden = jnp.einsum(
        "erd,efd->erf", grad_out_rows, wd_low, preferred_element_type=jnp.float32
    )
    grad_down_w = jnp.einsum(
        "erf,erd->efd", hidden, grad_out_rows, preferred_element_type=jnp.float32
    )
    silu_slope = sigmoid_gate * (1.0 + gate_lin * (1.0 - sigmoid_gate))
    grad_gate_lin = (grad_hidden * up_lin * silu_slope).astype(jnp.bfloat16)
    grad_up_lin = (grad_hidden * activated).astype(jnp.bfloat16)
    grad_gate_w = jnp.einsum(
        "erd,erf->edf", expert_rows, grad_gate_lin, preferred_element_type=jnp.float32
    )
    grad_up_w = jnp.einsum(
        "erd,erf->edf", expert_rows, grad_up_lin, preferred_element_type=jnp.float32
    )
    grad_rows_in = jnp.einsum(
        "erf,edf->erd", grad_gate_lin, wg_low, preferred_element_type=jnp.float32
    )
    grad_rows_in = grad_rows_in + jnp.einsum(
        "erf,edf->erd", grad_up_lin, wu_low, preferred_element_type=jnp.float32
    )
    returned_grad = lax.all_to_all(
        to_sources(grad_rows_in.astype(jnp.bfloat16), sources, capacity),
        "expert",
        split_axis=0,
        concat_axis=0,
        tiled=True,
    )
    picked_grad = returned_grad.reshape(experts * capacity, D)[flat_slot]
    grad_ffn_part = jnp.zeros((SEQ, D), jnp.float32)
    for route_index in range(TOP):
        grad_ffn_part = grad_ffn_part + picked_grad[:, route_index].astype(jnp.float32)
    grad_ffn_in = lax.psum(grad_ffn_part, "tensor")
    grad_chosen = gates * (grad_gate_sel - jnp.sum(gates * grad_gate_sel, axis=1, keepdims=True))
    grad_logits = jnp.sum(jnp.where(route_hot, grad_chosen[:, :, None], 0.0), axis=1).astype(
        jnp.bfloat16
    )
    grad_router_w = contract_rows(ffn_in, grad_logits)
    grad_ffn_in = grad_ffn_in + contract_cols(grad_logits, router_full)
    grad_gain_two = jnp.sum(grad_ffn_in * normed_two, axis=0)
    grad_one = grad_two + norm_back(grad_ffn_in * gain_two, normed_two, inverse_two)
    grad_attn = grad_one.astype(jnp.bfloat16)
    grad_wo = contract_rows(grad_attn, mixed)
    grad_mixed = (
        jnp.dot(grad_attn, wo_full, preferred_element_type=jnp.float32)
        .astype(jnp.bfloat16)
        .reshape(SEQ, heads_here, HD)
    )
    masked = masked_scores()
    attn_probs = jnp.exp(masked - log_total)
    probs_again = attn_probs.astype(jnp.bfloat16)
    grad_probs = jnp.einsum(
        "qhd,khd->hqk", grad_mixed, values_b, preferred_element_type=jnp.float32
    )
    grad_values = jnp.einsum(
        "hqk,qhd->khd", probs_again, grad_mixed, preferred_element_type=jnp.float32
    )
    grad_scores = (
        attn_probs * (grad_probs - jnp.sum(attn_probs * grad_probs, axis=-1, keepdims=True))
    ).astype(jnp.bfloat16)
    grad_queries = (
        jnp.einsum("hqk,khd->qhd", grad_scores, keys_rot, preferred_element_type=jnp.float32)
        * scale
    )
    grad_keys = (
        jnp.einsum("hqk,qhd->khd", grad_scores, queries, preferred_element_type=jnp.float32) * scale
    )
    grad_query_scaled = rotate_back(grad_queries, cosine, sine_tab)
    grad_key_scaled = rotate_back(grad_keys, cosine, sine_tab)
    grad_gain_query = jnp.sum(grad_query_scaled * query_hat, axis=(0, 1))
    grad_gain_key = jnp.sum(grad_key_scaled * key_hat, axis=(0, 1))
    grad_query_lin = (
        norm_back(grad_query_scaled * gain_query, query_hat, query_inv)
        .astype(jnp.bfloat16)
        .reshape(SEQ, heads_here * HD)
    )
    grad_key_lin = (
        norm_back(grad_key_scaled * gain_key, key_hat, key_inv)
        .astype(jnp.bfloat16)
        .reshape(SEQ, heads_here * HD)
    )
    grad_value_lin = grad_values.astype(jnp.bfloat16).reshape(SEQ, heads_here * HD)
    grad_wq = contract_rows(attn_in, grad_query_lin)
    grad_wk = contract_rows(attn_in, grad_key_lin)
    grad_wv = contract_rows(attn_in, grad_value_lin)
    grad_attn_part = (
        contract_cols(grad_query_lin, wq_full)
        + contract_cols(grad_key_lin, wk_full)
        + contract_cols(grad_value_lin, wv_full)
    )
    grad_attn_in, grad_gain_query, grad_gain_key = (
        lax.psum(grad_attn_part.astype(jnp.bfloat16), "tensor").astype(jnp.float32),
        lax.psum(grad_gain_query.astype(jnp.bfloat16), "tensor").astype(jnp.float32),
        lax.psum(grad_gain_key.astype(jnp.bfloat16), "tensor").astype(jnp.float32),
    )
    grad_gain_one = jnp.sum(grad_attn_in * normed_one, axis=0)
    grad_input = grad_one + norm_back(grad_attn_in * gain_one, normed_one, inverse_one)
    reduced = (
        lax.psum_scatter(grad_gain_one, "expert", scatter_dimension=0, tiled=True),
        lax.psum_scatter(grad_wq, "expert", scatter_dimension=0, tiled=True),
        lax.psum_scatter(grad_wk, "expert", scatter_dimension=0, tiled=True),
        lax.psum_scatter(grad_wv, "expert", scatter_dimension=0, tiled=True),
        lax.psum_scatter(grad_gain_query, "expert", scatter_dimension=0, tiled=True),
        lax.psum_scatter(grad_gain_key, "expert", scatter_dimension=0, tiled=True),
        lax.psum_scatter(grad_wo, "expert", scatter_dimension=0, tiled=True),
        lax.psum_scatter(grad_gain_two, "expert", scatter_dimension=0, tiled=True),
        lax.psum_scatter(grad_router_w, "expert", scatter_dimension=0, tiled=True),
    )
    return (
        output,
        grad_input.astype(jnp.bfloat16),
        reduced[0],
        reduced[1],
        reduced[2],
        reduced[3],
        reduced[4],
        reduced[5],
        reduced[6],
        reduced[7],
        reduced[8],
        grad_gate_w,
        grad_up_w,
        grad_down_w,
    )


def solution(mesh):
    return jax.shard_map(
        local,
        mesh=mesh,
        in_specs=(
            P("expert", None),
            P("expert"),
            P("expert", None),
            P("expert"),
            P("expert", "tensor"),
            P("expert", "tensor"),
            P("expert", "tensor"),
            P("expert"),
            P("expert"),
            P("expert", "tensor"),
            P("expert"),
            P("expert", None),
            P("expert", None, "tensor"),
            P("expert", None, "tensor"),
            P("expert", "tensor", None),
            P("expert", None),
        ),
        out_specs=(
            P("expert", None),
            P("expert", None),
            P("expert"),
            P("expert", "tensor"),
            P("expert", "tensor"),
            P("expert", "tensor"),
            P("expert"),
            P("expert"),
            P("expert", "tensor"),
            P("expert"),
            P("expert", None),
            P("expert", None, "tensor"),
            P("expert", None, "tensor"),
            P("expert", "tensor", None),
        ),
        check_vma=False,
    )
```

profile of v0, /device:TPU:0, one launch (start us, length us, event | category | flops | bytes accessed | tf_op | source)
XLA Modules:
  0.0 3563.2 jit_solution(8706941331362449946)
XLA Ops:
  17.3 44.0 %all-reduce.9 = (bf16[128]{0:T(256)(128)(2,1)S(1)}, bf16[128]{0:T(256)(128)(2,1)S(1)}) all-reduce(bf16[128]{0:T(256)(128)(2,1)S(1)} %dynamic-update-slice.1, bf16[128]{0:T(256)(128)(2,1)S(1)} %dynamic-update-slice), channel_id=1, replica_groups=mesh['expert'=16,'tensor'=2] {'expert'}, use_global_device_ids=true, to_apply=%add.3 | all-reduce | flops 256 | bytes 1024
  61.4 36.3 %all-gather = bf16[16,1,128]{2,1,0:T(2,128)(2,1)S(1)} all-gather(bf16[1,1,128]{2,1,0:T(2,128)(2,1)S(1)} %convert_bitcast_fusion.1), channel_id=1, replica_groups=mesh['expert'=16,'tensor'=2] {'expert'}, dimensions={0}, use_global_device_ids=true | all-gather | bytes 4352 | tf_op jit(solution)/shard_map/all_gather | solution.py:133
  106.0 61.6 %all-gather.11.cloned.1.call-done = bf16[2048,1024]{1,0:T(8,128)(2,1)} async-done(((bf16[128,1024]{1,0:T(8,128)(2,1)}), bf16[2048,1024]{1,0:T(8,128)(2,1)}) %all-gather.11.cloned.1.call-update) | async-done | bytes 4194320 | tf_op jit(solution)/shard_map/all_gather | solution.py:129
  186.8 58.4 %all-gather.7.cloned.1.call-done = bf16[2048,1024]{1,0:T(8,128)(2,1)} async-done(((bf16[128,1024]{1,0:T(8,128)(2,1)}), bf16[2048,1024]{1,0:T(8,128)(2,1)}) %all-gather.7.cloned.1.call-update) | async-done | bytes 4194320 | tf_op jit(solution)/shard_map/all_gather | solution.py:130
  252.6 70.0 %all-gather.13.cloned.1.call-done = bf16[2048,1024]{1,0:T(8,128)(2,1)} async-done(((bf16[128,1024]{1,0:T(8,128)(2,1)}), bf16[2048,1024]{1,0:T(8,128)(2,1)}) %all-gather.13.cloned.1.call-update) | async-done | bytes 4194320 | tf_op jit(solution)/shard_map/all_gather | solution.py:131
  329.9 38.3 %all-gather.1 = bf16[16,1,128]{2,1,0:T(2,128)(2,1)S(1)} all-gather(bf16[1,1,128]{2,1,0:T(2,128)(2,1)S(1)} %convert_bitcast_fusion), channel_id=1, replica_groups=mesh['expert'=16,'tensor'=2] {'expert'}, dimensions={0}, use_global_device_ids=true | all-gather | bytes 4352 | tf_op jit(solution)/shard_map/all_gather | solution.py:134
  411.2 404.8 %all_to_all.20 = bf16[16,288,2048]{2,1,0:T(8,128)(2,1)S(1)} all-to-all(bf16[16,288,2048]{2,1,0:T(8,128)(2,1)} %bitcast.289), channel_id=1, replica_groups=mesh['expert'=16,'tensor'=2] {'expert'}, dimensions={0} | all-to-all | bytes 37748736 | tf_op jit(solution)/shard_map/all_to_all | solution.py:200
  873.0 65.6 %all-reduce.18.cloned.1.call-done = bf16[16,288,2048]{2,1,0:T(8,128)(2,1)} async-done(((bf16[16,288,2048]{2,1,0:T(8,128)(2,1)}), bf16[16,288,2048]{2,1,0:T(8,128)(2,1)}) %all-reduce.18.cloned.1.call-update) | async-done | bytes 18874384 | tf_op jit(solution)/shard_map/psum | solution.py:212
  945.9 443.1 %all_gather.35 = bf16[2048,16]{0,1:T(8,128)(2,1)S(1)} all-gather(bf16[128,16]{0,1:T(8,128)(2,1)S(1)} %convert_element_type.360), channel_id=1, replica_groups=mesh['expert'=16,'tensor'=2] {'expert'}, dimensions={0}, use_global_device_ids=true | all-gather | bytes 69632 | tf_op jit(solution)/shard_map/all_gather | solution.py:132
  1389.7 40.1 %gather_fusion.1 = bf16[4096,2048]{1,0:T(8,128)(2,1)} fusion(bf16[4608,2048]{1,0:T(8,128)(2,1)} %bitcast.18, s32[4096]{0:T(1024)S(1)} %broadcast_clamp_fusion), kind=kCustom, calls=%fused_computation.1 | custom fusion | bytes 33570816 | tf_op jit(solution)/shard_map/gather | solution.py:216
  1429.9 72.7 %fusion.104 = (bf16[512,1,2048]{2,1,0:T(2,128)(2,1)S(1)}, bf16[512,1,2048]{2,1,0:T(2,128)(2,1)S(1)}, bf16[512,1,2048]{2,1,0:T(2,128)(2,1)}, bf16[512,1,2048]{2,1...) fusion(bf16[512,8,2048]{2,1,0:T(8,128)(2,1)} %bitcast.287), kind=kLoop, calls=%fused_computation.229 | loop fusion | bytes 33554432 | tf_op jit(solution)/shard_map/slice | solution.py:219
  1502.7 26.7 fusion.27
  1559.3 36.1 %gather_fusion.2 = f32[4608,2048]{1,0:T(8,128)} fusion(f32[513,2048]{1,0:T(8,128)} %concatenate.34, s32[5120]{0:T(1024)S(1)} %copy-done.59), kind=kCustom, calls=%fused_computation.2 | custom fusion | bytes 75515904 | tf_op jit(solution)/shard_map/gather | solution.py:236
  1609.0 409.8 %all_to_all.21 = bf16[16,288,2048]{2,1,0:T(8,128)(2,1)} all-to-all(bf16[16,288,2048]{2,1,0:T(8,128)(2,1)S(1)} %multiply_convert_fusion), channel_id=1, replica_groups=mesh['expert'=16,'tensor'=2] {'expert'}, dimensions={0} | all-to-all | bytes 37748736 | tf_op jit(solution)/shard_map/all_to_all | solution.py:238
  2090.1 411.5 %all_to_all.22 = bf16[16,288,2048]{2,1,0:T(8,128)(2,1)} all-to-all(bf16[16,288,2048]{2,1,0:T(8,128)(2,1)} %bitcast.301), channel_id=1, replica_groups=mesh['expert'=16,'tensor'=2] {'expert'}, dimensions={0} | all-to-all | bytes 37748736 | tf_op jit(solution)/shard_map/all_to_all | solution.py:261
  2501.6 40.1 %gather_fusion.4 = bf16[4096,2048]{1,0:T(8,128)(2,1)} fusion(bf16[4608,2048]{1,0:T(8,128)(2,1)} %bitcast.283, s32[4096]{0:T(1024)S(1)} %copy-done.20), kind=kCustom, calls=%fused_computation.4 | custom fusion | bytes 33570816 | tf_op jit(solution)/shard_map/gather | solution.py:268
  2541.7 72.8 %fusion.103 = (bf16[512,1,2048]{2,1,0:T(2,128)(2,1)S(1)}, bf16[512,1,2048]{2,1,0:T(2,128)(2,1)S(1)}, bf16[512,1,2048]{2,1,0:T(2,128)(2,1)}, bf16[512,1,2048]{2,1...) fusion(bf16[512,8,2048]{2,1,0:T(8,128)(2,1)} %bitcast.286), kind=kLoop, calls=%fused_computation.228 | loop fusion | bytes 33554432 | tf_op jit(solution)/shard_map/slice | solution.py:271
  2639.8 26.4 all-reduce.20.cloned.1.call-done
  2756.6 28.0 fusion.19
  2837.0 78.1 %all-reduce.8 = (f32[2048]{0:T(1024)S(1)}, f32[128]{0:T(128)S(1)}, f32[128]{0:T(128)S(1)}, f32[2048]{0:T(1024)S(1)}) all-reduce(f32[2048]{0:T(1024)S(1)} %get-tuple-element.16, bf16[128]{0:T(256)(128)(2,1)S(1)} %get-tuple-element.32, ...), channel_id=2, replica_groups=mesh['expert'=16,'tensor'=2] {'expert'}, use_global_device_ids=true, to_apply=%region_34.35.clone | all-reduce | flops 4352 | bytes 34304
  2922.9 83.9 %reduce-scatter.12.cloned.1.call-done = f32[128,1024]{1,0:T(8,128)} async-done(((f32[2048,1024]{1,0:T(8,128)}), f32[128,1024]{1,0:T(8,128)}) %reduce-scatter.12.cloned.1.call-update) | async-done | bytes 524304 | tf_op jit(solution)/shard_map/reduce_scatter | solution.py:344
  3006.9 183.1 %reduce-scatter.10.cloned.1.call-done = f32[128,1024]{1,0:T(8,128)} async-done(((f32[2048,1024]{1,0:T(8,128)}), f32[128,1024]{1,0:T(8,128)}) %reduce-scatter.10.cloned.1.call-update) | async-done | bytes 524304 | tf_op jit(solution)/shard_map/reduce_scatter | solution.py:341
  3190.0 183.1 %reduce-scatter.6.cloned.1.call-done = f32[128,1024]{1,0:T(8,128)} async-done(((f32[2048,1024]{1,0:T(8,128)}), f32[128,1024]{1,0:T(8,128)}) %reduce-scatter.6.cloned.1.call-update) | async-done | bytes 524304 | tf_op jit(solution)/shard_map/reduce_scatter | solution.py:339
  3373.0 183.2 %reduce-scatter.8.cloned.1.call-done = f32[128,1024]{1,0:T(8,128)} async-done(((f32[2048,1024]{1,0:T(8,128)}), f32[128,1024]{1,0:T(8,128)}) %reduce-scatter.8.cloned.1.call-update) | async-done | bytes 524304 | tf_op jit(solution)/shard_map/reduce_scatter | solution.py:340
  (374 shorter events, 446.9 us)
Async XLA Ops:
  7.2 90.5 %copy-start.15 = (bf16[512,2048]{1,0:T(8,128)(2,1)S(1)}, bf16[512,2048]{1,0:T(8,128)(2,1)}, u32[]{:S(2)}) copy-start(bf16[512,2048]{1,0:T(8,128)(2,1)} %param.16) | copy-start | bytes 6291460
  7.2 92.0 %all-gather.9.cloned.1.call-start = ((), (), s32[]{:S(2)}) async-start(), calls=%async_computation.10 | async-start | bytes 4456448 | tf_op jit(solution)/shard_map/all_gather | solution.py:128
  9.2 158.4 %all-gather.11.cloned.1.call-start = ((), (), s32[]{:S(2)}) async-start(), calls=%async_computation.11 | async-start | bytes 4456448 | tf_op jit(solution)/shard_map/all_gather | solution.py:129
  11.1 234.1 %all-gather.7.cloned.1.call-start = ((), (), s32[]{:S(2)}) async-start(), calls=%async_computation.9 | async-start | bytes 4456448 | tf_op jit(solution)/shard_map/all_gather | solution.py:130
  12.9 309.7 %all-gather.13.cloned.1.call-start = ((), (), s32[]{:S(2)}) async-start(), calls=%async_computation.12 | async-start | bytes 4456448 | tf_op jit(solution)/shard_map/all_gather | solution.py:131
  14.8 372.6 %all-reduce.16.cloned.1.call-start = ((), (), s32[]{:S(2)}) async-start(), calls=%async_computation.13 | async-start | bytes 8388608 | tf_op jit(solution)/shard_map/psum | solution.py:190
  61.3 114.0 %copy-start.82 = (f32[128]{0:T(128)}, f32[128]{0:T(128)S(1)}, u32[]{:S(2)}) copy-start(f32[128]{0:T(128)S(1)} %convert_element_type.351) | copy-start | bytes 1540
  61.3 114.0 %copy-start.80 = (f32[128]{0:T(128)}, f32[128]{0:T(128)S(1)}, u32[]{:S(2)}) copy-start(f32[128]{0:T(128)S(1)} %convert_element_type.346) | copy-start | bytes 1540
  97.7 147.5 %copy-start.67 = (f32[16,1,128]{2,1,0:T(1,128)}, f32[16,1,128]{2,1,0:T(1,128)S(1)}, u32[]{:S(2)}) copy-start(f32[16,1,128]{2,1,0:T(1,128)S(1)} %convert_element_type.431) | copy-start | bytes 24580
  98.2 146.9 %copy-start.76 = (f32[512]{0:T(512)}, f32[512]{0:T(512)S(1)}, u32[]{:S(2)}) copy-start(f32[512]{0:T(512)S(1)} %add_rsqrt_fusion.3) | copy-start | bytes 6148
  99.2 78.9 %copy-start.32 = (f32[512,64]{1,0:T(8,128)}, f32[512,64]{1,0:T(8,128)S(1)}, u32[]{:S(2)}) copy-start(f32[512,64]{1,0:T(8,128)S(1)} %get-tuple-element.89) | copy-start | bytes 393220
  329.2 609.3 %all-reduce.18.cloned.1.call-start = ((), (), s32[]{:S(2)}) async-start(), calls=%async_computation.14 | async-start | bytes 37748736 | tf_op jit(solution)/shard_map/psum | solution.py:212
  873.0 516.0 %copy-start.8 = (bf16[512,2048]{1,0:T(8,128)(2,1)S(1)}, bf16[512,2048]{1,0:T(8,128)(2,1)}, u32[]{:S(2)}) copy-start(bf16[512,2048]{1,0:T(8,128)(2,1)} %copy-done.7) | copy-start | bytes 6291460
  873.0 516.6 %copy-start.50 = (s32[512,8]{0,1:T(8,128)S(1)}, s32[512,8]{0,1:T(8,128)}, u32[]{:S(2)}) copy-start(s32[512,8]{0,1:T(8,128)} %param.18) | copy-start | bytes 49156
  938.6 451.2 %all-to-all-start.1 = ((bf16[16,288,2048]{2,1,0:T(8,128)(2,1)}), bf16[16,288,2048]{2,1,0:T(8,128)(2,1)}, u32[]{:S(2)}, u32[]{:S(2)}) async-start(bf16[16,288,2048]{2,1,0:T(8,128)(2,1)} %all-reduce.18.cloned.1.call-done), calls=%async_computation.1 | async-start | bytes 37748736 | tf_op jit(solution)/shard_map/all_to_all | solution.py:213
  945.5 1720.7 %all-reduce.20.cloned.1.call-start = ((), (), s32[]{:S(2)}) async-start(), calls=%async_computation.15 | async-start | bytes 8388608 | tf_op jit(solution)/shard_map/psum | solution.py:272
  1388.9 113.7 %copy-start.74 = (f32[512]{0:T(512)}, f32[512]{0:T(512)S(1)}, u32[]{:S(2)}) copy-start(f32[512]{0:T(512)S(1)} %fusion.90) | copy-start | bytes 6148
  2090.1 411.5 %copy-start.20 = (s32[4096]{0:T(1024)S(1)}, s32[4096]{0:T(1024)}, u32[]{:S(2)}) copy-start(s32[4096]{0:T(1024)} %copy-done.19) | copy-start | bytes 49156
  2638.1 196.0 %all-reduce.22.cloned.1.call-start = ((), (), s32[]{:S(2)}) async-start(), calls=%async_computation.16 | async-start | bytes 4194304 | tf_op jit(solution)/shard_map/psum | solution.py:331
  2723.8 199.1 %reduce-scatter.14.cloned.1.call-start = ((), (), s32[]{:S(2)}) async-start(), calls=%async_computation.21 | async-start | bytes 139264 | tf_op jit(solution)/shard_map/reduce_scatter | solution.py:346
  2725.0 281.9 %reduce-scatter.12.cloned.1.call-start = ((), (), s32[]{:S(2)}) async-start(), calls=%async_computation.20 | async-start | bytes 8912896 | tf_op jit(solution)/shard_map/reduce_scatter | solution.py:344
  2733.4 456.5 %reduce-scatter.10.cloned.1.call-start = ((), (), s32[]{:S(2)}) async-start(), calls=%async_computation.19 | async-start | bytes 8912896 | tf_op jit(solution)/shard_map/reduce_scatter | solution.py:341
  2741.3 631.7 %reduce-scatter.6.cloned.1.call-start = ((), (), s32[]{:S(2)}) async-start(), calls=%async_computation.17 | async-start | bytes 8912896 | tf_op jit(solution)/shard_map/reduce_scatter | solution.py:339
  2748.4 807.8 %reduce-scatter.8.cloned.1.call-start = ((), (), s32[]{:S(2)}) async-start(), calls=%async_computation.18 | async-start | bytes 8912896 | tf_op jit(solution)/shard_map/reduce_scatter | solution.py:340
  (91 other events, 1342.1 us)
Sparse Core Ops, SparseCore 0:
  11.4 78.6 all-gather.8
  93.4 74.1 all-gather.10
  171.0 74.1 all-gather.6
  248.4 74.1 all-gather.12
  329.3 26.6 all-reduce.15
  873.1 65.4 all-reduce.17
  2638.2 27.9 all-reduce.19
  2724.0 22.4 all-reduce.21
  2749.3 78.0 reduce-scatter.13
  2830.0 176.7 reduce-scatter.11
  3009.8 180.1 reduce-scatter.9
  3192.7 180.2 reduce-scatter.5
  3375.9 180.2 reduce-scatter.7
where the time goes:
time: 3570 us; the launch traced here: 3560 us
  blocking collectives  1870 us (52%)
  waiting for transfers between devices  915 us (26%)
  local copies, waits for them, and re-layouts  362 us (10%)
  matrix products  251 us (7%)
  other arithmetic  140 us (4%)
    all_gather x1, blocking collectives, local(): lax.all_gather(w_router.astype(jnp.bfloat16), 'expert', axis=0, tiled=True)  443 us
    all_to_all x1, blocking collectives, local(): lax.all_to_all(to_sources(grad_rows_in.astype(jnp.bfloat16), sources, cap...  412 us
    all_to_all x1, blocking collectives, local(): lax.all_to_all(grad_send, 'expert', split_axis=0, concat_axis=0, tiled=True)  410 us
    all_to_all x1, blocking collectives, local(): lax.all_to_all(send_rows, 'expert', split_axis=0, concat_axis=0, tiled=True)  405 us
    reduce_scatter x1, waiting for transfers between devices, local(): lax.psum_scatter(grad_wk, 'expert', scatter_dimension=0, tiled=True)  183 us
    reduce_scatter x1, waiting for transfers between devices, local(): lax.psum_scatter(grad_wv, 'expert', scatter_dimension=0, tiled=True)  183 us
    reduce_scatter x1, waiting for transfers between devices, local(): lax.psum_scatter(grad_wq, 'expert', scatter_dimension=0, tiled=True)  183 us
    unnamed x2, blocking collectives  122 us
  transfers between devices with their start and end apart: 14, of which 9 were waited for; matrix products, arithmetic and copies ran while one was open for 5% of the time, Pallas kernels for 0%

commit v1 on v0

v1 whole, which is shorter than its diff:
```python
import math

import jax
import jax.numpy as jnp
from jax import lax
from jax.experimental import pallas as pl
from jax.experimental.pallas import tpu as pltpu
from jax.sharding import PartitionSpec as P

D = 2048
HD = 128
TOP = 8
SEQ = 512


EPSILON = 1e-06
ROPE_BASE = 10000.0
NEG_BIG = -1e30


def rope_tables(seq_len, head_dim):
    half_dim = head_dim // 2
    inverse = ROPE_BASE ** (-(jnp.arange(half_dim).astype(jnp.float32) * 2.0 / head_dim))
    angles = jnp.arange(seq_len).astype(jnp.float32)[:, None] * inverse[None, :]
    return (jnp.cos(angles), jnp.sin(angles))


def rotate(values, cosine, sine_tab):
    half_dim = values.shape[-1] // 2
    lower_half = values[..., :half_dim]
    upper_half = values[..., half_dim:]
    cos_b = cosine[:, None, :]
    sin_b = sine_tab[:, None, :]
    return jnp.concatenate(
        [lower_half * cos_b - upper_half * sin_b, upper_half * cos_b + lower_half * sin_b], axis=-1
    )


def rotate_back(grads_in, cosine, sine_tab):
    half_dim = grads_in.shape[-1] // 2
    lower_half = grads_in[..., :half_dim]
    upper_half = grads_in[..., half_dim:]
    cos_b = cosine[:, None, :]
    sin_b = sine_tab[:, None, :]
    return jnp.concatenate(
        [lower_half * cos_b + upper_half * sin_b, upper_half * cos_b - lower_half * sin_b], axis=-1
    )


def norm_stats(values):
    inverse = lax.rsqrt(jnp.mean(values * values, axis=-1, keepdims=True) + EPSILON)
    return (values * inverse, inverse)


def norm_back(grad_normed, normed, inverse):
    return inverse * (grad_normed - normed * jnp.mean(grad_normed * normed, axis=-1, keepdims=True))


def contract_rows(left_mat, right_mat):
    return lax.dot_general(
        left_mat, right_mat, (((0,), (0,)), ((), ())), preferred_element_type=jnp.float32
    )


def contract_cols(left_mat, right_mat):
    return lax.dot_general(
        left_mat, right_mat, (((1,), (1,)), ((), ())), preferred_element_type=jnp.float32
    )


PLANES = 4
CORES = 2


class Grid:
    def __init__(self, count):
        self.count = count
        self.plane = count // PLANES
        self.side = math.isqrt(self.plane)
        self.near = range(1, self.side)

    def first(self, step):
        return (step, step * self.side)

    def second(self, step):
        return (step * self.side, step)

    def planes_of(self, turn):
        return ((0, 3)[turn] * self.plane, (1, 2)[turn] * self.plane)

    def send(self, value, masks):
        pairs = [
            (device * CORES + core, (device ^ masks[core]) * CORES + core)
            for device in range(self.count)
            for core in range(CORES)
        ]
        return lax.ppermute(value, ("expert", "tensor"), pairs)


def swap(value):
    return lax.ppermute(value, "tensor", [(0, 1), (1, 0)])


def spread(grid, base):
    row = [base] + [grid.send(base, grid.first(step)) for step in grid.near]
    blocks = list(row)
    for step in grid.near:
        blocks += [grid.send(block, grid.second(step)) for block in row]
    return blocks


def gather_tokens(grid, block):
    return [spread(grid, grid.send(block, grid.planes_of(turn))) for turn in range(2)]


def collect(grid, blocks):
    side = grid.side
    sums = [block.astype(jnp.float32) for block in blocks[:side]]
    for far in grid.near:
        for step in range(side):
            sums[step] = sums[step] + grid.send(
                blocks[far * side + step], grid.second(far)
            ).astype(jnp.float32)
    total = sums[0]
    for step in grid.near:
        total = total + grid.send(sums[step].astype(jnp.bfloat16), grid.first(step)).astype(
            jnp.float32
        )
    return total


def scatter_tokens(grid, turns):
    total = None
    for turn in (1, 0):
        part = grid.send(collect(grid, turns[turn]).astype(jnp.bfloat16), grid.planes_of(turn))
        part = part.astype(jnp.float32)
        total = part if total is None else total + part
    total = total.astype(jnp.bfloat16)
    return total.astype(jnp.float32) + swap(total).astype(jnp.float32)


def scatter_rows(grid, value, axes, wire):
    me = lax.axis_index("expert")
    units = (grid.plane, grid.side, 1)
    sizes = (PLANES, grid.side, grid.side)
    gone = []
    for axis in axes:
        unit, size = units[axis], sizes[axis]
        place = (me // unit) % size
        at = axis - sum(1 for other in gone if other < axis)
        total = lax.dynamic_index_in_dim(value, place, at, keepdims=False).astype(jnp.float32)
        for step in range(1, size):
            part = lax.dynamic_index_in_dim(value, place ^ step, at, keepdims=False).astype(wire)
            total = total + grid.send(part, (unit * step,) * CORES).astype(jnp.float32)
        value = total
        gone.append(axis)
    return value


def assemble(grid, blocks, rows, extra):
    count, width = grid.count, blocks[0].shape[1]
    me = lax.axis_index("expert")
    core = lax.axis_index("tensor")
    place = jnp.arange(count)
    top, mid, low = place // grid.plane, (place // grid.side) % grid.side, place % grid.side
    turned = top * grid.plane + low * grid.side + mid
    owner = me ^ jnp.where(core == 0, place, turned)

    def body(owner_ref, *refs):
        ins, outs, small, sem = refs[:count], refs[count : count + 4], refs[count + 4], refs[-1]
        copies = []
        for index in range(count):
            at = owner_ref[index]
            for which in range(4):
                copies.append(
                    pltpu.make_async_copy(
                        ins[index].at[pl.ds(which * rows, rows)],
                        outs[which].at[pl.ds(pl.multiple_of(at * rows, rows), rows)],
                        sem.at[index, which],
                    )
                )
            copies.append(
                pltpu.make_async_copy(
                    ins[index].at[pl.ds(4 * rows, extra)], small.at[at], sem.at[index, 4]
                )
            )
        for copy in copies:
            copy.start()
        for copy in copies:
            copy.wait()

    full = jax.ShapeDtypeStruct((count * rows, width), jnp.bfloat16)
    small = jax.ShapeDtypeStruct((count, extra, width), jnp.bfloat16)
    return pl.pallas_call(
        body,
        grid_spec=pltpu.PrefetchScalarGridSpec(
            num_scalar_prefetch=1,
            grid=(),
            in_specs=[pl.BlockSpec(memory_space=pl.ANY)] * count,
            out_specs=[pl.BlockSpec(memory_space=pltpu.VMEM)] * 5,
            scratch_shapes=[pltpu.SemaphoreType.DMA((count, 5))],
        ),
        out_shape=[full] * 4 + [small],
        name="assemble",
    )(owner, *blocks)


def split_three(value):
    high = value.astype(jnp.bfloat16)
    rest = value - high.astype(jnp.float32)
    middle = rest.astype(jnp.bfloat16)
    low = (rest - middle.astype(jnp.float32)).astype(jnp.bfloat16)
    return jnp.concatenate([high, middle, low], axis=-1)


def join_three(parts, length):
    parts = parts.astype(jnp.float32)
    return (
        parts[..., :length] + parts[..., length : 2 * length] + parts[..., 2 * length : 3 * length]
    )


def expert_turn(blocks, grads, weights, capacity):
    wg, wu, wd = weights
    me = lax.axis_index("expert")
    experts = blocks[0].shape[0] - SEQ
    gate = jnp.concatenate(
        [
            join_three(lax.dynamic_slice(block, (SEQ + me, 0), (1, 3 * SEQ)), SEQ)
            for block in blocks
        ],
        axis=0,
    )
    used = gate > 0.0
    ordered = (jnp.arange(SEQ)[:, None] < jnp.arange(SEQ)[None, :]).astype(jnp.bfloat16)
    slot = jnp.dot(used.astype(jnp.bfloat16), ordered, preferred_element_type=jnp.float32)
    slot = slot.astype(jnp.int32)
    hot = (jnp.arange(capacity)[None, :, None] == slot[:, None, :]) & used[:, None, :]
    pick = hot.astype(jnp.bfloat16)
    slot_gate = jnp.sum(jnp.where(hot, gate[:, None, :], 0.0), axis=2).reshape(-1, 1)
    rows = jnp.concatenate(
        [
            jnp.dot(pick[i], block[:SEQ], preferred_element_type=jnp.float32).astype(jnp.bfloat16)
            for i, block in enumerate(blocks)
        ],
        axis=0,
    )
    grad_rows = jnp.concatenate(
        [
            jnp.dot(pick[i], block, preferred_element_type=jnp.float32).astype(jnp.bfloat16)
            for i, block in enumerate(grads)
        ],
        axis=0,
    )
    gate_lin = jnp.dot(rows, wg, preferred_element_type=jnp.float32)
    up_lin = jnp.dot(rows, wu, preferred_element_type=jnp.float32)
    grad_full = contract_cols(grad_rows, wd)
    sigmoid_gate = jax.nn.sigmoid(gate_lin)
    activated = gate_lin * sigmoid_gate
    hidden = activated * up_lin
    hidden_low = (hidden * slot_gate).astype(jnp.bfloat16)
    slot_grad = jnp.sum(hidden * grad_full, axis=1).reshape(len(blocks), capacity, 1)
    grad_hidden = grad_full * slot_gate
    silu_slope = sigmoid_gate * (1.0 + gate_lin * (1.0 - sigmoid_gate))
    grad_gate = (grad_hidden * up_lin * silu_slope).astype(jnp.bfloat16)
    grad_up = (grad_hidden * activated).astype(jnp.bfloat16)
    value = jnp.dot(hidden_low, wd, preferred_element_type=jnp.float32).astype(jnp.bfloat16)
    grad_in = (contract_cols(grad_gate, wg) + contract_cols(grad_up, wu)).astype(jnp.bfloat16)
    token_grad = split_three(jnp.sum(jnp.where(hot, slot_grad, 0.0), axis=1))
    outs, backs = [], []
    for i in range(len(blocks)):
        span = slice(i * capacity, (i + 1) * capacity)
        outs.append(contract_rows(pick[i], value[span]).astype(jnp.bfloat16))
        back = contract_rows(pick[i], grad_in[span]).astype(jnp.bfloat16)
        extra = jnp.where(
            (jnp.arange(experts) == me)[:, None],
            jnp.pad(token_grad[i : i + 1], ((0, 0), (0, D - 3 * SEQ))),
            0,
        )
        backs.append(jnp.concatenate([back, extra], axis=0))
    return outs, backs, (rows, grad_rows, hidden_low, grad_gate, grad_up)


def local(
    tokens,
    lengths,
    routes,
    attn_gain,
    w_query,
    w_key,
    w_value,
    query_gain,
    key_gain,
    w_out,
    ffn_gain,
    w_router,
    w_gate,
    w_up,
    w_down,
    cotangent,
):
    grid = Grid(lax.axis_size("expert"))
    count = grid.count
    experts = w_router.shape[1]
    capacity = SEQ * TOP * 9 // (8 * experts)
    scale = 1.0 / math.sqrt(HD)
    low = jnp.bfloat16
    own_rows, width = w_query.shape
    heads_here = width // HD
    core = lax.axis_index("tensor")

    small = jnp.concatenate(
        [
            w_router.astype(low).T,
            jnp.pad(
                jnp.stack(
                    [
                        attn_gain.astype(low),
                        ffn_gain.astype(low),
                        jnp.pad(query_gain.astype(low), (0, own_rows - HD // count)),
                        jnp.pad(key_gain.astype(low), (0, own_rows - HD // count)),
                    ]
                ),
                ((0, experts - 4), (0, 0)),
            ),
        ],
        axis=1,
    )
    small = jnp.pad(small, ((0, 0), (0, width - 2 * own_rows)))
    mine = jnp.concatenate(
        [w_query.astype(low), w_key.astype(low), w_value.astype(low), w_out.astype(low), small],
        axis=0,
    )
    arrived = []
    for top in range(PLANES):
        base = mine if top == 0 else grid.send(mine, (top * grid.plane,) * CORES)
        arrived += spread(grid, base)
    wq_full, wk_full, wv_full, wo_full, smalls = assemble(grid, arrived, own_rows, experts)
    router_t = smalls[:, :, :own_rows].transpose(1, 0, 2).reshape(experts, D)
    gain_one = smalls[:, 0, own_rows : 2 * own_rows].reshape(D).astype(jnp.float32)
    gain_two = smalls[:, 1, own_rows : 2 * own_rows].reshape(D).astype(jnp.float32)
    head_cols = slice(own_rows, own_rows + HD // count)
    gain_query = smalls[:, 2, head_cols].reshape(HD).astype(jnp.float32)
    gain_key = smalls[:, 3, head_cols].reshape(HD).astype(jnp.float32)

    wg_own, wu_own, wd_own = (w_gate[0].astype(low), w_up[0].astype(low), w_down[0].astype(low))
    wg = jnp.concatenate([wg_own, swap(wg_own)], axis=1)
    wu = jnp.concatenate([wu_own, swap(wu_own)], axis=1)
    wd = jnp.concatenate([wd_own, swap(wd_own)], axis=0)

    allowed = jnp.arange(SEQ) < lengths[0]
    grad_two_low = jnp.where(allowed[:, None], cotangent, 0)
    grad_two_sent, wq_full, wk_full, wv_full, wo_full = lax.optimization_barrier(
        (grad_two_low, wq_full, wk_full, wv_full, wo_full)
    )
    grad_turns = gather_tokens(grid, grad_two_sent)
    grad_two = grad_two_low.astype(jnp.float32)

    cosine, sine_tab = rope_tables(SEQ, HD)
    resid_zero = tokens.astype(jnp.float32)
    normed_one, inverse_one = norm_stats(resid_zero)
    attn_in = (normed_one * gain_one).astype(low)
    query_lin = jnp.dot(attn_in, wq_full, preferred_element_type=jnp.float32).reshape(
        SEQ, heads_here, HD
    )
    key_lin = jnp.dot(attn_in, wk_full, preferred_element_type=jnp.float32).reshape(
        SEQ, heads_here, HD
    )
    values_b = (
        jnp.dot(attn_in, wv_full, preferred_element_type=jnp.float32)
        .astype(low)
        .reshape(SEQ, heads_here, HD)
    )
    query_hat, query_inv = norm_stats(query_lin)
    key_hat, key_inv = norm_stats(key_lin)
    queries = rotate(query_hat * gain_query, cosine, sine_tab).astype(low)
    keys_rot = rotate(key_hat * gain_key, cosine, sine_tab).astype(low)

    def masked_scores():
        scores = (
            jnp.einsum("qhd,khd->hqk", queries, keys_rot, preferred_element_type=jnp.float32)
            * scale
        )
        return jnp.where(allowed[None, None, :], scores, NEG_BIG)

    masked = masked_scores()
    top_score = jnp.max(masked, axis=-1, keepdims=True)
    expo_vals = jnp.exp(masked - top_score)
    totals = jnp.sum(expo_vals, axis=-1, keepdims=True)
    probs_low = (expo_vals / totals).astype(low)
    log_total = top_score + jnp.log(totals)
    mixed = (
        jnp.einsum("hqk,khd->qhd", probs_low, values_b, preferred_element_type=jnp.float32)
        .reshape(SEQ, heads_here * HD)
        .astype(low)
    )
    attn_part = contract_cols(mixed, wo_full)
    resid_one = resid_zero + (attn_part + swap(attn_part))
    normed_two, inverse_two = norm_stats(resid_one)
    ffn_in = (normed_two * gain_two).astype(low)
    logits = contract_cols(ffn_in, router_t)
    route_hot = routes[:, :, None] == jnp.arange(experts)[None, None, :]
    chosen = jnp.sum(jnp.where(route_hot, logits[:, None, :], 0.0), axis=2)
    gates = jax.nn.softmax(chosen, axis=1)
    gates_wide = jnp.sum(jnp.where(route_hot, gates[:, :, None], 0.0), axis=1)

    gate_rows = jnp.pad(split_three(gates_wide.T), ((0, 0), (0, D - 3 * SEQ)))
    token_turns = gather_tokens(grid, jnp.concatenate([ffn_in, gate_rows], axis=0))
    out_turns, back_turns, saved = [], [], []
    for turn in range(2):
        outs, backs, kept = expert_turn(
            token_turns[turn], grad_turns[turn], (wg, wu, wd), capacity
        )
        out_turns.append(outs)
        back_turns.append(backs)
        saved.append(kept)
    back_sum = scatter_tokens(grid, back_turns)
    out_sum = scatter_tokens(grid, out_turns)
    output = (resid_one + out_sum).astype(low)

    def over_turns(left, right):
        return sum(contract_rows(kept[left], kept[right]) for kept in saved)

    half = w_gate.shape[2]
    gate_w = over_turns(0, 3)
    up_w = over_turns(0, 4)
    down_w = over_turns(2, 1)
    grad_gate_w = (gate_w[:, :half] + swap(gate_w[:, half:]))[None]
    grad_up_w = (up_w[:, :half] + swap(up_w[:, half:]))[None]
    grad_down_w = (down_w[:half] + swap(down_w[half:]))[None]

    grad_gates_wide = join_three(back_sum[SEQ:], SEQ).T
    grad_gate_sel = jnp.sum(jnp.where(route_hot, grad_gates_wide[:, None, :], 0.0), axis=2)
    grad_chosen = gates * (grad_gate_sel - jnp.sum(gates * grad_gate_sel, axis=1, keepdims=True))
    grad_logits = jnp.sum(jnp.where(route_hot, grad_chosen[:, :, None], 0.0), axis=1).astype(low)
    grad_router_t = contract_rows(grad_logits, ffn_in)
    grad_ffn_in = back_sum[:SEQ] + jnp.dot(
        grad_logits, router_t, preferred_element_type=jnp.float32
    )
    grad_gain_two = jnp.sum(grad_ffn_in * normed_two, axis=0)
    grad_one = grad_two + norm_back(grad_ffn_in * gain_two, normed_two, inverse_two)
    grad_attn = grad_one.astype(low)

    def reduce_weight(left, right, axes):
        whole = contract_rows(left, right)
        return scatter_rows(
            grid, whole.reshape(PLANES, grid.side, grid.side, own_rows, width), axes, low
        )

    grad_wo = reduce_weight(grad_attn, mixed, (1, 2, 0))
    grad_mixed = (
        jnp.dot(grad_attn, wo_full, preferred_element_type=jnp.float32)
        .astype(low)
        .reshape(SEQ, heads_here, HD)
    )
    masked = masked_scores()
    attn_probs = jnp.exp(masked - log_total)
    probs_again = attn_probs.astype(low)
    grad_probs = jnp.einsum(
        "qhd,khd->hqk", grad_mixed, values_b, preferred_element_type=jnp.float32
    )
    grad_values = jnp.einsum(
        "hqk,qhd->khd", probs_again, grad_mixed, preferred_element_type=jnp.float32
    )
    grad_value_lin = grad_values.astype(low).reshape(SEQ, heads_here * HD)
    grad_wv = reduce_weight(attn_in, grad_value_lin, (2, 1, 0))
    grad_scores = (
        attn_probs * (grad_probs - jnp.sum(attn_probs * grad_probs, axis=-1, keepdims=True))
    ).astype(low)
    grad_queries = (
        jnp.einsum("hqk,khd->qhd", grad_scores, keys_rot, preferred_element_type=jnp.float32)
        * scale
    )
    grad_keys = (
        jnp.einsum("hqk,qhd->khd", grad_scores, queries, preferred_element_type=jnp.float32) * scale
    )
    grad_query_scaled = rotate_back(grad_queries, cosine, sine_tab)
    grad_key_scaled = rotate_back(grad_keys, cosine, sine_tab)
    grad_gain_query = jnp.sum(grad_query_scaled * query_hat, axis=(0, 1))
    grad_gain_key = jnp.sum(grad_key_scaled * key_hat, axis=(0, 1))
    grad_query_lin = (
        norm_back(grad_query_scaled * gain_query, query_hat, query_inv)
        .astype(low)
        .reshape(SEQ, heads_here * HD)
    )
    grad_key_lin = (
        norm_back(grad_key_scaled * gain_key, key_hat, key_inv)
        .astype(low)
        .reshape(SEQ, heads_here * HD)
    )
    grad_wq = reduce_weight(attn_in, grad_query_lin, (1, 2, 0))
    grad_wk = reduce_weight(attn_in, grad_key_lin, (2, 1, 0))
    grad_attn_part = (
        contract_cols(grad_query_lin, wq_full)
        + contract_cols(grad_key_lin, wk_full)
        + contract_cols(grad_value_lin, wv_full)
    ).astype(low)
    grad_attn_in = grad_attn_part.astype(jnp.float32) + swap(grad_attn_part).astype(jnp.float32)
    grad_gain_one = jnp.sum(grad_attn_in * normed_one, axis=0)
    grad_input = grad_one + norm_back(grad_attn_in * gain_one, normed_one, inverse_one)

    head_part = HD // count
    heads_row = jnp.stack([grad_gain_query, grad_gain_key]).reshape(2, count, head_part)
    heads_row = jnp.pad(heads_row, ((0, 0), (0, 0), (0, own_rows - head_part)))
    parts = jnp.concatenate(
        [
            jnp.concatenate([grad_router_t, grad_gain_one[None], grad_gain_two[None]]).reshape(
                experts + 2, count, own_rows
            ),
            heads_row,
        ],
        axis=0,
    ).transpose(1, 0, 2)
    sums = scatter_rows(
        grid,
        parts.reshape(PLANES, grid.side, grid.side, experts + 4, own_rows),
        (1, 2, 0),
        jnp.float32,
    )
    sums = sums + swap(sums)
    return (
        output,
        grad_input.astype(low),
        0.5 * sums[experts],
        grad_wq,
        grad_wk,
        grad_wv,
        sums[experts + 2, :head_part],
        sums[experts + 3, :head_part],
        grad_wo,
        0.5 * sums[experts + 1],
        0.5 * sums[:experts].T,
        grad_gate_w,
        grad_up_w,
        grad_down_w,
    )


def solution(mesh):
    return jax.shard_map(
        local,
        mesh=mesh,
        in_specs=(
            P("expert", None),
            P("expert"),
            P("expert", None),
            P("expert"),
            P("expert", "tensor"),
            P("expert", "tensor"),
            P("expert", "tensor"),
            P("expert"),
            P("expert"),
            P("expert", "tensor"),
            P("expert"),
            P("expert", None),
            P("expert", None, "tensor"),
            P("expert", None, "tensor"),
            P("expert", "tensor", None),
            P("expert", None),
        ),
        out_specs=(
            P("expert", None),
            P("expert", None),
            P("expert"),
            P("expert", "tensor"),
            P("expert", "tensor"),
            P("expert", "tensor"),
            P("expert"),
            P("expert"),
            P("expert", "tensor"),
            P("expert"),
            P("expert", None),
            P("expert", None, "tensor"),
            P("expert", None, "tensor"),
            P("expert", "tensor", None),
        ),
        check_vma=False,
    )
```

time: 3570 us -> 1600 us (0.45)
  blocking collectives: 1870 us -> 0 us
  starting transfers between devices: 7.65 us -> 455 us
  waiting for transfers between devices: 915 us -> 568 us
  local copies, waits for them, and re-layouts: 362 us -> 53.9 us
  matrix products: 251 us -> 346 us
    all_to_all x3 -> x0, blocking collectives: 1230 us -> none  [the longest x1 412 us: local(): lax.all_to_all(to_sources(grad_rows_in.astype(jnp.bfloat16), sources, cap...]
    reduce_scatter x5 -> x0, waiting for transfers between devices: 633 us -> none  [the longest x1 183 us: local(): lax.psum_scatter(grad_wk, 'expert', scatter_dimension=0, tiled=True)]
    ppermute x0 -> x83, waiting for transfers between devices: none -> 568 us  [the longest x72 561 us: send(): return lax.ppermute(value, ('expert', 'tensor'), pairs)]
    all_gather x3 -> x0, blocking collectives: 518 us -> none  [the longest x1 443 us: local(): lax.all_gather(w_router.astype(jnp.bfloat16), 'expert', axis=0, tiled=True)]
    ppermute x0 -> x83, starting transfers between devices: none -> 455 us  [the longest x11 300 us: swap(): return lax.ppermute(value, 'tensor', [(0, 1), (1, 0)])]
    all_gather x4 -> x0, waiting for transfers between devices: 190 us -> none  [the longest x1 70 us: local(): lax.all_gather(w_out.astype(jnp.bfloat16), 'expert', axis=0, tiled=True)]
    gather x5 -> x0, local copies, waits for them, and re-layouts: 159 us -> none  [the longest x1 40.1 us: local(): picked = returned.reshape(experts * capacity, D)[flat_slot]]
    slice x4 -> x5, local copies, waits for them, and re-layouts: 146 us -> 7.42 us  [the longest x1 2.68 us: local(): grad_gate_w = (gate_w[:, :half] + swap(gate_w[:, half:]))[None]]
  transfers between devices with their start and end apart: 14 -> 83, of which waited for: 9 -> 26; matrix products, arithmetic and copies ran while one was open for 5% -> 24% of each run, Pallas kernels for 0% -> 0%
where the time goes in v1:
time: 1600 us; the launch traced here: 1580 us
  waiting for transfers between devices  568 us (36%)
  starting transfers between devices  455 us (28%)
  matrix products  346 us (22%)
  other arithmetic  143 us (9%)
  local copies, waits for them, and re-layouts  53.9 us (3%)
    ppermute x72, waiting for transfers between devices, send(): return lax.ppermute(value, ('expert', 'tensor'), pairs)  561 us
    ppermute x11, starting transfers between devices, swap(): return lax.ppermute(value, 'tensor', [(0, 1), (1, 0)])  300 us
    ppermute x72, starting transfers between devices, send(): return lax.ppermute(value, ('expert', 'tensor'), pairs)  155 us
    dot_general x27, matrix products, contract_rows(): lax.dot_general(left_mat, right_mat, (((0,), (0,)), ((), ())), preferred_...  124 us
    dot_general x11, matrix products, contract_cols(): lax.dot_general(left_mat, right_mat, (((1,), (1,)), ((), ())), preferred_...  88.7 us
  transfers between devices with their start and end apart: 83, of which 26 were waited for; matrix products, arithmetic and copies ran while one was open for 24% of the time, Pallas kernels for 0%

profile of v1, /device:TPU:0, one launch (start us, length us, event | category | flops | bytes accessed | tf_op | source)
XLA Modules:
  0.0 1582.9 jit_solution(17397610219447037995)
XLA Ops:
  15.6 66.6 %collective-permute-done.7.refs_8_ = bf16[528,1024]{1,0:T(8,128)(2,1)} collective-permute-done((bf16[528,1024]{1,0:T(8,128)(2,1)S(1)}, bf16[528,1024]{1,0:T(8,128)(2,1)}, u32[]{:S(2)}, u32[]{:S(2)}) %collective-permute-start.7) | collective-permute-done | bytes 1081376 | tf_op jit(solution)/shard_map/ppermute | solution.py:97
  89.7 19.5 %collective-permute-done.8.refs_9_ = bf16[528,1024]{1,0:T(8,128)(2,1)} collective-permute-done((bf16[528,1024]{1,0:T(8,128)(2,1)}, bf16[528,1024]{1,0:T(8,128)(2,1)}, u32[]{:S(2)}, u32[]{:S(2)}) %collective-permute-start.8) | collective-permute-done | bytes 1081376 | tf_op jit(solution)/shard_map/ppermute | solution.py:97
  111.0 21.3 %collective-permute-done.12.refs_13_ = bf16[528,1024]{1,0:T(8,128)(2,1)} collective-permute-done((bf16[528,1024]{1,0:T(8,128)(2,1)S(1)}, bf16[528,1024]{1,0:T(8,128)(2,1)}, u32[]{:S(2)}, u32[]{:S(2)}) %collective-permute-start.12) | collective-permute-done | bytes 1081376 | tf_op jit(solution)/shard_map/ppermute | solution.py:97
  134.2 21.3 %collective-permute-done.4.refs_5_ = bf16[528,1024]{1,0:T(8,128)(2,1)} collective-permute-done((bf16[528,1024]{1,0:T(8,128)(2,1)}, bf16[528,1024]{1,0:T(8,128)(2,1)}, u32[]{:S(2)}, u32[]{:S(2)}) %collective-permute-start.4) | collective-permute-done | bytes 1081376 | tf_op jit(solution)/shard_map/ppermute | solution.py:97
  267.1 17.6 %collective-permute-start.27 = (bf16[528,2048]{1,0:T(8,128)(2,1)}, bf16[528,2048]{1,0:T(8,128)(2,1)}, u32[]{:S(2)}, u32[]{:S(2)}) collective-permute-start(bf16[528,2048]{1,0:T(8,128)(2,1)} %pad_maximum_fusion.7), channel_id=1, source_target_pairs={{0,0},{1,9},{2,2},{3,11},{4,4},{5,13},{6,6},{7,15},{8,8},{9,1},{10... | collective-permute-start | bytes 6488072 | tf_op jit(solution)/shard_map/ppermute | solution.py:97
  287.9 18.9 %collective-permute-done.16 = bf16[528,2048]{1,0:T(8,128)(2,1)} collective-permute-done((bf16[528,2048]{1,0:T(8,128)(2,1)}, bf16[528,2048]{1,0:T(8,128)(2,1)}, u32[]{:S(2)}, u32[]{:S(2)}) %collective-permute-start.16) | collective-permute-done | bytes 2162720 | tf_op jit(solution)/shard_map/ppermute | solution.py:97
  333.9 26.7 %collective-permute-done.36 = bf16[512,2048]{1,0:T(8,128)(2,1)} collective-permute-done((bf16[512,2048]{1,0:T(8,128)(2,1)}, bf16[512,2048]{1,0:T(8,128)(2,1)}, u32[]{:S(2)}, u32[]{:S(2)}) %collective-permute-start.36) | collective-permute-done | bytes 2097184 | tf_op jit(solution)/shard_map/ppermute | solution.py:97
  360.5 25.6 %collective-permute-start.44 = (bf16[512,2048]{1,0:T(8,128)(2,1)}, bf16[512,2048]{1,0:T(8,128)(2,1)}, u32[]{:S(2)}, u32[]{:S(2)}) collective-permute-start(bf16[512,2048]{1,0:T(8,128)(2,1)} %broadcast_select_fusion), channel_id=1, source_target_pairs={{0,0},{1,9},{2,2},{3,11},{4,4},{5,13},{6,6},{7,15},{8,8},{9,1},{10... | collective-permute-start | bytes 6291464 | tf_op jit(solution)/shard_map/ppermute | solution.py:97
  388.7 83.2 %collective-permute-start.20 = (bf16[2048,512]{1,0:T(8,128)(2,1)S(1)}, bf16[2048,512]{1,0:T(8,128)(2,1)S(1)}, u32[]{:S(2)}, u32[]{:S(2)}) collective-permute-start(bf16[2048,512]{1,0:T(8,128)(2,1)S(1)} %convert_bitcast_fusion.2), channel_id=1, source_target_pairs={{0,1},{1,0},{2,3},{3,2},{4,5},{5,4},{6,7},{7,6},{8,9},{9,8},{10,11... | collective-permute-start | bytes 6291464 | tf_op jit(solution)/shard_map/ppermute | solution.py:101
  501.2 40.2 %collective-permute-start.22 = (bf16[512,2048]{1,0:T(8,128)(2,1)S(1)}, bf16[512,2048]{1,0:T(8,128)(2,1)}, u32[]{:S(2)}, u32[]{:S(2)}) collective-permute-start(bf16[512,2048]{1,0:T(8,128)(2,1)S(1)} %copy-done.54), channel_id=1, source_target_pairs={{0,1},{1,0},{2,3},{3,2},{4,5},{5,4},{6,7},{7,6},{8,9},{9,8},{10,11... | collective-permute-start | bytes 6291464 | tf_op jit(solution)/shard_map/ppermute | solution.py:101
  809.0 19.7 %collective-permute-done.24 = bf16[512,2048]{1,0:T(8,128)(2,1)} collective-permute-done((bf16[512,2048]{1,0:T(8,128)(2,1)}, bf16[512,2048]{1,0:T(8,128)(2,1)}, u32[]{:S(2)}, u32[]{:S(2)}) %collective-permute-start.24) | collective-permute-done | bytes 2097184 | tf_op jit(solution)/shard_map/ppermute | solution.py:97
  841.3 76.0 %collective-permute-done.32 = bf16[512,2048]{1,0:T(8,128)(2,1)} collective-permute-done((bf16[512,2048]{1,0:T(8,128)(2,1)}, bf16[512,2048]{1,0:T(8,128)(2,1)}, u32[]{:S(2)}, u32[]{:S(2)}) %collective-permute-start.32) | collective-permute-done | bytes 2097184 | tf_op jit(solution)/shard_map/ppermute | solution.py:97
  933.2 14.3 collective-permute-start.82
  955.9 31.6 %collective-permute-done.23 = bf16[512,2048]{1,0:T(8,128)(2,1)} collective-permute-done((bf16[512,2048]{1,0:T(8,128)(2,1)}, bf16[512,2048]{1,0:T(8,128)(2,1)}, u32[]{:S(2)}, u32[]{:S(2)}) %collective-permute-start.23) | collective-permute-done | bytes 2097184 | tf_op jit(solution)/shard_map/ppermute | solution.py:97
  1002.9 27.5 %collective-permute-done.31 = bf16[512,2048]{1,0:T(8,128)(2,1)} collective-permute-done((bf16[512,2048]{1,0:T(8,128)(2,1)}, bf16[512,2048]{1,0:T(8,128)(2,1)}, u32[]{:S(2)}, u32[]{:S(2)}) %collective-permute-start.31) | collective-permute-done | bytes 2097184 | tf_op jit(solution)/shard_map/ppermute | solution.py:97
  1030.4 51.2 %collective-permute-start.81 = (f32[2048,512]{1,0:T(8,128)}, f32[2048,512]{1,0:T(8,128)}, u32[]{:S(2)}, u32[]{:S(2)}) collective-permute-start(f32[2048,512]{1,0:T(8,128)} %slice.480), channel_id=1, source_target_pairs={{0,1},{1,0},{2,3},{3,2},{4,5},{5,4},{6,7},{7,6},{8,9},{9,8},{10,11... | collective-permute-start | bytes 12582920 | tf_op jit(solution)/shard_map/ppermute | solution.py:101
  1088.1 17.1 %collective-permute-start.34 = (bf16[512,2048]{1,0:T(8,128)(2,1)}, bf16[512,2048]{1,0:T(8,128)(2,1)}, u32[]{:S(2)}, u32[]{:S(2)}) collective-permute-start(bf16[512,2048]{1,0:T(8,128)(2,1)} %add_convert_fusion.10), channel_id=1, source_target_pairs={{0,0},{1,9},{2,2},{3,11},{4,4},{5,13},{6,6},{7,15},{8,8},{9,1},{10... | collective-permute-start | bytes 6291464 | tf_op jit(solution)/shard_map/ppermute | solution.py:97
  1106.1 74.9 %collective-permute-start.52 = (bf16[528,2048]{1,0:T(8,128)(2,1)S(1)}, bf16[528,2048]{1,0:T(8,128)(2,1)}, u32[]{:S(2)}, u32[]{:S(2)}) collective-permute-start(bf16[528,2048]{1,0:T(8,128)(2,1)S(1)} %add_convert_fusion.2), channel_id=1, source_target_pairs={{0,1},{1,0},{2,3},{3,2},{4,5},{5,4},{6,7},{7,6},{8,9},{9,8},{10,11... | collective-permute-start | bytes 6488072 | tf_op jit(solution)/shard_map/ppermute | solution.py:101
  1203.3 25.2 %collective-permute-start.35 = (bf16[512,2048]{1,0:T(8,128)(2,1)S(1)}, bf16[512,2048]{1,0:T(8,128)(2,1)S(1)}, u32[]{:S(2)}, u32[]{:S(2)}) collective-permute-start(bf16[512,2048]{1,0:T(8,128)(2,1)S(1)} %add_convert_fusion.9), channel_id=1, source_target_pairs={{0,1},{1,0},{2,3},{3,2},{4,5},{5,4},{6,7},{7,6},{8,9},{9,8},{10,11... | collective-permute-start | bytes 6291464 | tf_op jit(solution)/shard_map/ppermute | solution.py:101
  1332.8 31.2 %collective-permute-done.75 = bf16[4,2,128,1024]{3,2,1,0:T(8,128)(2,1)} collective-permute-done((bf16[4,2,128,1024]{3,2,1,0:T(8,128)(2,1)}, bf16[4,2,128,1024]{3,2,1,0:T(8,128)(2,1)}, u32[]{:S(2)}, u32[]{:S(2)}) %collective-permute-start.75) | collective-permute-done | bytes 2097184 | tf_op jit(solution)/shard_map/ppermute | solution.py:97
  1383.4 56.3 %collective-permute-done.55 = f32[4,20,128]{2,0,1:T(4,128)S(1)} collective-permute-done((f32[4,20,128]{2,0,1:T(4,128)S(1)}, f32[4,20,128]{2,0,1:T(4,128)S(1)}, u32[]{:S(2)}, u32[]{:S(2)}) %collective-permute-start.55) | collective-permute-done | bytes 40992 | tf_op jit(solution)/shard_map/ppermute | solution.py:97
  1466.3 25.5 %collective-permute-done.65 = bf16[4,2,128,1024]{3,2,1,0:T(8,128)(2,1)} collective-permute-done((bf16[4,2,128,1024]{3,2,1,0:T(8,128)(2,1)}, bf16[4,2,128,1024]{3,2,1,0:T(8,128)(2,1)}, u32[]{:S(2)}, u32[]{:S(2)}) %collective-permute-start.65) | collective-permute-done | bytes 2097184 | tf_op jit(solution)/shard_map/ppermute | solution.py:97
  1502.8 15.5 collective-permute-done.71
  1562.2 19.4 %collective-permute-done.63 = bf16[128,1024]{1,0:T(8,128)(2,1)S(1)} collective-permute-done((bf16[128,1024]{1,0:T(8,128)(2,1)S(1)}, bf16[128,1024]{1,0:T(8,128)(2,1)S(1)}, u32[]{:S(2)}, u32[]{:S(2)}) %collective-permute-start.63) | collective-permute-done | bytes 262176 | tf_op jit(solution)/shard_map/ppermute | solution.py:97
  (699 shorter events, 752.2 us)
Async XLA Ops:
  333.9 138.9 %collective-permute-start.19 = (bf16[528,2048]{1,0:T(8,128)(2,1)}, bf16[528,2048]{1,0:T(8,128)(2,1)S(1)}, u32[]{:S(2)}, u32[]{:S(2)}) collective-permute-start(bf16[528,2048]{1,0:T(8,128)(2,1)} %collective-permute-done.17), channel_id=1, source_target_pairs={{0,4},{1,3},{2,6},{3,1},{4,0},{5,7},{6,2},{7,5},{8,12},{9,11},{10,... | collective-permute-start | bytes 6488072 | tf_op jit(solution)/shard_map/ppermute | solution.py:97
  360.5 121.9 %collective-permute-start.44 = (bf16[512,2048]{1,0:T(8,128)(2,1)}, bf16[512,2048]{1,0:T(8,128)(2,1)}, u32[]{:S(2)}, u32[]{:S(2)}) collective-permute-start(bf16[512,2048]{1,0:T(8,128)(2,1)} %broadcast_select_fusion), channel_id=1, source_target_pairs={{0,0},{1,9},{2,2},{3,11},{4,4},{5,13},{6,6},{7,15},{8,8},{9,1},{10... | collective-permute-start | bytes 6291464 | tf_op jit(solution)/shard_map/ppermute | solution.py:97
  386.2 96.8 %collective-permute-start.37 = (bf16[512,2048]{1,0:T(8,128)(2,1)}, bf16[512,2048]{1,0:T(8,128)(2,1)S(1)}, u32[]{:S(2)}, u32[]{:S(2)}) collective-permute-start(bf16[512,2048]{1,0:T(8,128)(2,1)} %collective-permute-done.36), channel_id=1, source_target_pairs={{0,2},{1,5},{2,0},{3,7},{4,6},{5,1},{6,4},{7,3},{8,10},{9,13},{10,... | collective-permute-start | bytes 6291464 | tf_op jit(solution)/shard_map/ppermute | solution.py:97
  387.5 96.0 %collective-permute-start.30 = (bf16[528,2048]{1,0:T(8,128)(2,1)}, bf16[528,2048]{1,0:T(8,128)(2,1)S(1)}, u32[]{:S(2)}, u32[]{:S(2)}) collective-permute-start(bf16[528,2048]{1,0:T(8,128)(2,1)} %collective-permute-done.28), channel_id=1, source_target_pairs={{0,4},{1,3},{2,6},{3,1},{4,0},{5,7},{6,2},{7,5},{8,12},{9,11},{10,... | collective-permute-start | bytes 6488072 | tf_op jit(solution)/shard_map/ppermute | solution.py:97
  388.7 112.4 %collective-permute-start.20 = (bf16[2048,512]{1,0:T(8,128)(2,1)S(1)}, bf16[2048,512]{1,0:T(8,128)(2,1)S(1)}, u32[]{:S(2)}, u32[]{:S(2)}) collective-permute-start(bf16[2048,512]{1,0:T(8,128)(2,1)S(1)} %convert_bitcast_fusion.2), channel_id=1, source_target_pairs={{0,1},{1,0},{2,3},{3,2},{4,5},{5,4},{6,7},{7,6},{8,9},{9,8},{10,11... | collective-permute-start | bytes 6291464 | tf_op jit(solution)/shard_map/ppermute | solution.py:101
  472.8 91.1 %collective-permute-start.21 = (bf16[2048,512]{1,0:T(8,128)(2,1)}, bf16[2048,512]{1,0:T(8,128)(2,1)}, u32[]{:S(2)}, u32[]{:S(2)}) collective-permute-start(bf16[2048,512]{1,0:T(8,128)(2,1)} %convert_bitcast_fusion.1), channel_id=1, source_target_pairs={{0,1},{1,0},{2,3},{3,2},{4,5},{5,4},{6,7},{7,6},{8,9},{9,8},{10,11... | collective-permute-start | bytes 6291464 | tf_op jit(solution)/shard_map/ppermute | solution.py:101
  550.8 90.3 %collective-permute-start.46 = (bf16[512,2048]{1,0:T(8,128)(2,1)}, bf16[512,2048]{1,0:T(8,128)(2,1)}, u32[]{:S(2)}, u32[]{:S(2)}) collective-permute-start(bf16[512,2048]{1,0:T(8,128)(2,1)} %collective-permute-done.44), channel_id=1, source_target_pairs={{0,4},{1,3},{2,6},{3,1},{4,0},{5,7},{6,2},{7,5},{8,12},{9,11},{10,... | collective-permute-start | bytes 6291464 | tf_op jit(solution)/shard_map/ppermute | solution.py:97
  550.8 102.4 %collective-permute-start.47 = (bf16[512,2048]{1,0:T(8,128)(2,1)}, bf16[512,2048]{1,0:T(8,128)(2,1)}, u32[]{:S(2)}, u32[]{:S(2)}) collective-permute-start(bf16[512,2048]{1,0:T(8,128)(2,1)} %collective-permute-done.45), channel_id=1, source_target_pairs={{0,4},{1,3},{2,6},{3,1},{4,0},{5,7},{6,2},{7,5},{8,12},{9,11},{10,... | collective-permute-start | bytes 6291464 | tf_op jit(solution)/shard_map/ppermute | solution.py:97
  789.4 129.7 %collective-permute-start.40 = (bf16[528,2048]{1,0:T(8,128)(2,1)S(1)}, bf16[528,2048]{1,0:T(8,128)(2,1)}, u32[]{:S(2)}, u32[]{:S(2)}) collective-permute-start(bf16[528,2048]{1,0:T(8,128)(2,1)S(1)} %pad_maximum_fusion.8), channel_id=1, source_target_pairs={{0,4},{1,3},{2,6},{3,1},{4,0},{5,7},{6,2},{7,5},{8,12},{9,11},{10,... | collective-permute-start | bytes 6488072 | tf_op jit(solution)/shard_map/ppermute | solution.py:97
  798.1 119.2 %collective-permute-start.32 = (bf16[512,2048]{1,0:T(8,128)(2,1)}, bf16[512,2048]{1,0:T(8,128)(2,1)}, u32[]{:S(2)}, u32[]{:S(2)}) collective-permute-start(bf16[512,2048]{1,0:T(8,128)(2,1)} %convolution_convert_fusion.10), channel_id=1, source_target_pairs={{0,4},{1,3},{2,6},{3,1},{4,0},{5,7},{6,2},{7,5},{8,12},{9,11},{10,... | collective-permute-start | bytes 6291464 | tf_op jit(solution)/shard_map/ppermute | solution.py:97
  802.9 148.3 %collective-permute-start.48 = (bf16[528,2048]{1,0:T(8,128)(2,1)S(1)}, bf16[528,2048]{1,0:T(8,128)(2,1)S(1)}, u32[]{:S(2)}, u32[]{:S(2)}) collective-permute-start(bf16[528,2048]{1,0:T(8,128)(2,1)S(1)} %pad_maximum_fusion.10), channel_id=1, source_target_pairs={{0,4},{1,3},{2,6},{3,1},{4,0},{5,7},{6,2},{7,5},{8,12},{9,11},{10,... | collective-permute-start | bytes 6488072 | tf_op jit(solution)/shard_map/ppermute | solution.py:97
  804.9 128.3 %collective-permute-start.42 = (bf16[528,2048]{1,0:T(8,128)(2,1)S(1)}, bf16[528,2048]{1,0:T(8,128)(2,1)S(1)}, u32[]{:S(2)}, u32[]{:S(2)}) collective-permute-start(bf16[528,2048]{1,0:T(8,128)(2,1)S(1)} %add_convert_fusion.6), channel_id=1, source_target_pairs={{0,2},{1,5},{2,0},{3,7},{4,6},{5,1},{6,4},{7,3},{8,10},{9,13},{10,... | collective-permute-start | bytes 6488072 | tf_op jit(solution)/shard_map/ppermute | solution.py:97
  828.6 124.2 %collective-permute-start.50 = (bf16[528,2048]{1,0:T(8,128)(2,1)S(1)}, bf16[528,2048]{1,0:T(8,128)(2,1)S(1)}, u32[]{:S(2)}, u32[]{:S(2)}) collective-permute-start(bf16[528,2048]{1,0:T(8,128)(2,1)S(1)} %add_convert_fusion.4), channel_id=1, source_target_pairs={{0,2},{1,5},{2,0},{3,7},{4,6},{5,1},{6,4},{7,3},{8,10},{9,13},{10,... | collective-permute-start | bytes 6488072 | tf_op jit(solution)/shard_map/ppermute | solution.py:97
  933.2 262.0 %collective-permute-start.82 = (f32[512,2048]{1,0:T(8,128)}, f32[512,2048]{1,0:T(8,128)}, u32[]{:S(2)}, u32[]{:S(2)}) collective-permute-start(f32[512,2048]{1,0:T(8,128)} %slice.482), channel_id=1, source_target_pairs={{0,1},{1,0},{2,3},{3,2},{4,5},{5,4},{6,7},{7,6},{8,9},{9,8},{10,11... | collective-permute-start | bytes 12582920 | tf_op jit(solution)/shard_map/ppermute | solution.py:101
  952.8 128.8 %collective-permute-start.33 = (bf16[512,2048]{1,0:T(8,128)(2,1)}, bf16[512,2048]{1,0:T(8,128)(2,1)}, u32[]{:S(2)}, u32[]{:S(2)}) collective-permute-start(bf16[512,2048]{1,0:T(8,128)(2,1)} %add_convert_fusion.11), channel_id=1, source_target_pairs={{0,2},{1,5},{2,0},{3,7},{4,6},{5,1},{6,4},{7,3},{8,10},{9,13},{10,... | collective-permute-start | bytes 6291464 | tf_op jit(solution)/shard_map/ppermute | solution.py:97
  987.5 100.5 %collective-permute-start.43 = (bf16[528,2048]{1,0:T(8,128)(2,1)S(1)}, bf16[528,2048]{1,0:T(8,128)(2,1)S(1)}, u32[]{:S(2)}, u32[]{:S(2)}) collective-permute-start(bf16[528,2048]{1,0:T(8,128)(2,1)S(1)} %add_convert_fusion.5), channel_id=1, source_target_pairs={{0,24},{1,17},{2,26},{3,19},{4,28},{5,21},{6,30},{7,23},{8,16},{9,... | collective-permute-start | bytes 6488072 | tf_op jit(solution)/shard_map/ppermute | solution.py:97
  987.5 117.6 %collective-permute-start.51 = (bf16[528,2048]{1,0:T(8,128)(2,1)S(1)}, bf16[528,2048]{1,0:T(8,128)(2,1)S(1)}, u32[]{:S(2)}, u32[]{:S(2)}) collective-permute-start(bf16[528,2048]{1,0:T(8,128)(2,1)S(1)} %add_convert_fusion.3), channel_id=1, source_target_pairs={{0,0},{1,9},{2,2},{3,11},{4,4},{5,13},{6,6},{7,15},{8,8},{9,1},{10... | collective-permute-start | bytes 6488072 | tf_op jit(solution)/shard_map/ppermute | solution.py:97
  1030.4 263.3 %collective-permute-start.81 = (f32[2048,512]{1,0:T(8,128)}, f32[2048,512]{1,0:T(8,128)}, u32[]{:S(2)}, u32[]{:S(2)}) collective-permute-start(f32[2048,512]{1,0:T(8,128)} %slice.480), channel_id=1, source_target_pairs={{0,1},{1,0},{2,3},{3,2},{4,5},{5,4},{6,7},{7,6},{8,9},{9,8},{10,11... | collective-permute-start | bytes 12582920 | tf_op jit(solution)/shard_map/ppermute | solution.py:101
  1081.6 118.6 %collective-permute-start.26 = (bf16[512,2048]{1,0:T(8,128)(2,1)}, bf16[512,2048]{1,0:T(8,128)(2,1)}, u32[]{:S(2)}, u32[]{:S(2)}) collective-permute-start(bf16[512,2048]{1,0:T(8,128)(2,1)} %add_convert_fusion.12), channel_id=1, source_target_pairs={{0,24},{1,17},{2,26},{3,19},{4,28},{5,21},{6,30},{7,23},{8,16},{9,... | collective-permute-start | bytes 6291464 | tf_op jit(solution)/shard_map/ppermute | solution.py:97
  1088.1 112.2 %collective-permute-start.34 = (bf16[512,2048]{1,0:T(8,128)(2,1)}, bf16[512,2048]{1,0:T(8,128)(2,1)}, u32[]{:S(2)}, u32[]{:S(2)}) collective-permute-start(bf16[512,2048]{1,0:T(8,128)(2,1)} %add_convert_fusion.10), channel_id=1, source_target_pairs={{0,0},{1,9},{2,2},{3,11},{4,4},{5,13},{6,6},{7,15},{8,8},{9,1},{10... | collective-permute-start | bytes 6291464 | tf_op jit(solution)/shard_map/ppermute | solution.py:97
  1106.1 122.4 %collective-permute-start.52 = (bf16[528,2048]{1,0:T(8,128)(2,1)S(1)}, bf16[528,2048]{1,0:T(8,128)(2,1)}, u32[]{:S(2)}, u32[]{:S(2)}) collective-permute-start(bf16[528,2048]{1,0:T(8,128)(2,1)S(1)} %add_convert_fusion.2), channel_id=1, source_target_pairs={{0,1},{1,0},{2,3},{3,2},{4,5},{5,4},{6,7},{7,6},{8,9},{9,8},{10,11... | collective-permute-start | bytes 6488072 | tf_op jit(solution)/shard_map/ppermute | solution.py:101
  1195.2 103.7 %collective-permute-start.80 = (f32[2048,512]{1,0:T(8,128)}, f32[2048,512]{1,0:T(8,128)}, u32[]{:S(2)}, u32[]{:S(2)}) collective-permute-start(f32[2048,512]{1,0:T(8,128)} %slice.478), channel_id=1, source_target_pairs={{0,1},{1,0},{2,3},{3,2},{4,5},{5,4},{6,7},{7,6},{8,9},{9,8},{10,11... | collective-permute-start | bytes 12582920 | tf_op jit(solution)/shard_map/ppermute | solution.py:101
  1369.1 86.8 %collective-permute-start.76 = (bf16[4,128,1024]{2,1,0:T(8,128)(2,1)}, bf16[4,128,1024]{2,1,0:T(8,128)(2,1)}, u32[]{:S(2)}, u32[]{:S(2)}) collective-permute-start(bf16[4,128,1024]{2,1,0:T(8,128)(2,1)} %fusion.72), channel_id=1, source_target_pairs={{0,2},{1,3},{2,0},{3,1},{4,6},{5,7},{6,4},{7,5},{8,10},{9,11},{10,... | collective-permute-start | bytes 3145736 | tf_op jit(solution)/shard_map/ppermute | solution.py:97
  1374.9 84.6 %collective-permute-start.70 = (bf16[4,2,128,1024]{3,2,1,0:T(8,128)(2,1)}, bf16[4,2,128,1024]{3,2,1,0:T(8,128)(2,1)}, u32[]{:S(2)}, u32[]{:S(2)}) collective-permute-start(bf16[4,2,128,1024]{3,2,1,0:T(8,128)(2,1)} %fusion.28), channel_id=1, source_target_pairs={{0,2},{1,3},{2,0},{3,1},{4,6},{5,7},{6,4},{7,5},{8,10},{9,11},{10,... | collective-permute-start | bytes 6291464 | tf_op jit(solution)/shard_map/ppermute | solution.py:97
  (203 other events, 5468.7 us)

commit v2 on v1

--- a/solution.py
+++ b/solution.py
@@ -1,3 +1,4 @@
+import functools
 import math
 
 import jax
@@ -99,6 +100,10 @@
 
 def swap(value):
     return lax.ppermute(value, "tensor", [(0, 1), (1, 0)])
+
+
+def both_cores(part):
+    return part.astype(jnp.float32) + swap(part).astype(jnp.float32)
 
 
 def spread(grid, base):
@@ -135,8 +140,7 @@
         part = grid.send(collect(grid, turns[turn]).astype(jnp.bfloat16), grid.planes_of(turn))
         part = part.astype(jnp.float32)
         total = part if total is None else total + part
-    total = total.astype(jnp.bfloat16)
-    return total.astype(jnp.float32) + swap(total).astype(jnp.float32)
+    return both_cores(total.astype(jnp.bfloat16))
 
 
 def scatter_rows(grid, value, axes, wire):
@@ -281,6 +285,375 @@
     return outs, backs, (rows, grad_rows, hidden_low, grad_gate, grad_up)
 
 
+def moe_kernel(
+    capacity,
+    experts,
+    own,
+    wg,
+    wu,
+    wd,
+    *refs,
+):
+    grads, refs = refs[:8], refs[8:]
+    parts, refs = refs[:8], refs[8:]
+    (
+    blocks,
+    far_sums,
+    near_sums,
+    plane_sums,
+    rows_out,
+    grows_out,
+    hidden_out,
+    gate_out,
+    up_out,
+    result,
+    wg_v,
+    wu_v,
+    wd_v,
+    block_v,
+    grad_v,
+    rows_v,
+    grows_v,
+    hidden_v,
+    gate_v,
+    up_v,
+    pick_v,
+    pick_t,
+    ordered,
+    stage,
+    part_v,
+    taken,
+    weight_sem,
+    load_sem,
+    save_sem,
+    send_sem,
+    recv_sem,
+    back_send,
+    back_recv,
+    ) = refs
+    me = lax.axis_index("expert")
+    core = lax.axis_index("tensor")
+    top, mid, low = me // 4, (me // 2) % 2, me % 2
+    flip_low = me + 1 - 2 * low
+    flip_mid = me + 2 - 4 * mid
+    first = flip_low + core * (flip_mid - flip_low)
+    second = flip_mid + core * (flip_low - flip_mid)
+    plane_one = me + 4 - 8 * (top % 2)
+    plane_two = me + 8 - 16 * (top // 2)
+    plane_three = me + 12 - 8 * top
+    far_plane = plane_three + core * (plane_two - plane_three)
+    mesh = pl.DeviceIdType.MESH
+
+    barrier = pltpu.get_barrier_semaphore()
+    for device in (first, second, plane_one, plane_two, plane_three):
+        pl.semaphore_signal(barrier, inc=1, device_id=(device, core), device_id_type=mesh)
+    pl.semaphore_wait(barrier, 5)
+
+    def pass_on(source, slot, device):
+        return pltpu.make_async_remote_copy(
+            src_ref=source,
+            dst_ref=blocks.at[slot],
+            send_sem=send_sem.at[slot],
+            recv_sem=recv_sem.at[slot],
+            device_id=(device, core),
+            device_id_type=mesh,
+        )
+
+    def give(source, target, index, device):
+        return pltpu.make_async_remote_copy(
+            src_ref=source,
+            dst_ref=target,
+            send_sem=back_send.at[index],
+            recv_sem=back_recv.at[index],
+            device_id=(device, core),
+            device_id_type=mesh,
+        )
+
+    loads = [
+        pltpu.make_async_copy(source, target, weight_sem.at[index])
+        for index, (source, target) in enumerate(((wg, wg_v), (wu, wu_v), (wd, wd_v)))
+    ]
+
+    @pl.when(core == 0)
+    def _():
+        pass_on(own, 1, first).start()
+        pass_on(own, 2, second).start()
+
+    @pl.when(core == 1)
+    def _():
+        pass_on(own, 0, plane_one).start()
+
+    pass_on(own, 4, far_plane).start()
+    for copy in loads:
+        copy.start()
+
+    length = SEQ
+    ordered[...] = jnp.where(
+        lax.broadcasted_iota(jnp.int32, (length, length), 0)
+        < lax.broadcasted_iota(jnp.int32, (length, length), 1),
+        1.0,
+        0.0,
+    ).astype(jnp.bfloat16)
+    width = block_v.shape[1]
+    hidden = hidden_v.shape[1]
+    both = (((1,), (1,)), ((), ()))
+
+    def dot(left, right):
+        return jnp.dot(left, right, preferred_element_type=jnp.float32)
+
+    def dot_t(left, right):
+        return lax.dot_general(left, right, both, preferred_element_type=jnp.float32)
+
+    def add_block(slot, sources):
+        for index, source in enumerate(sources):
+            pltpu.make_async_copy(source, taken.at[index], load_sem.at[2 + index]).start()
+        for index, source in enumerate(sources):
+            pltpu.make_async_copy(source, taken.at[index], load_sem.at[2 + index]).wait()
+
+        def rows_of(step, carry):
+            span = pl.ds(pl.multiple_of(step * 16, 16), 16)
+            total = stage[slot, span, :].astype(jnp.float32)
+            for index in range(len(sources)):
+                total = total + taken[index, span, :].astype(jnp.float32)
+            stage[slot, span, :] = total.astype(jnp.bfloat16)
+            return carry
+
+        lax.fori_loop(0, (length + experts) // 16, rows_of, 0)
+
+    def first_sum(turn):
+        give(far_sums.at[2 * turn + 1], far_sums.at[2 * turn + 1], 2 * turn + 1, second).wait_recv()
+        add_block(4 * turn + 1, [far_sums.at[2 * turn + 1]])
+        give(stage.at[4 * turn + 1], near_sums.at[turn], 4 + turn, first).start()
+
+    def plane_sum(turn):
+        give(far_sums.at[2 * turn], far_sums.at[2 * turn], 2 * turn, second).wait_recv()
+        give(near_sums.at[turn], near_sums.at[turn], 4 + turn, first).wait_recv()
+        add_block(4 * turn, [far_sums.at[2 * turn], near_sums.at[turn]])
+
+    def block_step(k, carry):
+        turn_at = k % 4
+        relayed = jnp.logical_or(k != 0, core != 0)
+
+        @pl.when(relayed)
+        def _():
+            pass_on(blocks.at[k], k, first).wait_recv()
+            pltpu.make_async_copy(blocks.at[k], block_v, load_sem.at[0]).start()
+
+        @pl.when(jnp.logical_not(relayed))
+        def _():
+            pltpu.make_async_copy(own, block_v, load_sem.at[0]).start()
+
+        @pl.when(jnp.logical_and(relayed, turn_at == 0))
+        def _():
+            pass_on(blocks.at[k], k + 1, first).start()
+
+        @pl.when(jnp.logical_and(relayed, turn_at < 2))
+        def _():
+            pass_on(blocks.at[k], k + 2, second).start()
+
+        for index in range(8):
+
+            @pl.when(k == index)
+            def _():
+                pltpu.make_async_copy(grads[index], grad_v, load_sem.at[1]).start()
+
+
+        @pl.when(k == 0)
+        def _():
+            for copy in loads:
+                copy.wait()
+
+        pltpu.make_async_copy(blocks.at[k], block_v, load_sem.at[0]).wait()
+
+        here = lax.broadcasted_iota(jnp.int32, (experts, 3 * length), 0) == me
+        row = jnp.sum(
+            jnp.where(here, block_v[length:, : 3 * length].astype(jnp.float32), 0.0),
+            axis=0,
+            keepdims=True,
+        )
+        gate = row[:, :length] + row[:, length : 2 * length] + row[:, 2 * length :]
+        used = jnp.where(gate > 0.0, 1.0, 0.0)
+        slot = dot(jnp.broadcast_to(used, (16, length)).astype(jnp.bfloat16), ordered[...])[:1]
+        slot = jnp.where(gate > 0.0, slot, -1.0)
+        number = lax.broadcasted_iota(jnp.int32, (capacity, length), 0).astype(jnp.float32)
+        pick = jnp.where(number == slot, 1.0, 0.0)
+        slot_gate = jnp.sum(pick * gate, axis=1, keepdims=True)
+        pick_v[...] = pick.astype(jnp.bfloat16)
+        pick_t[...] = pick.T.astype(jnp.bfloat16)
+        for at in range(0, width, 512):
+            span = slice(at, at + 512)
+            rows_v[:, span] = dot(pick_v[...], block_v[:length, span]).astype(jnp.bfloat16)
+        pltpu.make_async_copy(grads[0], grad_v, load_sem.at[1]).wait()
+        for at in range(0, width, 512):
+            span = slice(at, at + 512)
+            grows_v[:, span] = dot(pick_v[...], grad_v[:, span]).astype(jnp.bfloat16)
+        slot_grad = jnp.zeros((capacity, 1), jnp.float32)
+        for at in range(0, hidden, 256):
+            span = slice(at, at + 256)
+            gate_lin = dot(rows_v[...], wg_v[:, span])
+            up_lin = dot(rows_v[...], wu_v[:, span])
+            grad_full = dot_t(grows_v[...], wd_v[span, :])
+            sigmoid_gate = 1.0 / (1.0 + jnp.exp(-gate_lin))
+            activated = gate_lin * sigmoid_gate
+            value = activated * up_lin
+            hidden_v[:, span] = (value * slot_gate).astype(jnp.bfloat16)
+            slot_grad = slot_grad + jnp.sum(value * grad_full, axis=1, keepdims=True)
+            grad_hidden = grad_full * slot_gate
+            slope = sigmoid_gate * (1.0 + gate_lin * (1.0 - sigmoid_gate))
+            gate_v[:, span] = (grad_hidden * up_lin * slope).astype(jnp.bfloat16)
+            up_v[:, span] = (grad_hidden * activated).astype(jnp.bfloat16)
+        at = pl.multiple_of(k * capacity, capacity)
+        saves = [
+            pltpu.make_async_copy(source, target.at[pl.ds(at, capacity)], save_sem.at[index])
+            for index, (source, target) in enumerate(
+                (
+                    (rows_v, rows_out),
+                    (grows_v, grows_out),
+                    (hidden_v, hidden_out),
+                    (gate_v, gate_out),
+                    (up_v, up_out),
+                )
+            )
+        ]
+        for copy in saves:
+            copy.start()
+
+        @pl.when(k > 0)
+        def _():
+            pltpu.make_async_copy(part_v, parts[0], save_sem.at[5]).wait()
+
+        for at in range(0, width, 512):
+            span = slice(at, at + 512)
+            value = dot(hidden_v[...], wd_v[:, span]).astype(jnp.bfloat16)
+            part_v[:, span] = dot(pick_t[...], value).astype(jnp.bfloat16)
+            back = dot_t(gate_v[...], wg_v[span, :]) + dot_t(up_v[...], wu_v[span, :])
+            stage[k, :length, span] = dot(pick_t[...], back.astype(jnp.bfloat16)).astype(
+                jnp.bfloat16
+            )
+        total = jnp.sum(pick_v[...].astype(jnp.float32) * slot_grad, axis=0, keepdims=True)
+        here = lax.broadcasted_iota(jnp.int32, (experts, length), 0) == me
+        for index in range(3):
+            high = total.astype(jnp.bfloat16).astype(jnp.float32)
+            stage[k, length:, index * length : (index + 1) * length] = jnp.where(
+                here, high, 0.0
+            ).astype(jnp.bfloat16)
+            total = total - high
+        stage[k, length:, 3 * length :] = jnp.zeros((experts, width - 3 * length), jnp.bfloat16)
+        for index in range(8):
+
+            @pl.when(k == index)
+            def _():
+                pltpu.make_async_copy(part_v, parts[index], save_sem.at[5]).start()
+
+        @pl.when(turn_at >= 2)
+        def _():
+            index = 2 * (k // 4) + turn_at - 2
+            give(stage.at[k], far_sums.at[index], index, second).start()
+
+        @pl.when(k == 5)
+        def _():
+            first_sum(0)
+
+        @pl.when(k == 6)
+        def _():
+            plane_sum(0)
+
+            @pl.when(core == 1)
+            def _():
+                give(stage.at[0], plane_sums.at[0], 6, plane_one).start()
+
+        for copy in saves:
+            copy.wait()
+        return carry
+
+    lax.fori_loop(0, 8, block_step, 0)
+    first_sum(1)
+    plane_sum(1)
+    give(stage.at[4], plane_sums.at[1], 7, far_plane).start()
+    give(stage.at[4], plane_sums.at[1], 7, far_plane).wait_recv()
+
+    @pl.when(core == 1)
+    def _():
+        give(stage.at[0], plane_sums.at[0], 6, plane_one).wait()
+        pltpu.make_async_copy(plane_sums.at[0], stage.at[0], load_sem.at[0]).start()
+        pltpu.make_async_copy(plane_sums.at[0], stage.at[0], load_sem.at[0]).wait()
+
+    add_block(0, [plane_sums.at[1]])
+    final = pltpu.make_async_copy(stage.at[0], result, load_sem.at[0])
+    final.start()
+    pltpu.make_async_copy(part_v, parts[7], save_sem.at[5]).wait()
+    for k in range(8):
+        if k > 0:
+            pass_on(blocks.at[k], k, first).wait_send()
+    @pl.when(core == 1)
+    def _():
+        pass_on(blocks.at[0], 0, first).wait_send()
+
+    for index in range(8):
+        if index != 6:
+            give(result, result, index, first).wait_send()
+    final.wait()
+
+
+def moe_layer(own, grads, wg, wu, wd, capacity):
+    rows, width = own.shape
+    hidden = wg.shape[1]
+    experts = rows - SEQ
+    low = jnp.bfloat16
+    hbm = pl.BlockSpec(memory_space=pl.ANY)
+
+    def shape(*dims):
+        return jax.ShapeDtypeStruct(dims, low)
+
+    return pl.pallas_call(
+        functools.partial(moe_kernel, capacity, experts),
+        in_specs=[hbm] * 12,
+        out_specs=[hbm] * 18,
+        out_shape=[shape(SEQ, width)] * 8
+        + [
+            shape(8, rows, width),
+            shape(4, rows, width),
+            shape(2, rows, width),
+            shape(2, rows, width),
+            shape(8 * capacity, width),
+            shape(8 * capacity, width),
+            shape(8 * capacity, hidden),
+            shape(8 * capacity, hidden),
+            shape(8 * capacity, hidden),
+            shape(rows, width),
+        ],
+        scratch_shapes=[
+            pltpu.VMEM((width, hidden), low),
+            pltpu.VMEM((width, hidden), low),
+            pltpu.VMEM((hidden, width), low),
+            pltpu.VMEM((rows, width), low),
+            pltpu.VMEM((SEQ, width), low),
+            pltpu.VMEM((capacity, width), low),
+            pltpu.VMEM((capacity, width), low),
+            pltpu.VMEM((capacity, hidden), low),
+            pltpu.VMEM((capacity, hidden), low),
+            pltpu.VMEM((capacity, hidden), low),
+            pltpu.VMEM((capacity, SEQ), low),
+            pltpu.VMEM((SEQ, capacity), low),
+            pltpu.VMEM((SEQ, SEQ), low),
+            pltpu.VMEM((8, rows, width), low),
+            pltpu.VMEM((SEQ, width), low),
+            pltpu.VMEM((2, rows, width), low),
+            pltpu.SemaphoreType.DMA((3,)),
+            pltpu.SemaphoreType.DMA((4,)),
+            pltpu.SemaphoreType.DMA((6,)),
+            pltpu.SemaphoreType.DMA((8,)),
+            pltpu.SemaphoreType.DMA((8,)),
+            pltpu.SemaphoreType.DMA((8,)),
+            pltpu.SemaphoreType.DMA((8,)),
+        ],
+        compiler_params=pltpu.CompilerParams(
+            collective_id=0, has_side_effects=True, vmem_limit_bytes=67043328
+        ),
+        name="moe_layer",
+    )(own, wg, wu, wd, *grads)
+
+
 def local(
     tokens,
     lengths,
@@ -405,16 +778,23 @@
     gates_wide = jnp.sum(jnp.where(route_hot, gates[:, :, None], 0.0), axis=1)
 
     gate_rows = jnp.pad(split_three(gates_wide.T), ((0, 0), (0, D - 3 * SEQ)))
-    token_turns = gather_tokens(grid, jnp.concatenate([ffn_in, gate_rows], axis=0))
-    out_turns, back_turns, saved = [], [], []
-    for turn in range(2):
-        outs, backs, kept = expert_turn(
-            token_turns[turn], grad_turns[turn], (wg, wu, wd), capacity
-        )
-        out_turns.append(outs)
-        back_turns.append(backs)
-        saved.append(kept)
-    back_sum = scatter_tokens(grid, back_turns)
+    token_block = jnp.concatenate([ffn_in, gate_rows], axis=0)
+    if grid.side == 2:
+        done = moe_layer(token_block, grad_turns[0] + grad_turns[1], wg, wu, wd, capacity)
+        saved = [tuple(done[12:17])]
+        out_turns = [done[:4], done[4:8]]
+        back_sum = both_cores(done[17])
+    else:
+        token_turns = gather_tokens(grid, token_block)
+        out_turns, back_turns, saved = [], [], []
+        for turn in range(2):
+            outs, backs, kept = expert_turn(
+                token_turns[turn], grad_turns[turn], (wg, wu, wd), capacity
+            )
+            out_turns.append(outs)
+            back_turns.append(backs)
+            saved.append(kept)
+        back_sum = scatter_tokens(grid, back_turns)
     out_sum = scatter_tokens(grid, out_turns)
     output = (resid_one + out_sum).astype(low)
 

time: 1600 us -> 1480 us (0.925)
  Pallas kernels: 13.3 us -> 384 us
  matrix products: 346 us -> 112 us
  starting transfers between devices: 455 us -> 273 us
  waiting for transfers between devices: 568 us -> 511 us
    pallas_call x0 -> x1, Pallas kernels: none -> 371 us  [moe_layer(): pl.pallas_call(functools.partial(moe_kernel, capacity, experts), in_specs...]
    ppermute x11, starting transfers between devices: 300 us -> 174 us  [swap(): return lax.ppermute(value, 'tensor', [(0, 1), (1, 0)])]
    dot_general x24 -> x0, matrix products: 102 us -> none  [the longest x8 27.7 us: expert_turn(): jnp.dot(pick[i], block, preferred_element_type=jnp.float32)]
    dot_general x11 -> x5, matrix products: 88.7 us -> 19.2 us  [contract_cols(): lax.dot_general(left_mat, right_mat, (((1,), (1,)), ((), ())), preferred_...]
    dot_general x27 -> x8, matrix products: 124 us -> 60.7 us  [contract_rows(): lax.dot_general(left_mat, right_mat, (((0,), (0,)), ((), ())), preferred_...]
    ppermute x72 -> x56, starting transfers between devices: 155 us -> 98.5 us  [send(): return lax.ppermute(value, ('expert', 'tensor'), pairs)]
    ppermute x72 -> x56, waiting for transfers between devices: 561 us -> 511 us  [send(): return lax.ppermute(value, ('expert', 'tensor'), pairs)]
    convert_element_type x12 -> x1, other arithmetic: 22.5 us -> 3.17 us  [scatter_tokens(): return both_cores(total.astype(jnp.bfloat16))]
  transfers between devices with their start and end apart: 83 -> 67, of which waited for: 26 -> 26; matrix products, arithmetic and copies ran while one was open for 24% -> 18% of each run, Pallas kernels for 0% -> 1%
where the time goes in v2:
time: 1480 us; the launch traced here: 1470 us
  waiting for transfers between devices  511 us (35%)
  Pallas kernels  384 us (26%)
  starting transfers between devices  273 us (18%)
  other arithmetic  132 us (9%)
  matrix products  112 us (8%)
  local copies, waits for them, and re-layouts  53.8 us (4%)
    ppermute x56, waiting for transfers between devices, send(): return lax.ppermute(value, ('expert', 'tensor'), pairs)  511 us
    pallas_call x1, Pallas kernels, moe_layer(): pl.pallas_call(functools.partial(moe_kernel, capacity, experts), in_specs...  371 us
    ppermute x11, starting transfers between devices, swap(): return lax.ppermute(value, 'tensor', [(0, 1), (1, 0)])  174 us
    ppermute x56, starting transfers between devices, send(): return lax.ppermute(value, ('expert', 'tensor'), pairs)  98.5 us
    dot_general x8, matrix products, contract_rows(): lax.dot_general(left_mat, right_mat, (((0,), (0,)), ((), ())), preferred_...  60.7 us
  transfers between devices with their start and end apart: 67, of which 26 were waited for; matrix products, arithmetic and copies ran while one was open for 18% of the time, Pallas kernels for 1%

profile of v2, /device:TPU:0, one launch (start us, length us, event | category | flops | bytes accessed | tf_op | source)
XLA Modules:
  0.0 1468.5 jit_solution(5317055482778639108)
XLA Ops:
  15.8 21.2 %collective-permute-done.11.refs_12_ = bf16[528,1024]{1,0:T(8,128)(2,1)} collective-permute-done((bf16[528,1024]{1,0:T(8,128)(2,1)S(1)}, bf16[528,1024]{1,0:T(8,128)(2,1)}, u32[]{:S(2)}, u32[]{:S(2)}) %collective-permute-start.11) | collective-permute-done | bytes 1081376 | tf_op jit(solution)/shard_map/ppermute | solution.py:98
  38.6 66.0 %collective-permute-done.7.refs_8_ = bf16[528,1024]{1,0:T(8,128)(2,1)} collective-permute-done((bf16[528,1024]{1,0:T(8,128)(2,1)S(1)}, bf16[528,1024]{1,0:T(8,128)(2,1)}, u32[]{:S(2)}, u32[]{:S(2)}) %collective-permute-start.7) | collective-permute-done | bytes 1081376 | tf_op jit(solution)/shard_map/ppermute | solution.py:98
  112.9 40.1 %collective-permute-done.8.refs_9_ = bf16[528,1024]{1,0:T(8,128)(2,1)} collective-permute-done((bf16[528,1024]{1,0:T(8,128)(2,1)}, bf16[528,1024]{1,0:T(8,128)(2,1)}, u32[]{:S(2)}, u32[]{:S(2)}) %collective-permute-start.8) | collective-permute-done | bytes 1081376 | tf_op jit(solution)/shard_map/ppermute | solution.py:98
  214.8 13.3 assemble.1
  247.1 17.3 %collective-permute-start.19 = (bf16[512,2048]{1,0:T(8,128)(2,1)}, bf16[512,2048]{1,0:T(8,128)(2,1)}, u32[]{:S(2)}, u32[]{:S(2)}) collective-permute-start(bf16[512,2048]{1,0:T(8,128)(2,1)} %broadcast_select_fusion), channel_id=1, source_target_pairs={{0,0},{1,9},{2,2},{3,11},{4,4},{5,13},{6,6},{7,15},{8,8},{9,1},{10... | collective-permute-start | bytes 6291464 | tf_op jit(solution)/shard_map/ppermute | solution.py:98
  289.1 41.4 %collective-permute-done.23.refs_4_ = bf16[512,2048]{1,0:T(8,128)(2,1)} collective-permute-done((bf16[512,2048]{1,0:T(8,128)(2,1)}, bf16[512,2048]{1,0:T(8,128)(2,1)}, u32[]{:S(2)}, u32[]{:S(2)}) %collective-permute-start.23) | collective-permute-done | bytes 2097184 | tf_op jit(solution)/shard_map/ppermute | solution.py:98
  374.1 42.2 %collective-permute-done.25.refs_6_ = bf16[512,2048]{1,0:T(8,128)(2,1)} collective-permute-done((bf16[512,2048]{1,0:T(8,128)(2,1)}, bf16[512,2048]{1,0:T(8,128)(2,1)}, u32[]{:S(2)}, u32[]{:S(2)}) %collective-permute-start.25) | collective-permute-done | bytes 2097184 | tf_op jit(solution)/shard_map/ppermute | solution.py:98
  416.3 25.2 %collective-permute-done.22.refs_3_ = bf16[512,2048]{1,0:T(8,128)(2,1)} collective-permute-done((bf16[512,2048]{1,0:T(8,128)(2,1)}, bf16[512,2048]{1,0:T(8,128)(2,1)}, u32[]{:S(2)}, u32[]{:S(2)}) %collective-permute-start.22) | collective-permute-done | bytes 2097184 | tf_op jit(solution)/shard_map/ppermute | solution.py:98
  441.5 22.5 %collective-permute-done.26.refs_7_ = bf16[512,2048]{1,0:T(8,128)(2,1)} collective-permute-done((bf16[512,2048]{1,0:T(8,128)(2,1)}, bf16[512,2048]{1,0:T(8,128)(2,1)}, u32[]{:S(2)}, u32[]{:S(2)}) %collective-permute-start.26) | collective-permute-done | bytes 2097184 | tf_op jit(solution)/shard_map/ppermute | solution.py:98
  464.0 370.6 %moe_layer.1 = (bf16[512,2048]{1,0:T(8,128)(2,1)}, bf16[512,2048]{1,0:T(8,128)(2,1)}, bf16[512,2048]{1,0:T(8,128)(2,1)}, bf16[512,2048]{1,0:T(8,128)(2,1)}, bf16...) custom-call(bf16[528,2048]{1,0:T(8,128)(2,1)} %pad_maximum_fusion.3., ...), custom_call_target="tpu_custom_call" | custom-call | tf_op jit(solution)/shard_map/moe_layer/pallas_call | solution.py:608
  840.4 14.4 fusion.135
  855.3 70.4 %collective-permute-start.66 = (f32[512,2048]{1,0:T(8,128)S(1)}, f32[512,2048]{1,0:T(8,128)S(1)}, u32[]{:S(2)}, u32[]{:S(2)}) collective-permute-start(f32[512,2048]{1,0:T(8,128)S(1)} %slice.138), channel_id=1, source_target_pairs={{0,1},{1,0},{2,3},{3,2},{4,5},{5,4},{6,7},{7,6},{8,9},{9,8},{10,11... | collective-permute-start | bytes 12582920 | tf_op jit(solution)/shard_map/ppermute | solution.py:102
  934.0 14.6 fusion.134
  953.4 14.6 collective-permute-done.27
  968.0 50.0 %collective-permute-start.65 = (f32[2048,512]{1,0:T(8,128)}, f32[2048,512]{1,0:T(8,128)}, u32[]{:S(2)}, u32[]{:S(2)}) collective-permute-start(f32[2048,512]{1,0:T(8,128)} %slice.136), channel_id=1, source_target_pairs={{0,1},{1,0},{2,3},{3,2},{4,5},{5,4},{6,7},{7,6},{8,9},{9,8},{10,11... | collective-permute-start | bytes 12582920 | tf_op jit(solution)/shard_map/ppermute | solution.py:102
  1029.9 17.1 %collective-permute-start.34 = (bf16[512,2048]{1,0:T(8,128)(2,1)}, bf16[512,2048]{1,0:T(8,128)(2,1)}, u32[]{:S(2)}, u32[]{:S(2)}) collective-permute-start(bf16[512,2048]{1,0:T(8,128)(2,1)} %add_convert_fusion.3), channel_id=1, source_target_pairs={{0,0},{1,9},{2,2},{3,11},{4,4},{5,13},{6,6},{7,15},{8,8},{9,1},{10... | collective-permute-start | bytes 6291464 | tf_op jit(solution)/shard_map/ppermute | solution.py:98
  1047.0 14.4 fusion.133
  1073.5 50.2 %collective-permute-start.35 = (bf16[512,2048]{1,0:T(8,128)(2,1)S(1)}, bf16[512,2048]{1,0:T(8,128)(2,1)S(1)}, u32[]{:S(2)}, u32[]{:S(2)}) collective-permute-start(bf16[512,2048]{1,0:T(8,128)(2,1)S(1)} %add_convert_fusion.2), channel_id=1, source_target_pairs={{0,1},{1,0},{2,3},{3,2},{4,5},{5,4},{6,7},{7,6},{8,9},{9,8},{10,11... | collective-permute-start | bytes 6291464 | tf_op jit(solution)/shard_map/ppermute | solution.py:102
  1231.7 21.5 %collective-permute-done.59 = bf16[4,2,128,1024]{3,2,1,0:T(8,128)(2,1)} collective-permute-done((bf16[4,2,128,1024]{3,2,1,0:T(8,128)(2,1)}, bf16[4,2,128,1024]{3,2,1,0:T(8,128)(2,1)}, u32[]{:S(2)}, u32[]{:S(2)}) %collective-permute-start.59) | collective-permute-done | bytes 2097184 | tf_op jit(solution)/shard_map/ppermute | solution.py:98
  1271.1 56.7 %collective-permute-done.39 = f32[4,20,128]{2,0,1:T(4,128)S(1)} collective-permute-done((f32[4,20,128]{2,0,1:T(4,128)S(1)}, f32[4,20,128]{2,0,1:T(4,128)S(1)}, u32[]{:S(2)}, u32[]{:S(2)}) %collective-permute-start.39) | collective-permute-done | bytes 40992 | tf_op jit(solution)/shard_map/ppermute | solution.py:98
  1352.5 27.3 %collective-permute-done.49 = bf16[4,2,128,1024]{3,2,1,0:T(8,128)(2,1)} collective-permute-done((bf16[4,2,128,1024]{3,2,1,0:T(8,128)(2,1)}, bf16[4,2,128,1024]{3,2,1,0:T(8,128)(2,1)}, u32[]{:S(2)}, u32[]{:S(2)}) %collective-permute-start.49) | collective-permute-done | bytes 2097184 | tf_op jit(solution)/shard_map/ppermute | solution.py:98
  1389.8 16.3 %collective-permute-done.55 = bf16[4,128,1024]{2,1,0:T(8,128)(2,1)S(1)} collective-permute-done((bf16[4,128,1024]{2,1,0:T(8,128)(2,1)S(1)}, bf16[4,128,1024]{2,1,0:T(8,128)(2,1)S(1)}, u32[]{:S(2)}, u32[]{:S(2)}) %collective-permute-start.55) | collective-permute-done | bytes 1048608 | tf_op jit(solution)/shard_map/ppermute | solution.py:98
  1411.0 14.0 collective-permute-done.50
  1449.0 18.4 %collective-permute-done.47 = bf16[128,1024]{1,0:T(8,128)(2,1)S(1)} collective-permute-done((bf16[128,1024]{1,0:T(8,128)(2,1)S(1)}, bf16[128,1024]{1,0:T(8,128)(2,1)S(1)}, u32[]{:S(2)}, u32[]{:S(2)}) %collective-permute-start.47) | collective-permute-done | bytes 262176 | tf_op jit(solution)/shard_map/ppermute | solution.py:98
  (486 shorter events, 405.8 us)
Async XLA Ops:
  12.0 92.6 %collective-permute-start.7 = (bf16[528,1024]{1,0:T(8,128)(2,1)S(1)}, bf16[528,1024]{1,0:T(8,128)(2,1)}, u32[]{:S(2)}, u32[]{:S(2)}) collective-permute-start(bf16[528,1024]{1,0:T(8,128)(2,1)S(1)} %fusion.93.refs_0_), channel_id=1, source_target_pairs={{0,16},{1,17},{2,18},{3,19},{4,20},{5,21},{6,22},{7,23},{8,24},{9,... | collective-permute-start | bytes 3244040 | tf_op jit(solution)/shard_map/ppermute | solution.py:98
  12.0 94.2 %collective-permute-start.3 = (bf16[528,1024]{1,0:T(8,128)(2,1)S(1)}, bf16[528,1024]{1,0:T(8,128)(2,1)}, u32[]{:S(2)}, u32[]{:S(2)}) collective-permute-start(bf16[528,1024]{1,0:T(8,128)(2,1)S(1)} %fusion.93.refs_0_), channel_id=1, source_target_pairs={{0,8},{1,9},{2,10},{3,11},{4,12},{5,13},{6,14},{7,15},{8,0},{9,1},... | collective-permute-start | bytes 3244040 | tf_op jit(solution)/shard_map/ppermute | solution.py:98
  12.6 95.0 %collective-permute-start = (bf16[528,1024]{1,0:T(8,128)(2,1)S(1)}, bf16[528,1024]{1,0:T(8,128)(2,1)S(1)}, u32[]{:S(2)}, u32[]{:S(2)}) collective-permute-start(bf16[528,1024]{1,0:T(8,128)(2,1)S(1)} %fusion.93.refs_0_), channel_id=1, source_target_pairs={{0,2},{1,5},{2,0},{3,7},{4,6},{5,1},{6,4},{7,3},{8,10},{9,13},{10,... | collective-permute-start | bytes 3244040 | tf_op jit(solution)/shard_map/ppermute | solution.py:98
  14.3 93.9 %collective-permute-start.1 = (bf16[528,1024]{1,0:T(8,128)(2,1)S(1)}, bf16[528,1024]{1,0:T(8,128)(2,1)S(1)}, u32[]{:S(2)}, u32[]{:S(2)}) collective-permute-start(bf16[528,1024]{1,0:T(8,128)(2,1)S(1)} %fusion.93.refs_0_), channel_id=1, source_target_pairs={{0,4},{1,3},{2,6},{3,1},{4,0},{5,7},{6,2},{7,5},{8,12},{9,11},{10,... | collective-permute-start | bytes 3244040 | tf_op jit(solution)/shard_map/ppermute | solution.py:98
  36.9 117.6 %collective-permute-start.12 = (bf16[528,1024]{1,0:T(8,128)(2,1)}, bf16[528,1024]{1,0:T(8,128)(2,1)}, u32[]{:S(2)}, u32[]{:S(2)}) collective-permute-start(bf16[528,1024]{1,0:T(8,128)(2,1)} %collective-permute-done.11.refs_12_), channel_id=1, source_target_pairs={{0,2},{1,5},{2,0},{3,7},{4,6},{5,1},{6,4},{7,3},{8,10},{9,13},{10,... | collective-permute-start | bytes 3244040 | tf_op jit(solution)/shard_map/ppermute | solution.py:98
  157.1 57.7 %collective-permute-start.6 = (bf16[528,1024]{1,0:T(8,128)(2,1)}, bf16[528,1024]{1,0:T(8,128)(2,1)}, u32[]{:S(2)}, u32[]{:S(2)}) collective-permute-start(bf16[528,1024]{1,0:T(8,128)(2,1)} %collective-permute-done.4.refs_5_), channel_id=1, source_target_pairs={{0,4},{1,3},{2,6},{3,1},{4,0},{5,7},{6,2},{7,5},{8,12},{9,11},{10,... | collective-permute-start | bytes 3244040 | tf_op jit(solution)/shard_map/ppermute | solution.py:98
  168.5 118.6 %collective-permute-start.16 = (bf16[2048,512]{1,0:T(8,128)(2,1)}, bf16[2048,512]{1,0:T(8,128)(2,1)}, u32[]{:S(2)}, u32[]{:S(2)}) collective-permute-start(bf16[2048,512]{1,0:T(8,128)(2,1)} %convert_bitcast_fusion.2), channel_id=1, source_target_pairs={{0,1},{1,0},{2,3},{3,2},{4,5},{5,4},{6,7},{7,6},{8,9},{9,8},{10,11... | collective-permute-start | bytes 6291464 | tf_op jit(solution)/shard_map/ppermute | solution.py:102
  281.5 69.8 %collective-permute-start.15 = (f32[512,2048]{1,0:T(8,128)}, f32[512,2048]{1,0:T(8,128)}, u32[]{:S(2)}, u32[]{:S(2)}) collective-permute-start(f32[512,2048]{1,0:T(8,128)} %fusion.128), channel_id=1, source_target_pairs={{0,1},{1,0},{2,3},{3,2},{4,5},{5,4},{6,7},{7,6},{8,9},{9,8},{10,11... | collective-permute-start | bytes 12582920 | tf_op jit(solution)/shard_map/ppermute | solution.py:102
  287.6 62.2 %collective-permute-start.20 = (bf16[512,2048]{1,0:T(8,128)(2,1)}, bf16[512,2048]{1,0:T(8,128)(2,1)}, u32[]{:S(2)}, u32[]{:S(2)}) collective-permute-start(bf16[512,2048]{1,0:T(8,128)(2,1)} %collective-permute-done.19.refs_0_), channel_id=1, source_target_pairs={{0,2},{1,5},{2,0},{3,7},{4,6},{5,1},{6,4},{7,3},{8,10},{9,13},{10,... | collective-permute-start | bytes 6291464 | tf_op jit(solution)/shard_map/ppermute | solution.py:98
  349.3 67.0 %collective-permute-start.25 = (bf16[512,2048]{1,0:T(8,128)(2,1)}, bf16[512,2048]{1,0:T(8,128)(2,1)}, u32[]{:S(2)}, u32[]{:S(2)}) collective-permute-start(bf16[512,2048]{1,0:T(8,128)(2,1)} %collective-permute-done.23.refs_4_), channel_id=1, source_target_pairs={{0,4},{1,3},{2,6},{3,1},{4,0},{5,7},{6,2},{7,5},{8,12},{9,11},{10,... | collective-permute-start | bytes 6291464 | tf_op jit(solution)/shard_map/ppermute | solution.py:98
  349.8 91.7 %collective-permute-start.22 = (bf16[512,2048]{1,0:T(8,128)(2,1)}, bf16[512,2048]{1,0:T(8,128)(2,1)}, u32[]{:S(2)}, u32[]{:S(2)}) collective-permute-start(bf16[512,2048]{1,0:T(8,128)(2,1)} %collective-permute-done.20.refs_1_), channel_id=1, source_target_pairs={{0,4},{1,3},{2,6},{3,1},{4,0},{5,7},{6,2},{7,5},{8,12},{9,11},{10,... | collective-permute-start | bytes 6291464 | tf_op jit(solution)/shard_map/ppermute | solution.py:98
  356.8 107.1 %collective-permute-start.26 = (bf16[512,2048]{1,0:T(8,128)(2,1)}, bf16[512,2048]{1,0:T(8,128)(2,1)}, u32[]{:S(2)}, u32[]{:S(2)}) collective-permute-start(bf16[512,2048]{1,0:T(8,128)(2,1)} %collective-permute-done.24.refs_5_), channel_id=1, source_target_pairs={{0,4},{1,3},{2,6},{3,1},{4,0},{5,7},{6,2},{7,5},{8,12},{9,11},{10,... | collective-permute-start | bytes 6291464 | tf_op jit(solution)/shard_map/ppermute | solution.py:98
  834.6 93.1 %collective-permute-start.28 = (bf16[512,2048]{1,0:T(8,128)(2,1)}, bf16[512,2048]{1,0:T(8,128)(2,1)S(1)}, u32[]{:S(2)}, u32[]{:S(2)}) collective-permute-start(bf16[512,2048]{1,0:T(8,128)(2,1)} %get-tuple-element.51), channel_id=1, source_target_pairs={{0,4},{1,3},{2,6},{3,1},{4,0},{5,7},{6,2},{7,5},{8,12},{9,11},{10,... | collective-permute-start | bytes 6291464 | tf_op jit(solution)/shard_map/ppermute | solution.py:98
  838.3 91.9 %collective-permute-start.32 = (bf16[512,2048]{1,0:T(8,128)(2,1)}, bf16[512,2048]{1,0:T(8,128)(2,1)S(1)}, u32[]{:S(2)}, u32[]{:S(2)}) collective-permute-start(bf16[512,2048]{1,0:T(8,128)(2,1)} %get-tuple-element.55), channel_id=1, source_target_pairs={{0,4},{1,3},{2,6},{3,1},{4,0},{5,7},{6,2},{7,5},{8,12},{9,11},{10,... | collective-permute-start | bytes 6291464 | tf_op jit(solution)/shard_map/ppermute | solution.py:98
  855.3 271.9 %collective-permute-start.66 = (f32[512,2048]{1,0:T(8,128)S(1)}, f32[512,2048]{1,0:T(8,128)S(1)}, u32[]{:S(2)}, u32[]{:S(2)}) collective-permute-start(f32[512,2048]{1,0:T(8,128)S(1)} %slice.138), channel_id=1, source_target_pairs={{0,1},{1,0},{2,3},{3,2},{4,5},{5,4},{6,7},{7,6},{8,9},{9,8},{10,11... | collective-permute-start | bytes 12582920 | tf_op jit(solution)/shard_map/ppermute | solution.py:102
  925.7 99.4 %collective-permute-start.31 = (bf16[512,2048]{1,0:T(8,128)(2,1)}, bf16[512,2048]{1,0:T(8,128)(2,1)}, u32[]{:S(2)}, u32[]{:S(2)}) collective-permute-start(bf16[512,2048]{1,0:T(8,128)(2,1)} %get-tuple-element.53), channel_id=1, source_target_pairs={{0,4},{1,3},{2,6},{3,1},{4,0},{5,7},{6,2},{7,5},{8,12},{9,11},{10,... | collective-permute-start | bytes 6291464 | tf_op jit(solution)/shard_map/ppermute | solution.py:98
  929.8 88.2 %collective-permute-start.29 = (bf16[512,2048]{1,0:T(8,128)(2,1)}, bf16[512,2048]{1,0:T(8,128)(2,1)S(1)}, u32[]{:S(2)}, u32[]{:S(2)}) collective-permute-start(bf16[512,2048]{1,0:T(8,128)(2,1)} %add_convert_fusion.6), channel_id=1, source_target_pairs={{0,2},{1,5},{2,0},{3,7},{4,6},{5,1},{6,4},{7,3},{8,10},{9,13},{10,... | collective-permute-start | bytes 6291464 | tf_op jit(solution)/shard_map/ppermute | solution.py:98
  932.3 92.8 %collective-permute-start.33 = (bf16[512,2048]{1,0:T(8,128)(2,1)}, bf16[512,2048]{1,0:T(8,128)(2,1)}, u32[]{:S(2)}, u32[]{:S(2)}) collective-permute-start(bf16[512,2048]{1,0:T(8,128)(2,1)} %add_convert_fusion.4), channel_id=1, source_target_pairs={{0,2},{1,5},{2,0},{3,7},{4,6},{5,1},{6,4},{7,3},{8,10},{9,13},{10,... | collective-permute-start | bytes 6291464 | tf_op jit(solution)/shard_map/ppermute | solution.py:98
  968.0 222.6 %collective-permute-start.65 = (f32[2048,512]{1,0:T(8,128)}, f32[2048,512]{1,0:T(8,128)}, u32[]{:S(2)}, u32[]{:S(2)}) collective-permute-start(f32[2048,512]{1,0:T(8,128)} %slice.136), channel_id=1, source_target_pairs={{0,1},{1,0},{2,3},{3,2},{4,5},{5,4},{6,7},{7,6},{8,9},{9,8},{10,11... | collective-permute-start | bytes 12582920 | tf_op jit(solution)/shard_map/ppermute | solution.py:102
  1066.0 138.8 %collective-permute-start.64 = (f32[2048,512]{1,0:T(8,128)}, f32[2048,512]{1,0:T(8,128)}, u32[]{:S(2)}, u32[]{:S(2)}) collective-permute-start(f32[2048,512]{1,0:T(8,128)} %slice.134), channel_id=1, source_target_pairs={{0,1},{1,0},{2,3},{3,2},{4,5},{5,4},{6,7},{7,6},{8,9},{9,8},{10,11... | collective-permute-start | bytes 12582920 | tf_op jit(solution)/shard_map/ppermute | solution.py:102
  1073.5 56.4 %collective-permute-start.35 = (bf16[512,2048]{1,0:T(8,128)(2,1)S(1)}, bf16[512,2048]{1,0:T(8,128)(2,1)S(1)}, u32[]{:S(2)}, u32[]{:S(2)}) collective-permute-start(bf16[512,2048]{1,0:T(8,128)(2,1)S(1)} %add_convert_fusion.2), channel_id=1, source_target_pairs={{0,1},{1,0},{2,3},{3,2},{4,5},{5,4},{6,7},{7,6},{8,9},{9,8},{10,11... | collective-permute-start | bytes 6291464 | tf_op jit(solution)/shard_map/ppermute | solution.py:102
  1257.2 84.7 %collective-permute-start.60 = (bf16[4,128,1024]{2,1,0:T(8,128)(2,1)S(1)}, bf16[4,128,1024]{2,1,0:T(8,128)(2,1)}, u32[]{:S(2)}, u32[]{:S(2)}) collective-permute-start(bf16[4,128,1024]{2,1,0:T(8,128)(2,1)S(1)} %fusion.44), channel_id=1, source_target_pairs={{0,2},{1,3},{2,0},{3,1},{4,6},{5,7},{6,4},{7,5},{8,10},{9,11},{10,... | collective-permute-start | bytes 3145736 | tf_op jit(solution)/shard_map/ppermute | solution.py:98
  1260.0 87.6 %collective-permute-start.54 = (bf16[4,2,128,1024]{3,2,1,0:T(8,128)(2,1)S(1)}, bf16[4,2,128,1024]{3,2,1,0:T(8,128)(2,1)}, u32[]{:S(2)}, u32[]{:S(2)}) collective-permute-start(bf16[4,2,128,1024]{3,2,1,0:T(8,128)(2,1)S(1)} %fusion.24), channel_id=1, source_target_pairs={{0,2},{1,3},{2,0},{3,1},{4,6},{5,7},{6,4},{7,5},{8,10},{9,11},{10,... | collective-permute-start | bytes 6291464 | tf_op jit(solution)/shard_map/ppermute | solution.py:98
  1266.9 60.9 %collective-permute-start.39 = (f32[4,20,128]{2,0,1:T(4,128)S(1)}, f32[4,20,128]{2,0,1:T(4,128)S(1)}, u32[]{:S(2)}, u32[]{:S(2)}) collective-permute-start(f32[4,20,128]{2,0,1:T(4,128)S(1)} %bitcast.375), channel_id=1, source_target_pairs={{0,2},{1,3},{2,0},{3,1},{4,6},{5,7},{6,4},{7,5},{8,10},{9,11},{10,... | collective-permute-start | bytes 122888 | tf_op jit(solution)/shard_map/ppermute | solution.py:98
  (144 other events, 3478.8 us)

commit v3 on v2

--- a/solution.py
+++ b/solution.py
@@ -207,6 +207,433 @@
         out_shape=[full] * 4 + [small],
         name="assemble",
     )(owner, *blocks)
+
+
+class Place:
+    def __init__(self):
+        self.me = me = lax.axis_index("expert")
+        self.core = core = lax.axis_index("tensor")
+        top, mid, low = me // 4, (me // 2) % 2, me % 2
+        flip_low = me + 1 - 2 * low
+        flip_mid = me + 2 - 4 * mid
+        self.first = flip_low + core * (flip_mid - flip_low)
+        self.second = flip_mid + core * (flip_low - flip_mid)
+        self.planes = (
+            me,
+            me + 4 - 8 * (top % 2),
+            me + 8 - 16 * (top // 2),
+            me + 12 - 8 * top,
+        )
+
+    def owner(self, plane, far, near):
+        return self.planes[plane] + far * (self.second - self.me) + near * (self.first - self.me)
+
+    def greet(self, sibling):
+        barrier = pltpu.get_barrier_semaphore()
+        partners = [(device, self.core) for device in (self.first, self.second) + self.planes[1:]]
+        if sibling:
+            partners.append((self.me, 1 - self.core))
+        for partner in partners:
+            pl.semaphore_signal(
+                barrier, inc=1, device_id=partner, device_id_type=pl.DeviceIdType.MESH
+            )
+        pl.semaphore_wait(barrier, len(partners))
+
+
+def remote(source, target, send, recv, device):
+    return pltpu.make_async_remote_copy(
+        src_ref=source,
+        dst_ref=target,
+        send_sem=send,
+        recv_sem=recv,
+        device_id=device,
+        device_id_type=pl.DeviceIdType.MESH,
+    )
+
+
+def gather_kernel(rows, *refs):
+    mine, grad, halves, refs = refs[:5], refs[5], refs[6:9], refs[9:]
+    full, grads, others, refs = refs[:5], refs[5], refs[6:9], refs[9:]
+    send_sem, recv_sem, grad_send, grad_recv, half_send, half_recv, own_sem = refs
+    place = Place()
+    core = place.core
+    place.greet(True)
+
+    def part(which, plane, far, near):
+        owner = place.owner(plane, far, near)
+        if which == 4:
+            return full[4].at[owner]
+        return full[which].at[pl.ds(pl.multiple_of(owner * rows, rows), rows)]
+
+    def pass_weights(source, plane, slot, device):
+        out = []
+        for which in range(5):
+            here = part(which, *source)
+            out.append(
+                remote(
+                    mine[which] if source == (0, 0, 0) else here,
+                    here,
+                    send_sem.at[4 * plane + slot, which],
+                    recv_sem.at[4 * plane + slot, which],
+                    (device, core),
+                )
+            )
+        return out
+
+    def start(copies):
+        for copy in copies:
+            copy.start()
+
+    def arrived(plane, slot):
+        for copy in pass_weights((plane, slot // 2, slot % 2), plane, slot, place.first):
+            copy.wait_recv()
+
+    def pass_grad(source, slot, device):
+        return remote(
+            source, grads.at[slot], grad_send.at[slot], grad_recv.at[slot], (device, core)
+        )
+
+    for plane in (1, 2, 3):
+        start(pass_weights((0, 0, 0), plane, 0, place.planes[plane]))
+    start(pass_weights((0, 0, 0), 0, 1, place.first))
+    start(pass_weights((0, 0, 0), 0, 2, place.second))
+    far_plane = place.planes[3] + core * (place.planes[2] - place.planes[3])
+
+    @pl.when(core == 1)
+    def _():
+        pass_grad(grad, 0, place.planes[1]).start()
+
+    pass_grad(grad, 4, far_plane).start()
+    swaps = [
+        remote(halves[i], others[i], half_send.at[i], half_recv.at[i], (place.me, 1 - core))
+        for i in range(3)
+    ]
+    start(swaps)
+    keeps = [
+        pltpu.make_async_copy(mine[which], part(which, 0, 0, 0), own_sem.at[which])
+        for which in range(5)
+    ]
+    start(keeps)
+
+    @pl.when(core == 0)
+    def _():
+        pltpu.make_async_copy(grad, grads.at[0], own_sem.at[5]).start()
+
+    for plane in range(4):
+        if plane > 0:
+            arrived(plane, 0)
+            start(pass_weights((plane, 0, 0), plane, 1, place.first))
+            start(pass_weights((plane, 0, 0), plane, 2, place.second))
+        arrived(plane, 1)
+        start(pass_weights((plane, 0, 1), plane, 3, place.second))
+
+    @pl.when(core == 0)
+    def _():
+        pass_grad(grad, 1, place.first).start()
+        pass_grad(grad, 2, place.second).start()
+
+    @pl.when(core == 1)
+    def _():
+        pass_grad(grads.at[0], 0, place.first).wait_recv()
+        pass_grad(grads.at[0], 1, place.first).start()
+        pass_grad(grads.at[0], 2, place.second).start()
+
+    pass_grad(grads.at[1], 1, place.first).wait_recv()
+    pass_grad(grads.at[1], 3, place.second).start()
+    pass_grad(grads.at[4], 4, place.first).wait_recv()
+    pass_grad(grads.at[4], 5, place.first).start()
+    pass_grad(grads.at[4], 6, place.second).start()
+    pass_grad(grads.at[5], 5, place.first).wait_recv()
+    pass_grad(grads.at[5], 7, place.second).start()
+
+    for plane in range(4):
+        arrived(plane, 2)
+        arrived(plane, 3)
+    for slot in (2, 3, 6, 7):
+        pass_grad(grads.at[slot], slot, place.first).wait_recv()
+    for slot in range(1, 16):
+        for copy in pass_weights((slot // 4, 0, 0), slot // 4, slot % 4, place.first):
+            copy.wait_send()
+    for slot in range(1, 8):
+        pass_grad(grads.at[slot], slot, place.first).wait_send()
+
+    @pl.when(core == 1)
+    def _():
+        pass_grad(grads.at[0], 0, place.first).wait_send()
+
+    @pl.when(core == 0)
+    def _():
+        pltpu.make_async_copy(grad, grads.at[0], own_sem.at[5]).wait()
+
+    for copy in swaps + keeps:
+        copy.wait()
+
+
+def gather_all(mine, grad, halves, count):
+    rows, width = mine[0].shape
+    extra = mine[4].shape[0]
+    low = jnp.bfloat16
+    hbm = pl.BlockSpec(memory_space=pl.ANY)
+    full = jax.ShapeDtypeStruct((count * rows, width), low)
+    return pl.pallas_call(
+        functools.partial(gather_kernel, rows),
+        in_specs=[hbm] * 9,
+        out_specs=[hbm] * 9,
+        out_shape=[full] * 4
+        + [
+            jax.ShapeDtypeStruct((count, extra, width), low),
+            jax.ShapeDtypeStruct((8,) + grad.shape, low),
+        ]
+        + [jax.ShapeDtypeStruct(half.shape, low) for half in halves],
+        scratch_shapes=[
+            pltpu.SemaphoreType.DMA((16, 5)),
+            pltpu.SemaphoreType.DMA((16, 5)),
+            pltpu.SemaphoreType.DMA((8,)),
+            pltpu.SemaphoreType.DMA((8,)),
+            pltpu.SemaphoreType.DMA((3,)),
+            pltpu.SemaphoreType.DMA((3,)),
+            pltpu.SemaphoreType.DMA((6,)),
+        ],
+        compiler_params=pltpu.CompilerParams(collective_id=1, has_side_effects=True),
+        name="gather_all",
+    )(*mine, grad, *halves)
+
+
+def reduce_kernel(rows, *refs):
+    whole, small, halves, refs = refs[:4], refs[4], refs[5:8], refs[8:]
+    out, small_out, others, refs = refs[:4], refs[4], refs[5:8], refs[8:]
+    (
+        own,
+        far_in,
+        near_in,
+        plane_in,
+        near_stage,
+        plane_stage,
+        small_own,
+        small_far,
+        small_near,
+        small_plane,
+        small_near_stage,
+        small_plane_stage,
+        small_last,
+        small_other,
+        load_sem,
+        far_send,
+        far_recv,
+        near_send,
+        near_recv,
+        plane_send,
+        plane_recv,
+        half_send,
+        half_recv,
+        last_send,
+        last_recv,
+    ) = refs
+    place = Place()
+    core = place.core
+    sibling = (place.me, 1 - core)
+    place.greet(True)
+    second, first = (place.second, core), (place.first, core)
+
+    def source(which, plane, far, near):
+        owner = place.owner(plane, far, near)
+        if which == 4:
+            return small.at[owner]
+        return whole[which].at[pl.ds(pl.multiple_of(owner * rows, rows), rows)]
+
+    def load(which, plane, near):
+        target = small_own.at[2 * plane + near] if which == 4 else own.at[2 * plane + near, which]
+        return pltpu.make_async_copy(
+            source(which, plane, 0, near), target, load_sem.at[2 * plane + near, which]
+        )
+
+    def to_second(which, plane, near):
+        target = small_far.at[2 * plane + near]
+        if which != 4:
+            target = far_in.at[2 * plane + near, which]
+        return remote(
+            source(which, plane, 1, near),
+            target,
+            far_send.at[2 * plane + near, which],
+            far_recv.at[2 * plane + near, which],
+            second,
+        )
+
+    def to_first(which, plane):
+        here, there = small_near_stage.at[plane], small_near.at[plane]
+        if which is not None:
+            here, there = near_stage.at[plane, which], near_in.at[plane, which]
+        at = 4 if which is None else which
+        return remote(here, there, near_send.at[plane, at], near_recv.at[plane, at], first)
+
+    def to_plane(which, plane):
+        here, there = small_plane_stage.at[plane - 1], small_plane.at[plane - 1]
+        if which is not None:
+            here, there = plane_stage.at[plane - 1, which], plane_in.at[plane - 1, which]
+        at = 4 if which is None else which
+        return remote(
+            here,
+            there,
+            plane_send.at[plane - 1, at],
+            plane_recv.at[plane - 1, at],
+            (place.planes[plane], core),
+        )
+
+    for plane in (3, 2, 1, 0):
+        for near in (1, 0):
+            for which in range(5):
+                to_second(which, plane, near).start()
+    for plane in (3, 2, 1, 0):
+        for near in (1, 0):
+            for which in range(5):
+                load(which, plane, near).start()
+    middle = others[0].shape[1]
+    theirs = [
+        halves[0].at[:, pl.ds(middle, middle)],
+        halves[1].at[:, pl.ds(middle, middle)],
+        halves[2].at[pl.ds(middle, middle)],
+    ]
+    swaps = [
+        remote(theirs[i], others[i], half_send.at[i], half_recv.at[i], sibling) for i in range(3)
+    ]
+    for copy in swaps:
+        copy.start()
+
+    def added(parts, target):
+        total = parts[0].astype(jnp.float32)
+        for value in parts[1:]:
+            total = total + value.astype(jnp.float32)
+        return total.astype(target.dtype)
+
+    def over_rows(parts, target):
+        def body(step, carry):
+            span = pl.ds(pl.multiple_of(step * 16, 16), 16)
+            target[span, :] = added([part[span, :] for part in parts], target)
+            return carry
+
+        lax.fori_loop(0, rows // 16, body, 0)
+
+    def near_sums(plane):
+        for which in range(4):
+            load(which, plane, 1).wait()
+            to_second(which, plane, 1).wait_recv()
+            over_rows(
+                [own.at[2 * plane + 1, which], far_in.at[2 * plane + 1, which]],
+                near_stage.at[plane, which],
+            )
+            to_first(which, plane).start()
+        load(4, plane, 1).wait()
+        to_second(4, plane, 1).wait_recv()
+        small_near_stage[plane] = small_own[2 * plane + 1] + small_far[2 * plane + 1]
+        to_first(None, plane).start()
+
+    def plane_sums(plane):
+        for which in range(4):
+            load(which, plane, 0).wait()
+            to_second(which, plane, 0).wait_recv()
+            to_first(which, plane).wait_recv()
+            over_rows(
+                [
+                    own.at[2 * plane, which],
+                    far_in.at[2 * plane, which],
+                    near_in.at[plane, which],
+                ],
+                plane_stage.at[plane - 1, which],
+            )
+            to_plane(which, plane).start()
+        load(4, plane, 0).wait()
+        to_second(4, plane, 0).wait_recv()
+        to_first(None, plane).wait_recv()
+        small_plane_stage[plane - 1] = (
+            small_own[2 * plane] + small_far[2 * plane] + small_near[plane]
+        )
+        to_plane(None, plane).start()
+
+    near_sums(3)
+    near_sums(2)
+    plane_sums(3)
+    near_sums(1)
+    plane_sums(2)
+    near_sums(0)
+    plane_sums(1)
+    load(4, 0, 0).wait()
+    to_second(4, 0, 0).wait_recv()
+    to_first(None, 0).wait_recv()
+    for plane in (1, 2, 3):
+        to_plane(None, plane).wait_recv()
+    small_last[...] = (
+        small_own[0]
+        + small_far[0]
+        + small_near[0]
+        + small_plane[0]
+        + small_plane[1]
+        + small_plane[2]
+    )
+    last = remote(small_last, small_other, last_send.at[0], last_recv.at[0], sibling)
+    last.start()
+    for which in range(4):
+        load(which, 0, 0).wait()
+        to_second(which, 0, 0).wait_recv()
+        to_first(which, 0).wait_recv()
+        for plane in (1, 2, 3):
+            to_plane(which, plane).wait_recv()
+        over_rows(
+            [own.at[0, which], far_in.at[0, which], near_in.at[0, which]]
+            + [plane_in.at[plane, which] for plane in range(3)],
+            out[which],
+        )
+    last.wait()
+    small_out[...] = small_last[...] + small_other[...]
+    for plane in range(4):
+        for which in range(5):
+            at = None if which == 4 else which
+            for near in range(2):
+                to_second(which, plane, near).wait_send()
+            to_first(at, plane).wait_send()
+            if plane > 0:
+                to_plane(at, plane).wait_send()
+    for copy in swaps:
+        copy.wait()
+
+
+def reduce_all(whole, small, halves, count):
+    rows, width = whole[0].shape[0] // count, whole[0].shape[1]
+    low = jnp.bfloat16
+    hbm = pl.BlockSpec(memory_space=pl.ANY)
+    vmem = pl.BlockSpec(memory_space=pltpu.VMEM)
+    tiny = small.shape[1:]
+
+    def wide(*dims):
+        return pltpu.VMEM(dims + (rows, width), low)
+
+    def little(*dims):
+        return pltpu.VMEM(dims + tiny, jnp.float32)
+
+    def sems(*dims):
+        return pltpu.SemaphoreType.DMA(dims)
+
+    return pl.pallas_call(
+        functools.partial(reduce_kernel, rows),
+        in_specs=[hbm] * 8,
+        out_specs=[vmem] * 5 + [hbm] * 3,
+        out_shape=[jax.ShapeDtypeStruct((rows, width), jnp.float32)] * 4
+        + [jax.ShapeDtypeStruct(tiny, jnp.float32)]
+        + [
+            jax.ShapeDtypeStruct((dims[0] // cut, dims[1] // (3 - cut)), jnp.float32)
+            for dims, cut in ((halves[0].shape, 1), (halves[1].shape, 1), (halves[2].shape, 2))
+        ],
+        scratch_shapes=[wide(8, 4), wide(8, 4), wide(4, 4), wide(3, 4), wide(4, 4), wide(3, 4)]
+        + [little(8), little(8), little(4), little(3), little(4), little(3), little(), little()]
+        + [sems(8, 5)] * 3
+        + [sems(4, 5)] * 2
+        + [sems(3, 5)] * 2
+        + [sems(3)] * 2
+        + [sems(1)] * 2,
+        compiler_params=pltpu.CompilerParams(
+            collective_id=2, has_side_effects=True, vmem_limit_bytes=60 * 1024 * 1024
+        ),
+        name="reduce_all",
+    )(*whole, small, *halves)
 
 
 def split_three(value):
@@ -289,12 +716,9 @@
     capacity,
     experts,
     own,
-    wg,
-    wu,
-    wd,
     *refs,
 ):
-    grads, refs = refs[:8], refs[8:]
+    weights, grads, refs = refs[:6], refs[6], refs[7:]
     parts, refs = refs[:8], refs[8:]
     (
     blocks,
@@ -369,9 +793,13 @@
             device_id_type=mesh,
         )
 
+    half = wg_v.shape[1] // 2
+    targets = []
+    for span in (slice(0, half), slice(half, 2 * half)):
+        targets += [wg_v.at[:, span], wu_v.at[:, span], wd_v.at[span]]
     loads = [
         pltpu.make_async_copy(source, target, weight_sem.at[index])
-        for index, (source, target) in enumerate(((wg, wg_v), (wu, wu_v), (wd, wd_v)))
+        for index, (source, target) in enumerate(zip(weights, targets))
     ]
 
     @pl.when(core == 0)
@@ -451,12 +879,7 @@
         def _():
             pass_on(blocks.at[k], k + 2, second).start()
 
-        for index in range(8):
-
-            @pl.when(k == index)
-            def _():
-                pltpu.make_async_copy(grads[index], grad_v, load_sem.at[1]).start()
-
+        pltpu.make_async_copy(grads.at[k], grad_v, load_sem.at[1]).start()
 
         @pl.when(k == 0)
         def _():
@@ -483,7 +906,7 @@
         for at in range(0, width, 512):
             span = slice(at, at + 512)
             rows_v[:, span] = dot(pick_v[...], block_v[:length, span]).astype(jnp.bfloat16)
-        pltpu.make_async_copy(grads[0], grad_v, load_sem.at[1]).wait()
+        pltpu.make_async_copy(grads.at[k], grad_v, load_sem.at[1]).wait()
         for at in range(0, width, 512):
             span = slice(at, at + 512)
             grows_v[:, span] = dot(pick_v[...], grad_v[:, span]).astype(jnp.bfloat16)
@@ -595,9 +1018,9 @@
     final.wait()
 
 
-def moe_layer(own, grads, wg, wu, wd, capacity):
+def moe_layer(own, grads, weights, capacity):
     rows, width = own.shape
-    hidden = wg.shape[1]
+    hidden = 2 * weights[0].shape[1]
     experts = rows - SEQ
     low = jnp.bfloat16
     hbm = pl.BlockSpec(memory_space=pl.ANY)
@@ -607,7 +1030,7 @@
 
     return pl.pallas_call(
         functools.partial(moe_kernel, capacity, experts),
-        in_specs=[hbm] * 12,
+        in_specs=[hbm] * 8,
         out_specs=[hbm] * 18,
         out_shape=[shape(SEQ, width)] * 8
         + [
@@ -639,7 +1062,7 @@
             pltpu.VMEM((8, rows, width), low),
             pltpu.VMEM((SEQ, width), low),
             pltpu.VMEM((2, rows, width), low),
-            pltpu.SemaphoreType.DMA((3,)),
+            pltpu.SemaphoreType.DMA((6,)),
             pltpu.SemaphoreType.DMA((4,)),
             pltpu.SemaphoreType.DMA((6,)),
             pltpu.SemaphoreType.DMA((8,)),
@@ -651,7 +1074,7 @@
             collective_id=0, has_side_effects=True, vmem_limit_bytes=67043328
         ),
         name="moe_layer",
-    )(own, wg, wu, wd, *grads)
+    )(own, *weights, grads)
 
 
 def local(
@@ -700,15 +1123,21 @@
         axis=1,
     )
     small = jnp.pad(small, ((0, 0), (0, width - 2 * own_rows)))
-    mine = jnp.concatenate(
-        [w_query.astype(low), w_key.astype(low), w_value.astype(low), w_out.astype(low), small],
-        axis=0,
-    )
-    arrived = []
-    for top in range(PLANES):
-        base = mine if top == 0 else grid.send(mine, (top * grid.plane,) * CORES)
-        arrived += spread(grid, base)
-    wq_full, wk_full, wv_full, wo_full, smalls = assemble(grid, arrived, own_rows, experts)
+    mine = [w_query.astype(low), w_key.astype(low), w_value.astype(low), w_out.astype(low), small]
+    halves = [w_gate[0].astype(low), w_up[0].astype(low), w_down[0].astype(low)]
+    allowed = jnp.arange(SEQ) < lengths[0]
+    grad_two_low = jnp.where(allowed[:, None], cotangent, 0)
+    if grid.side == 2:
+        wq_full, wk_full, wv_full, wo_full, smalls, grad_blocks, *others = gather_all(
+            mine, grad_two_low, halves, count
+        )
+    else:
+        whole = jnp.concatenate(mine, axis=0)
+        arrived = []
+        for top in range(PLANES):
+            base = whole if top == 0 else grid.send(whole, (top * grid.plane,) * CORES)
+            arrived += spread(grid, base)
+        wq_full, wk_full, wv_full, wo_full, smalls = assemble(grid, arrived, own_rows, experts)
     router_t = smalls[:, :, :own_rows].transpose(1, 0, 2).reshape(experts, D)
     gain_one = smalls[:, 0, own_rows : 2 * own_rows].reshape(D).astype(jnp.float32)
     gain_two = smalls[:, 1, own_rows : 2 * own_rows].reshape(D).astype(jnp.float32)
@@ -716,17 +1145,6 @@
     gain_query = smalls[:, 2, head_cols].reshape(HD).astype(jnp.float32)
     gain_key = smalls[:, 3, head_cols].reshape(HD).astype(jnp.float32)
 
-    wg_own, wu_own, wd_own = (w_gate[0].astype(low), w_up[0].astype(low), w_down[0].astype(low))
-    wg = jnp.concatenate([wg_own, swap(wg_own)], axis=1)
-    wu = jnp.concatenate([wu_own, swap(wu_own)], axis=1)
-    wd = jnp.concatenate([wd_own, swap(wd_own)], axis=0)
-
-    allowed = jnp.arange(SEQ) < lengths[0]
-    grad_two_low = jnp.where(allowed[:, None], cotangent, 0)
-    grad_two_sent, wq_full, wk_full, wv_full, wo_full = lax.optimization_barrier(
-        (grad_two_low, wq_full, wk_full, wv_full, wo_full)
-    )
-    grad_turns = gather_tokens(grid, grad_two_sent)
     grad_two = grad_two_low.astype(jnp.float32)
 
     cosine, sine_tab = rope_tables(SEQ, HD)
@@ -780,11 +1198,15 @@
     gate_rows = jnp.pad(split_three(gates_wide.T), ((0, 0), (0, D - 3 * SEQ)))
     token_block = jnp.concatenate([ffn_in, gate_rows], axis=0)
     if grid.side == 2:
-        done = moe_layer(token_block, grad_turns[0] + grad_turns[1], wg, wu, wd, capacity)
+        done = moe_layer(token_block, grad_blocks, halves + others, capacity)
         saved = [tuple(done[12:17])]
         out_turns = [done[:4], done[4:8]]
         back_sum = both_cores(done[17])
     else:
+        wg, wu, wd = (
+            jnp.concatenate([half, swap(half)], axis=axis) for half, axis in zip(halves, (1, 1, 0))
+        )
+        grad_turns = gather_tokens(grid, grad_two_low)
         token_turns = gather_tokens(grid, token_block)
         out_turns, back_turns, saved = [], [], []
         for turn in range(2):
@@ -805,9 +1227,6 @@
     gate_w = over_turns(0, 3)
     up_w = over_turns(0, 4)
     down_w = over_turns(2, 1)
-    grad_gate_w = (gate_w[:, :half] + swap(gate_w[:, half:]))[None]
-    grad_up_w = (up_w[:, :half] + swap(up_w[:, half:]))[None]
-    grad_down_w = (down_w[:half] + swap(down_w[half:]))[None]
 
     grad_gates_wide = join_three(back_sum[SEQ:], SEQ).T
     grad_gate_sel = jnp.sum(jnp.where(route_hot, grad_gates_wide[:, None, :], 0.0), axis=2)
@@ -821,13 +1240,7 @@
     grad_one = grad_two + norm_back(grad_ffn_in * gain_two, normed_two, inverse_two)
     grad_attn = grad_one.astype(low)
 
-    def reduce_weight(left, right, axes):
-        whole = contract_rows(left, right)
-        return scatter_rows(
-            grid, whole.reshape(PLANES, grid.side, grid.side, own_rows, width), axes, low
-        )
-
-    grad_wo = reduce_weight(grad_attn, mixed, (1, 2, 0))
+    part_wo = contract_rows(grad_attn, mixed)
     grad_mixed = (
         jnp.dot(grad_attn, wo_full, preferred_element_type=jnp.float32)
         .astype(low)
@@ -843,7 +1256,7 @@
         "hqk,qhd->khd", probs_again, grad_mixed, preferred_element_type=jnp.float32
     )
     grad_value_lin = grad_values.astype(low).reshape(SEQ, heads_here * HD)
-    grad_wv = reduce_weight(attn_in, grad_value_lin, (2, 1, 0))
+    part_wv = contract_rows(attn_in, grad_value_lin)
     grad_scores = (
         attn_probs * (grad_probs - jnp.sum(attn_probs * grad_probs, axis=-1, keepdims=True))
     ).astype(low)
@@ -868,8 +1281,8 @@
         .astype(low)
         .reshape(SEQ, heads_here * HD)
     )
-    grad_wq = reduce_weight(attn_in, grad_query_lin, (1, 2, 0))
-    grad_wk = reduce_weight(attn_in, grad_key_lin, (2, 1, 0))
+    part_wq = contract_rows(attn_in, grad_query_lin)
+    part_wk = contract_rows(attn_in, grad_key_lin)
     grad_attn_part = (
         contract_cols(grad_query_lin, wq_full)
         + contract_cols(grad_key_lin, wk_full)
@@ -891,13 +1304,27 @@
         ],
         axis=0,
     ).transpose(1, 0, 2)
-    sums = scatter_rows(
-        grid,
-        parts.reshape(PLANES, grid.side, grid.side, experts + 4, own_rows),
-        (1, 2, 0),
-        jnp.float32,
-    )
-    sums = sums + swap(sums)
+    weight_parts = [part_wq, part_wk, part_wv, part_wo]
+    if grid.side == 2:
+        weight_parts = [part.astype(low) for part in weight_parts]
+        parts = jnp.pad(parts, ((0, 0), (0, 4), (0, 0)))
+        grad_wq, grad_wk, grad_wv, grad_wo, sums, *received = reduce_all(
+            weight_parts, parts, [gate_w, up_w, down_w], count
+        )
+    else:
+        shape = (PLANES, grid.side, grid.side)
+        grad_wq, grad_wk, grad_wv, grad_wo = [
+            scatter_rows(grid, part.reshape(shape + (own_rows, width)), axes, low)
+            for part, axes in zip(weight_parts, ((1, 2, 0), (2, 1, 0)) * 2)
+        ]
+        sums = scatter_rows(
+            grid, parts.reshape(shape + (experts + 4, own_rows)), (1, 2, 0), jnp.float32
+        )
+        sums = sums + swap(sums)
+        received = [swap(part) for part in (gate_w[:, half:], up_w[:, half:], down_w[half:])]
+    grad_gate_w = (gate_w[:, :half] + received[0])[None]
+    grad_up_w = (up_w[:, :half] + received[1])[None]
+    grad_down_w = (down_w[:half] + received[2])[None]
     return (
         output,
         grad_input.astype(low),

time: 1480 us -> 1260 us (0.85)
  waiting for transfers between devices: 511 us -> 75.5 us
  Pallas kernels: 384 us -> 815 us
  starting transfers between devices: 273 us -> 132 us
  other arithmetic: 132 us -> 84.6 us
  local copies, waits for them, and re-layouts: 53.8 us -> 30.9 us
    pallas_call x1 -> x2, Pallas kernels: 13.3 us -> 471 us  [the longest x1 297 us: gather_all(): pl.pallas_call(functools.partial(gather_kernel, rows), in_specs=[hbm] * 9...]
    ppermute x56 -> x8, waiting for transfers between devices: 511 us -> 68.7 us  [send(): return lax.ppermute(value, ('expert', 'tensor'), pairs)]
    ppermute x56 -> x8, starting transfers between devices: 98.5 us -> 9.72 us  [send(): return lax.ppermute(value, ('expert', 'tensor'), pairs)]
    ppermute x11 -> x4, starting transfers between devices: 174 us -> 122 us  [swap(): return lax.ppermute(value, 'tensor', [(0, 1), (1, 0)])]
    pallas_call x1, Pallas kernels: 371 us -> 345 us  [moe_layer(): pl.pallas_call(functools.partial(moe_kernel, capacity, experts), in_specs...]
    add x16 -> x1, other arithmetic: 19.6 us -> 3.09 us  [local(): grad_two + norm_back(grad_ffn_in * gain_two, normed_two, inverse_two)]
  transfers between devices with their start and end apart: 67 -> 12, of which waited for: 26 -> 3; matrix products, arithmetic and copies ran while one was open for 18% -> 7% of each run, Pallas kernels for 1% -> 0%
where the time goes in v3:
time: 1260 us; the launch traced here: 1250 us
  Pallas kernels  815 us (65%)
  starting transfers between devices  132 us (10%)
  matrix products  111 us (9%)
  other arithmetic  84.6 us (7%)
  waiting for transfers between devices  75.5 us (6%)
  local copies, waits for them, and re-layouts  30.9 us (2%)
    pallas_call x1, Pallas kernels, moe_layer(): pl.pallas_call(functools.partial(moe_kernel, capacity, experts), in_specs...  345 us
    pallas_call x1, Pallas kernels, gather_all(): pl.pallas_call(functools.partial(gather_kernel, rows), in_specs=[hbm] * 9...  297 us
    pallas_call x1, Pallas kernels, reduce_all(): pl.pallas_call(functools.partial(reduce_kernel, rows), in_specs=[hbm] * 8...  174 us
    ppermute x4, starting transfers between devices, swap(): return lax.ppermute(value, 'tensor', [(0, 1), (1, 0)])  122 us
    ppermute x8, waiting for transfers between devices, send(): return lax.ppermute(value, ('expert', 'tensor'), pairs)  68.7 us
    dot_general x8, matrix products, contract_rows(): lax.dot_general(left_mat, right_mat, (((0,), (0,)), ((), ())), preferred_...  64.2 us
  transfers between devices with their start and end apart: 12, of which 3 were waited for; matrix products, arithmetic and copies ran while one was open for 7% of the time, Pallas kernels for 0%

profile of v3, /device:TPU:0, one launch (start us, length us, event | category | flops | bytes accessed | tf_op | source)
XLA Modules:
  0.0 1252.7 jit_solution(10018591857881655971)
XLA Ops:
  17.3 297.0 %gather_all.1 = (bf16[2048,1024]{1,0:T(8,128)(2,1)}, bf16[2048,1024]{1,0:T(8,128)(2,1)}, bf16[2048,1024]{1,0:T(8,128)(2,1)}, bf16[2048,1024]{1,0:T(8,128)(2,1)},...) custom-call(bf16[128,1024]{1,0:T(8,128)(2,1)} %convert_element_type., ...), custom_call_target="tpu_custom_call" | custom-call | tf_op jit(solution)/shard_map/gather_all/pallas_call | solution.py:378
  316.6 4.6 fusion.81
  323.8 4.6 fusion.83
  331.0 4.7 fusion.36
  352.3 6.8 collective-permute-done
  365.3 344.6 %moe_layer.1 = (bf16[512,2048]{1,0:T(8,128)(2,1)}, bf16[512,2048]{1,0:T(8,128)(2,1)}, bf16[512,2048]{1,0:T(8,128)(2,1)}, bf16[512,2048]{1,0:T(8,128)(2,1)}, bf16...) custom-call(bf16[528,2048]{1,0:T(8,128)(2,1)} %pad_maximum_fusion.ow, ...), custom_call_target="tpu_custom_call" | custom-call | tf_op jit(solution)/shard_map/moe_layer/pallas_call | solution.py:1031
  719.7 69.7 %collective-permute-start.10 = (bf16[528,2048]{1,0:T(8,128)(2,1)}, bf16[528,2048]{1,0:T(8,128)(2,1)S(1)}, u32[]{:S(2)}, u32[]{:S(2)}) collective-permute-start(bf16[528,2048]{1,0:T(8,128)(2,1)} %get-tuple-element.62), channel_id=1, source_target_pairs={{0,1},{1,0},{2,3},{3,2},{4,5},{5,4},{6,7},{7,6},{8,9},{9,8},{10,11... | collective-permute-start | bytes 6488072 | tf_op jit(solution)/shard_map/ppermute | solution.py:102
  797.1 16.1 %fusion.92.refs_7_ = f32[1024,2048]{1,0:T(8,128)} fusion(bf16[2304,1024]{1,0:T(8,128)(2,1)} %get-tuple-element.66, bf16[2304,2048]{1,0:T(8,128)(2,1)} %get-tuple-element.67), kind=kOutput, calls=%fused_computation.200 | convolution fusion | flops 9663676416 | bytes 22544384 | tf_op jit(solution)/shard_map/dot_general | solution.py:61
  813.2 27.8 %collective-permute-done.3 = bf16[512,2048]{1,0:T(8,128)(2,1)S(1)} collective-permute-done((bf16[512,2048]{1,0:T(8,128)(2,1)S(1)}, bf16[512,2048]{1,0:T(8,128)(2,1)S(1)}, u32[]{:S(2)}, u32[]{:S(2)}) %collective-permute-start.3) | collective-permute-done | bytes 2097184 | tf_op jit(solution)/shard_map/ppermute | solution.py:98
  845.0 40.9 %collective-permute-done.7 = bf16[512,2048]{1,0:T(8,128)(2,1)S(1)} collective-permute-done((bf16[512,2048]{1,0:T(8,128)(2,1)S(1)}, bf16[512,2048]{1,0:T(8,128)(2,1)S(1)}, u32[]{:S(2)}, u32[]{:S(2)}) %collective-permute-start.7) | collective-permute-done | bytes 2097184 | tf_op jit(solution)/shard_map/ppermute | solution.py:98
  888.2 14.8 %fusion.91.refs_6_ = f32[2048,1024]{1,0:T(8,128)} fusion(bf16[2304,2048]{1,0:T(8,128)(2,1)S(1)} %bitcast.247, bf16[2304,1024]{1,0:T(8,128)(2,1)} %get-tuple-element.65), kind=kOutput, calls=%fused_computation.199 | convolution fusion | flops 9663676416 | bytes 22544384 | tf_op jit(solution)/shard_map/dot_general | solution.py:61
  903.0 14.7 %fusion.90.refs_5_ = f32[2048,1024]{1,0:T(8,128)} fusion(bf16[2304,2048]{1,0:T(8,128)(2,1)S(1)} %bitcast.247, bf16[2304,1024]{1,0:T(8,128)(2,1)} %get-tuple-element.64), kind=kOutput, calls=%fused_computation.198 | convolution fusion | flops 9663676416 | bytes 22544384 | tf_op jit(solution)/shard_map/dot_general | solution.py:61
  918.7 50.3 %collective-permute-start.9 = (bf16[512,2048]{1,0:T(8,128)(2,1)S(1)}, bf16[512,2048]{1,0:T(8,128)(2,1)S(1)}, u32[]{:S(2)}, u32[]{:S(2)}) collective-permute-start(bf16[512,2048]{1,0:T(8,128)(2,1)S(1)} %add_convert_fusion.2), channel_id=1, source_target_pairs={{0,1},{1,0},{2,3},{3,2},{4,5},{5,4},{6,7},{7,6},{8,9},{9,8},{10,11... | collective-permute-start | bytes 6291464 | tf_op jit(solution)/shard_map/ppermute | solution.py:102
  981.5 4.9 multiply_reduce_fusion
  1003.1 4.2 fusion.28
  1009.1 4.5 fusion.45
  1019.4 5.0 fusion.89
  1030.7 4.6 convolution_convert_fusion.1.refs_2_
  1035.3 4.8 convolution_convert_fusion.2.refs_1_
  1040.1 4.5 convolution_convert_fusion.3.refs_0_
  1044.6 4.4 convolution_convert_fusion.refs_3_
  1051.3 173.7 %reduce_all.1 = (f32[128,1024]{1,0:T(8,128)}, f32[128,1024]{1,0:T(8,128)}, f32[128,1024]{1,0:T(8,128)}, f32[128,1024]{1,0:T(8,128)}, f32[24,128]{1,0:T(8,128)}, ...) custom-call(bf16[2048,1024]{1,0:T(8,128)(2,1)} %convolution_convert_fusion.3.refs_0_, ...), custom_call_target="tpu_custom_call" | custom-call | tf_op jit(solution)/shard_map/reduce_all/pallas_call | solution.py:615
  1228.8 6.7 fusion.16
  1235.5 5.4 fusion.17
  (332 shorter events, 130.3 us)
Async XLA Ops:
  3.4 337.7 %copy-start.83 = (pred[512]{0:T(512)(128)(4,1)}, pred[512]{0:T(512)(128)(4,1)S(1)}, u32[]{:S(2)}) copy-start(pred[512]{0:T(512)(128)(4,1)S(1)} %iota_compare_fusion.4) | copy-start | bytes 1540
  17.3 298.8 %copy-start.5 = (bf16[512,2048]{1,0:T(8,128)(2,1)S(1)}, bf16[512,2048]{1,0:T(8,128)(2,1)}, u32[]{:S(2)}) copy-start(bf16[512,2048]{1,0:T(8,128)(2,1)} %param.16) | copy-start | bytes 6291460
  351.6 7.5 collective-permute-start
  709.9 83.6 %copy-start.41 = (bf16[512,2048]{1,0:T(8,128)(2,1)S(1)}, bf16[512,2048]{1,0:T(8,128)(2,1)}, u32[]{:S(2)}) copy-start(bf16[512,2048]{1,0:T(8,128)(2,1)} %get-tuple-element.60) | copy-start | bytes 6291460
  709.9 79.6 %collective-permute-start.2 = (bf16[512,2048]{1,0:T(8,128)(2,1)}, bf16[512,2048]{1,0:T(8,128)(2,1)}, u32[]{:S(2)}, u32[]{:S(2)}) collective-permute-start(bf16[512,2048]{1,0:T(8,128)(2,1)} %get-tuple-element.57), channel_id=1, source_target_pairs={{0,4},{1,3},{2,6},{3,1},{4,0},{5,7},{6,2},{7,5},{8,12},{9,11},{10,... | collective-permute-start | bytes 6291464 | tf_op jit(solution)/shard_map/ppermute | solution.py:98
  711.1 82.4 %collective-permute-start.6 = (bf16[512,2048]{1,0:T(8,128)(2,1)}, bf16[512,2048]{1,0:T(8,128)(2,1)}, u32[]{:S(2)}, u32[]{:S(2)}) collective-permute-start(bf16[512,2048]{1,0:T(8,128)(2,1)} %get-tuple-element.61), channel_id=1, source_target_pairs={{0,4},{1,3},{2,6},{3,1},{4,0},{5,7},{6,2},{7,5},{8,12},{9,11},{10,... | collective-permute-start | bytes 6291464 | tf_op jit(solution)/shard_map/ppermute | solution.py:98
  717.6 95.6 %collective-permute-start.1 = (bf16[512,2048]{1,0:T(8,128)(2,1)}, bf16[512,2048]{1,0:T(8,128)(2,1)S(1)}, u32[]{:S(2)}, u32[]{:S(2)}) collective-permute-start(bf16[512,2048]{1,0:T(8,128)(2,1)} %get-tuple-element.55), channel_id=1, source_target_pairs={{0,4},{1,3},{2,6},{3,1},{4,0},{5,7},{6,2},{7,5},{8,12},{9,11},{10,... | collective-permute-start | bytes 6291464 | tf_op jit(solution)/shard_map/ppermute | solution.py:98
  718.8 126.2 %collective-permute-start.5 = (bf16[512,2048]{1,0:T(8,128)(2,1)}, bf16[512,2048]{1,0:T(8,128)(2,1)S(1)}, u32[]{:S(2)}, u32[]{:S(2)}) collective-permute-start(bf16[512,2048]{1,0:T(8,128)(2,1)} %get-tuple-element.59), channel_id=1, source_target_pairs={{0,4},{1,3},{2,6},{3,1},{4,0},{5,7},{6,2},{7,5},{8,12},{9,11},{10,... | collective-permute-start | bytes 6291464 | tf_op jit(solution)/shard_map/ppermute | solution.py:98
  719.7 249.3 %collective-permute-start.10 = (bf16[528,2048]{1,0:T(8,128)(2,1)}, bf16[528,2048]{1,0:T(8,128)(2,1)S(1)}, u32[]{:S(2)}, u32[]{:S(2)}) collective-permute-start(bf16[528,2048]{1,0:T(8,128)(2,1)} %get-tuple-element.62), channel_id=1, source_target_pairs={{0,1},{1,0},{2,3},{3,2},{4,5},{5,4},{6,7},{7,6},{8,9},{9,8},{10,11... | collective-permute-start | bytes 6488072 | tf_op jit(solution)/shard_map/ppermute | solution.py:102
  792.4 48.6 %collective-permute-start.3 = (bf16[512,2048]{1,0:T(8,128)(2,1)S(1)}, bf16[512,2048]{1,0:T(8,128)(2,1)S(1)}, u32[]{:S(2)}, u32[]{:S(2)}) collective-permute-start(bf16[512,2048]{1,0:T(8,128)(2,1)S(1)} %add_convert_fusion.6), channel_id=1, source_target_pairs={{0,2},{1,5},{2,0},{3,7},{4,6},{5,1},{6,4},{7,3},{8,10},{9,13},{10,... | collective-permute-start | bytes 6291464 | tf_op jit(solution)/shard_map/ppermute | solution.py:98
  793.5 94.7 %slice-start.4 = ((s8[9437184]{0:T(1024)(128)(4,1)}), s8[4194304]{0:T(1024)(128)(4,1)S(1)}, s32[]{:S(2)}) async-start(s8[9437184]{0:T(1024)(128)(4,1)} %bitcast.246), calls=%async_computation.4 | async-start | bytes 8388608
  796.0 89.9 %collective-permute-start.7 = (bf16[512,2048]{1,0:T(8,128)(2,1)S(1)}, bf16[512,2048]{1,0:T(8,128)(2,1)S(1)}, u32[]{:S(2)}, u32[]{:S(2)}) collective-permute-start(bf16[512,2048]{1,0:T(8,128)(2,1)S(1)} %add_convert_fusion.4), channel_id=1, source_target_pairs={{0,2},{1,5},{2,0},{3,7},{4,6},{5,1},{6,4},{7,3},{8,10},{9,13},{10,... | collective-permute-start | bytes 6291464 | tf_op jit(solution)/shard_map/ppermute | solution.py:98
  797.1 91.1 %slice-start.5 = ((s8[9437184]{0:T(1024)(128)(4,1)}), s8[4194304]{0:T(1024)(128)(4,1)S(1)}, s32[]{:S(2)}) async-start(s8[9437184]{0:T(1024)(128)(4,1)} %bitcast.246), calls=%async_computation.5 | async-start | bytes 8388608
  797.1 91.1 %slice-start.6 = ((s8[9437184]{0:T(1024)(128)(4,1)}), s8[1048576]{0:T(1024)(128)(4,1)S(1)}, s32[]{:S(2)}) async-start(s8[9437184]{0:T(1024)(128)(4,1)} %bitcast.246), calls=%async_computation.6 | async-start | bytes 2097152
  842.4 75.2 %collective-permute-start.4 = (bf16[512,2048]{1,0:T(8,128)(2,1)S(1)}, bf16[512,2048]{1,0:T(8,128)(2,1)S(1)}, u32[]{:S(2)}, u32[]{:S(2)}) collective-permute-start(bf16[512,2048]{1,0:T(8,128)(2,1)S(1)} %add_convert_fusion.5), channel_id=1, source_target_pairs={{0,24},{1,17},{2,26},{3,19},{4,28},{5,21},{6,30},{7,23},{8,16},{9,... | collective-permute-start | bytes 6291464 | tf_op jit(solution)/shard_map/ppermute | solution.py:98
  887.4 30.3 %collective-permute-start.8 = (bf16[512,2048]{1,0:T(8,128)(2,1)S(1)}, bf16[512,2048]{1,0:T(8,128)(2,1)S(1)}, u32[]{:S(2)}, u32[]{:S(2)}) collective-permute-start(bf16[512,2048]{1,0:T(8,128)(2,1)S(1)} %add_convert_fusion.3), channel_id=1, source_target_pairs={{0,0},{1,9},{2,2},{3,11},{4,4},{5,13},{6,6},{7,15},{8,8},{9,1},{10... | collective-permute-start | bytes 6291464 | tf_op jit(solution)/shard_map/ppermute | solution.py:98
  917.6 51.3 %copy-start.40 = (bf16[528,2048]{1,0:T(8,128)(2,1)S(1)}, bf16[528,2048]{1,0:T(8,128)(2,1)}, u32[]{:S(2)}) copy-start(bf16[528,2048]{1,0:T(8,128)(2,1)} %get-tuple-element.62) | copy-start | bytes 6488068
  918.6 51.2 %copy-start.50 = (f32[512,8]{0,1:T(8,128)S(1)}, f32[512,8]{0,1:T(8,128)}, u32[]{:S(2)}) copy-start(f32[512,8]{0,1:T(8,128)} %copy-done.49) | copy-start | bytes 49156
  918.6 51.3 %copy-start.4 = (bf16[512,2048]{1,0:T(8,128)(2,1)S(1)}, bf16[512,2048]{1,0:T(8,128)(2,1)}, u32[]{:S(2)}) copy-start(bf16[512,2048]{1,0:T(8,128)(2,1)} %copy-done.3) | copy-start | bytes 6291460
  918.7 51.7 %copy-start.2 = (f32[512,2048]{1,0:T(8,128)S(1)}, f32[512,2048]{1,0:T(8,128)}, u32[]{:S(2)}) copy-start(f32[512,2048]{1,0:T(8,128)} %copy-done.1) | copy-start | bytes 12582916
  918.7 51.7 %copy-start.65 = (f32[16,1,128]{2,1,0:T(1,128)S(1)}, f32[16,1,128]{2,1,0:T(1,128)}, u32[]{:S(2)}) copy-start(f32[16,1,128]{2,1,0:T(1,128)} %copy-done.64) | copy-start | bytes 24580
  918.7 51.7 %copy-start.72 = (f32[512]{0:T(512)S(1)}, f32[512]{0:T(512)}, u32[]{:S(2)}) copy-start(f32[512]{0:T(512)} %copy-done.71) | copy-start | bytes 6148
  918.7 54.8 %collective-permute-start.9 = (bf16[512,2048]{1,0:T(8,128)(2,1)S(1)}, bf16[512,2048]{1,0:T(8,128)(2,1)S(1)}, u32[]{:S(2)}, u32[]{:S(2)}) collective-permute-start(bf16[512,2048]{1,0:T(8,128)(2,1)S(1)} %add_convert_fusion.2), channel_id=1, source_target_pairs={{0,1},{1,0},{2,3},{3,2},{4,5},{5,4},{6,7},{7,6},{8,9},{9,8},{10,11... | collective-permute-start | bytes 6291464 | tf_op jit(solution)/shard_map/ppermute | solution.py:102
  1029.3 19.7 %collective-permute-start.11 = (bf16[512,2048]{1,0:T(8,128)(2,1)S(1)}, bf16[512,2048]{1,0:T(8,128)(2,1)S(1)}, u32[]{:S(2)}, u32[]{:S(2)}) collective-permute-start(bf16[512,2048]{1,0:T(8,128)(2,1)S(1)} %add_convert_fusion), channel_id=1, source_target_pairs={{0,1},{1,0},{2,3},{3,2},{4,5},{5,4},{6,7},{7,6},{8,9},{9,8},{10,11... | collective-permute-start | bytes 6291464 | tf_op jit(solution)/shard_map/ppermute | solution.py:102
  (88 other events, 660.9 us)

commit v4 on v3

--- a/solution.py
+++ b/solution.py
@@ -754,6 +754,8 @@
     recv_sem,
     back_send,
     back_recv,
+    piece_send,
+    piece_recv,
     ) = refs
     me = lax.axis_index("expert")
     core = lax.axis_index("tensor")
@@ -832,21 +834,49 @@
     def dot_t(left, right):
         return lax.dot_general(left, right, both, preferred_element_type=jnp.float32)
 
-    def add_block(slot, sources):
-        for index, source in enumerate(sources):
-            pltpu.make_async_copy(source, taken.at[index], load_sem.at[2 + index]).start()
-        for index, source in enumerate(sources):
-            pltpu.make_async_copy(source, taken.at[index], load_sem.at[2 + index]).wait()
+    def add_block(slot, sources, start=0, size=length + experts):
+        part = pl.ds(start, size)
+        copies = [
+            pltpu.make_async_copy(source.at[part], taken.at[index, part], load_sem.at[2 + index])
+            for index, source in enumerate(sources)
+        ]
+        for copy in copies:
+            copy.start()
+        for copy in copies:
+            copy.wait()
 
         def rows_of(step, carry):
-            span = pl.ds(pl.multiple_of(step * 16, 16), 16)
+            span = pl.ds(pl.multiple_of(start + step * 16, 16), 16)
             total = stage[slot, span, :].astype(jnp.float32)
             for index in range(len(sources)):
                 total = total + taken[index, span, :].astype(jnp.float32)
             stage[slot, span, :] = total.astype(jnp.bfloat16)
             return carry
 
-        lax.fori_loop(0, (length + experts) // 16, rows_of, 0)
+        lax.fori_loop(0, size // 16, rows_of, 0)
+
+    pieces = 3
+    size = (length + experts) // pieces
+
+    def give_piece(source, target, kind, piece, device):
+        part = pl.ds(piece * size, size)
+        return pltpu.make_async_remote_copy(
+            src_ref=source.at[part],
+            dst_ref=target.at[part],
+            send_sem=piece_send.at[kind, piece],
+            recv_sem=piece_recv.at[kind, piece],
+            device_id=(device, core),
+            device_id_type=mesh,
+        )
+
+    def far_piece(which, piece):
+        return give_piece(stage.at[6 + which], far_sums.at[2 + which], which, piece, second)
+
+    def near_piece(piece):
+        return give_piece(stage.at[5], near_sums.at[1], 2, piece, first)
+
+    def plane_piece(piece):
+        return give_piece(stage.at[4], plane_sums.at[1], 3, piece, far_plane)
 
     def first_sum(turn):
         give(far_sums.at[2 * turn + 1], far_sums.at[2 * turn + 1], 2 * turn + 1, second).wait_recv()
@@ -968,10 +998,17 @@
             def _():
                 pltpu.make_async_copy(part_v, parts[index], save_sem.at[5]).start()
 
-        @pl.when(turn_at >= 2)
+        @pl.when(jnp.logical_and(turn_at >= 2, k < 4))
         def _():
-            index = 2 * (k // 4) + turn_at - 2
+            index = turn_at - 2
             give(stage.at[k], far_sums.at[index], index, second).start()
+
+        for which in range(2):
+
+            @pl.when(k == 6 + which)
+            def _():
+                for piece in range(pieces):
+                    far_piece(which, piece).start()
 
         @pl.when(k == 5)
         def _():
@@ -990,10 +1027,15 @@
         return carry
 
     lax.fori_loop(0, 8, block_step, 0)
-    first_sum(1)
-    plane_sum(1)
-    give(stage.at[4], plane_sums.at[1], 7, far_plane).start()
-    give(stage.at[4], plane_sums.at[1], 7, far_plane).wait_recv()
+    for piece in range(pieces):
+        far_piece(1, piece).wait_recv()
+        add_block(5, [far_sums.at[3]], piece * size, size)
+        near_piece(piece).start()
+    for piece in range(pieces):
+        far_piece(0, piece).wait_recv()
+        near_piece(piece).wait_recv()
+        add_block(4, [far_sums.at[2], near_sums.at[1]], piece * size, size)
+        plane_piece(piece).start()
 
     @pl.when(core == 1)
     def _():
@@ -1001,7 +1043,9 @@
         pltpu.make_async_copy(plane_sums.at[0], stage.at[0], load_sem.at[0]).start()
         pltpu.make_async_copy(plane_sums.at[0], stage.at[0], load_sem.at[0]).wait()
 
-    add_block(0, [plane_sums.at[1]])
+    for piece in range(pieces):
+        plane_piece(piece).wait_recv()
+        add_block(0, [plane_sums.at[1]], piece * size, size)
     final = pltpu.make_async_copy(stage.at[0], result, load_sem.at[0])
     final.start()
     pltpu.make_async_copy(part_v, parts[7], save_sem.at[5]).wait()
@@ -1012,9 +1056,13 @@
     def _():
         pass_on(blocks.at[0], 0, first).wait_send()
 
-    for index in range(8):
-        if index != 6:
-            give(result, result, index, first).wait_send()
+    for index in (0, 1, 4):
+        give(result, result, index, first).wait_send()
+    for piece in range(pieces):
+        for which in range(2):
+            far_piece(which, piece).wait_send()
+        near_piece(piece).wait_send()
+        plane_piece(piece).wait_send()
     final.wait()
 
 
@@ -1069,6 +1117,8 @@
             pltpu.SemaphoreType.DMA((8,)),
             pltpu.SemaphoreType.DMA((8,)),
             pltpu.SemaphoreType.DMA((8,)),
+            pltpu.SemaphoreType.DMA((4, 3)),
+            pltpu.SemaphoreType.DMA((4, 3)),
         ],
         compiler_params=pltpu.CompilerParams(
             collective_id=0, has_side_effects=True, vmem_limit_bytes=67043328
@@ -1200,7 +1250,7 @@
     if grid.side == 2:
         done = moe_layer(token_block, grad_blocks, halves + others, capacity)
         saved = [tuple(done[12:17])]
-        out_turns = [done[:4], done[4:8]]
+        far = [grid.send(done[at], grid.second(1)) for at in (6, 7, 2, 3)]
         back_sum = both_cores(done[17])
     else:
         wg, wu, wd = (
@@ -1217,8 +1267,6 @@
             back_turns.append(backs)
             saved.append(kept)
         back_sum = scatter_tokens(grid, back_turns)
-    out_sum = scatter_tokens(grid, out_turns)
-    output = (resid_one + out_sum).astype(low)
 
     def over_turns(left, right):
         return sum(contract_rows(kept[left], kept[right]) for kept in saved)
@@ -1227,6 +1275,8 @@
     gate_w = over_turns(0, 3)
     up_w = over_turns(0, 4)
     down_w = over_turns(2, 1)
+    if grid.side == 2:
+        back_sum, gate_w, up_w, down_w = lax.optimization_barrier((back_sum, gate_w, up_w, down_w))
 
     grad_gates_wide = join_three(back_sum[SEQ:], SEQ).T
     grad_gate_sel = jnp.sum(jnp.where(route_hot, grad_gates_wide[:, None, :], 0.0), axis=2)
@@ -1246,6 +1296,13 @@
         .astype(low)
         .reshape(SEQ, heads_here, HD)
     )
+    if grid.side == 2:
+        far, grad_mixed = lax.optimization_barrier((far, grad_mixed))
+        sums_kept = [
+            done[at].astype(jnp.float32) + part.astype(jnp.float32)
+            for at, part in zip((4, 5, 0, 1), far)
+        ]
+        near = [grid.send(sums_kept[at].astype(low), grid.first(1)) for at in (1, 3)]
     masked = masked_scores()
     attn_probs = jnp.exp(masked - log_total)
     probs_again = attn_probs.astype(low)
@@ -1260,6 +1317,12 @@
     grad_scores = (
         attn_probs * (grad_probs - jnp.sum(attn_probs * grad_probs, axis=-1, keepdims=True))
     ).astype(low)
+    if grid.side == 2:
+        near, grad_scores = lax.optimization_barrier((near, grad_scores))
+        crossing = [
+            grid.send((kept + part.astype(jnp.float32)).astype(low), grid.planes_of(turn))
+            for kept, part, turn in zip(sums_kept[::2], near, (1, 0))
+        ]
     grad_queries = (
         jnp.einsum("hqk,khd->qhd", grad_scores, keys_rot, preferred_element_type=jnp.float32)
         * scale
@@ -1311,6 +1374,10 @@
         grad_wq, grad_wk, grad_wv, grad_wo, sums, *received = reduce_all(
             weight_parts, parts, [gate_w, up_w, down_w], count
         )
+        crossing, sums = lax.optimization_barrier((crossing, sums))
+        out_sum = both_cores(
+            (crossing[0].astype(jnp.float32) + crossing[1].astype(jnp.float32)).astype(low)
+        )
     else:
         shape = (PLANES, grid.side, grid.side)
         grad_wq, grad_wk, grad_wv, grad_wo = [
@@ -1322,6 +1389,8 @@
         )
         sums = sums + swap(sums)
         received = [swap(part) for part in (gate_w[:, half:], up_w[:, half:], down_w[half:])]
+        out_sum = scatter_tokens(grid, out_turns)
+    output = (resid_one + out_sum).astype(low)
     grad_gate_w = (gate_w[:, :half] + received[0])[None]
     grad_up_w = (up_w[:, :half] + received[1])[None]
     grad_down_w = (down_w[:half] + received[2])[None]

time: 1260 us -> 1210 us (0.960)
  starting transfers between devices: 132 us -> 79.4 us
  Pallas kernels: 815 us -> 785 us
  matrix products: 111 us -> 134 us
    ppermute x4, starting transfers between devices: 122 us -> 54.1 us  [swap(): return lax.ppermute(value, 'tensor', [(0, 1), (1, 0)])]
    pallas_call x1, Pallas kernels: 345 us -> 324 us  [moe_layer(): pl.pallas_call(functools.partial(moe_kernel, capacity, experts), in_specs...]
    sub x0 -> x1, matrix products: none -> 16.2 us  [local(): grad_probs - jnp.sum(attn_probs * grad_probs, axis=-1, keepdims=True)]
    ppermute x8, starting transfers between devices: 9.72 us -> 25.3 us  [send(): return lax.ppermute(value, ('expert', 'tensor'), pairs)]
  transfers between devices with their start and end apart: 12 -> 12, of which waited for: 3 -> 6; matrix products, arithmetic and copies ran while one was open for 7% -> 10% of each run, Pallas kernels for 0% -> 14%
where the time goes in v4:
time: 1210 us; the launch traced here: 1200 us
  Pallas kernels  785 us (65%)
  matrix products  134 us (11%)
  other arithmetic  92.4 us (8%)
  waiting for transfers between devices  79.5 us (7%)
  starting transfers between devices  79.4 us (7%)
  local copies, waits for them, and re-layouts  30.3 us (3%)
    pallas_call x1, Pallas kernels, moe_layer(): pl.pallas_call(functools.partial(moe_kernel, capacity, experts), in_specs...  324 us
    pallas_call x1, Pallas kernels, gather_all(): pl.pallas_call(functools.partial(gather_kernel, rows), in_specs=[hbm] * 9...  297 us
    pallas_call x1, Pallas kernels, reduce_all(): pl.pallas_call(functools.partial(reduce_kernel, rows), in_specs=[hbm] * 8...  163 us
    ppermute x8, waiting for transfers between devices, send(): return lax.ppermute(value, ('expert', 'tensor'), pairs)  75.8 us
    dot_general x8, matrix products, contract_rows(): lax.dot_general(left_mat, right_mat, (((0,), (0,)), ((), ())), preferred_...  61.6 us
    ppermute x4, starting transfers between devices, swap(): return lax.ppermute(value, 'tensor', [(0, 1), (1, 0)])  54.1 us
    ppermute x8, starting transfers between devices, send(): return lax.ppermute(value, ('expert', 'tensor'), pairs)  25.3 us
  transfers between devices with their start and end apart: 12, of which 6 were waited for; matrix products, arithmetic and copies ran while one was open for 10% of the time, Pallas kernels for 14%

profile of v4, /device:TPU:0, one launch (start us, length us, event | category | flops | bytes accessed | tf_op | source)
XLA Modules:
  0.0 1203.0 jit_solution(1246453932235983061)
XLA Ops:
  15.2 297.0 %gather_all.1 = (bf16[2048,1024]{1,0:T(8,128)(2,1)}, bf16[2048,1024]{1,0:T(8,128)(2,1)}, bf16[2048,1024]{1,0:T(8,128)(2,1)}, bf16[2048,1024]{1,0:T(8,128)(2,1)},...) custom-call(bf16[128,1024]{1,0:T(8,128)(2,1)} %convert_element_type., ...), custom_call_target="tpu_custom_call" | custom-call | tf_op jit(solution)/shard_map/gather_all/pallas_call | solution.py:378
  314.5 4.6 fusion.93
  321.7 4.6 fusion.95
  328.9 4.7 fusion.45
  368.2 324.0 %moe_layer.1 = (bf16[512,2048]{1,0:T(8,128)(2,1)}, bf16[512,2048]{1,0:T(8,128)(2,1)}, bf16[512,2048]{1,0:T(8,128)(2,1)}, bf16[512,2048]{1,0:T(8,128)(2,1)}, bf16...) custom-call(bf16[528,2048]{1,0:T(8,128)(2,1)} %pad_maximum_fusion.ow, ...), custom_call_target="tpu_custom_call" | custom-call | tf_op jit(solution)/shard_map/moe_layer/pallas_call | solution.py:1079
  692.3 53.2 %collective-permute-start.5 = (bf16[528,2048]{1,0:T(8,128)(2,1)}, bf16[528,2048]{1,0:T(8,128)(2,1)S(1)}, u32[]{:S(2)}, u32[]{:S(2)}) collective-permute-start(bf16[528,2048]{1,0:T(8,128)(2,1)} %get-tuple-element.74), channel_id=1, source_target_pairs={{0,1},{1,0},{2,3},{3,2},{4,5},{5,4},{6,7},{7,6},{8,9},{9,8},{10,11... | collective-permute-start | bytes 6488072 | tf_op jit(solution)/shard_map/ppermute | solution.py:102
  745.5 16.6 %fusion.100.refs_6_ = f32[2048,1024]{1,0:T(8,128)} fusion(bf16[2304,2048]{1,0:T(8,128)(2,1)} %get-tuple-element.75, bf16[2304,1024]{1,0:T(8,128)(2,1)} %get-tuple-element.77), kind=kOutput, calls=%fused_computation.206 | convolution fusion | flops 9663676416 | bytes 22544384 | tf_op jit(solution)/shard_map/dot_general | solution.py:61
  762.1 14.1 %fusion.99.refs_5_ = f32[2048,1024]{1,0:T(8,128)} fusion(bf16[2304,2048]{1,0:T(8,128)(2,1)S(1)} %copy-done.98, bf16[2304,1024]{1,0:T(8,128)(2,1)} %get-tuple-element.76), kind=kOutput, calls=%fused_computation.205 | convolution fusion | flops 9663676416 | bytes 22544384 | tf_op jit(solution)/shard_map/dot_general | solution.py:61
  780.3 12.5 %fusion.101.refs_7_ = f32[1024,2048]{1,0:T(8,128)} fusion(bf16[2304,1024]{1,0:T(8,128)(2,1)S(1)} %bitcast.244, bf16[2304,2048]{1,0:T(8,128)(2,1)S(1)} %bitcast.242), kind=kOutput, calls=%fused_computation.207 | convolution fusion | flops 9663676416 | bytes 22544384 | tf_op jit(solution)/shard_map/dot_general | solution.py:61
  802.4 22.5 %collective-permute-done.2 = bf16[512,2048]{1,0:T(8,128)(2,1)S(1)} collective-permute-done((bf16[512,2048]{1,0:T(8,128)(2,1)}, bf16[512,2048]{1,0:T(8,128)(2,1)S(1)}, u32[]{:S(2)}, u32[]{:S(2)}) %collective-permute-start.2) | collective-permute-done | bytes 2097184 | tf_op jit(solution)/shard_map/ppermute | solution.py:98
  824.9 22.5 %collective-permute-done.3 = bf16[512,2048]{1,0:T(8,128)(2,1)S(1)} collective-permute-done((bf16[512,2048]{1,0:T(8,128)(2,1)}, bf16[512,2048]{1,0:T(8,128)(2,1)S(1)}, u32[]{:S(2)}, u32[]{:S(2)}) %collective-permute-start.3) | collective-permute-done | bytes 2097184 | tf_op jit(solution)/shard_map/ppermute | solution.py:98
  847.4 22.5 %collective-permute-done.4 = bf16[512,2048]{1,0:T(8,128)(2,1)S(1)} collective-permute-done((bf16[512,2048]{1,0:T(8,128)(2,1)S(1)}, bf16[512,2048]{1,0:T(8,128)(2,1)S(1)}, u32[]{:S(2)}, u32[]{:S(2)}) %collective-permute-start.4) | collective-permute-done | bytes 2097184 | tf_op jit(solution)/shard_map/ppermute | solution.py:98
  872.1 4.6 add_convert_fusion.5
  880.9 5.6 fusion.42
  887.5 4.6 convolution_convert_fusion.1.refs_2_
  892.1 4.5 fusion.48
  901.1 16.2 %multiply_convert_fusion = bf16[8,512,512]{1,2,0:T(8,128)(2,1)} fusion(f32[8,512,512]{1,2,0:T(8,128)} %fusion.48, f32[8,512]{1,0:T(8,128)S(1)} %copy-done.89, pred[512]{0:T(512)(128)(4,1)S(1)} %copy-done.91, bf16[512,8,64]{2,0,1:T(8,128)(2,1)} %copy-done.24, bf16[512,8,64]{2,0,1:T(8,128)(2,1)} %copy-done.25, bf16[512,8,64]{2,0,1:T(8,128)(2,1)} %copy-done.22, ...), kind=kOutput, calls=%fused_computation.1 | convolution fusion | flops 1103106560 | bytes 14696960 | tf_op jit(solution)/shard_map/sub | solution.py:1318
  917.3 8.2 collective-permute-done.6
  925.5 4.6 multiply_bitcast_fusion.1
  966.5 17.4 %collective-permute-start.9 = (bf16[512,2048]{1,0:T(8,128)(2,1)}, bf16[512,2048]{1,0:T(8,128)(2,1)}, u32[]{:S(2)}, u32[]{:S(2)}) collective-permute-start(bf16[512,2048]{1,0:T(8,128)(2,1)} %add_convert_fusion.3), channel_id=1, source_target_pairs={{0,0},{1,9},{2,2},{3,11},{4,4},{5,13},{6,6},{7,15},{8,8},{9,1},{10... | collective-permute-start | bytes 6291464 | tf_op jit(solution)/shard_map/ppermute | solution.py:98
  990.8 4.5 convolution_convert_fusion.2.refs_1_
  1004.2 163.5 %reduce_all.1 = (f32[128,1024]{1,0:T(8,128)}, f32[128,1024]{1,0:T(8,128)}, f32[128,1024]{1,0:T(8,128)}, f32[128,1024]{1,0:T(8,128)}, f32[24,128]{1,0:T(8,128)}, ...) custom-call(bf16[2048,1024]{1,0:T(8,128)(2,1)} %convolution_convert_fusion.3.refs_0_, ...), custom_call_target="tpu_custom_call" | custom-call | tf_op jit(solution)/shard_map/reduce_all/pallas_call | solution.py:615
  1171.6 6.7 add_bitcast_fusion
  1190.1 5.2 fusion.19
  (373 shorter events, 155.5 us)
Async XLA Ops:
  1.4 342.2 %copy-start.90 = (pred[512]{0:T(512)(128)(4,1)}, pred[512]{0:T(512)(128)(4,1)S(1)}, u32[]{:S(2)}) copy-start(pred[512]{0:T(512)(128)(4,1)S(1)} %iota_compare_fusion.4) | copy-start | bytes 1540
  15.2 298.8 %copy-start.6 = (bf16[512,2048]{1,0:T(8,128)(2,1)S(1)}, bf16[512,2048]{1,0:T(8,128)(2,1)}, u32[]{:S(2)}) copy-start(bf16[512,2048]{1,0:T(8,128)(2,1)} %param.16) | copy-start | bytes 6291460
  313.1 50.4 %copy-start.75 = (f32[16,1,128]{2,1,0:T(1,128)}, f32[16,1,128]{2,1,0:T(1,128)S(1)}, u32[]{:S(2)}) copy-start(f32[16,1,128]{2,1,0:T(1,128)S(1)} %get-tuple-element.132) | copy-start | bytes 24580
  321.6 30.5 %copy-start.71 = (f32[512,8]{0,1:T(8,128)}, f32[512,8]{0,1:T(8,128)S(1)}, u32[]{:S(2)}) copy-start(f32[512,8]{0,1:T(8,128)S(1)} %add_rsqrt_fusion) | copy-start | bytes 49156
  321.7 32.1 %copy-start.94 = (f32[128]{0:T(128)}, f32[128]{0:T(128)S(1)}, u32[]{:S(2)}) copy-start(f32[128]{0:T(128)S(1)} %reshape.330) | copy-start | bytes 1540
  328.8 24.1 %copy-start.69 = (f32[512,8]{0,1:T(8,128)}, f32[512,8]{0,1:T(8,128)S(1)}, u32[]{:S(2)}) copy-start(f32[512,8]{0,1:T(8,128)S(1)} %add_rsqrt_fusion.1) | copy-start | bytes 49156
  328.9 25.5 %copy-start.92 = (f32[128]{0:T(128)}, f32[128]{0:T(128)S(1)}, u32[]{:S(2)}) copy-start(f32[128]{0:T(128)S(1)} %reshape.329) | copy-start | bytes 1540
  351.4 7.8 collective-permute-start
  692.3 100.6 %collective-permute-start.5 = (bf16[528,2048]{1,0:T(8,128)(2,1)}, bf16[528,2048]{1,0:T(8,128)(2,1)S(1)}, u32[]{:S(2)}, u32[]{:S(2)}) collective-permute-start(bf16[528,2048]{1,0:T(8,128)(2,1)} %get-tuple-element.74), channel_id=1, source_target_pairs={{0,1},{1,0},{2,3},{3,2},{4,5},{5,4},{6,7},{7,6},{8,9},{9,8},{10,11... | collective-permute-start | bytes 6488072 | tf_op jit(solution)/shard_map/ppermute | solution.py:102
  745.5 34.8 %slice-start.4 = ((s8[9437184]{0:T(1024)(128)(4,1)}), s8[4194304]{0:T(1024)(128)(4,1)S(1)}, s32[]{:S(2)}) async-start(s8[9437184]{0:T(1024)(128)(4,1)} %bitcast.241), calls=%async_computation.4 | async-start | bytes 8388608
  745.5 34.8 %slice-start.5 = ((s8[9437184]{0:T(1024)(128)(4,1)}), s8[4194304]{0:T(1024)(128)(4,1)S(1)}, s32[]{:S(2)}) async-start(s8[9437184]{0:T(1024)(128)(4,1)} %bitcast.241), calls=%async_computation.5 | async-start | bytes 8388608
  745.5 34.8 %slice-start.7 = ((s8[4718592]{0:T(1024)(128)(4,1)}), s8[4194304]{0:T(1024)(128)(4,1)S(1)}, s32[]{:S(2)}) async-start(s8[4718592]{0:T(1024)(128)(4,1)} %bitcast.243), calls=%async_computation.7 | async-start | bytes 8388608
  776.2 26.2 %collective-permute-start.1 = (bf16[512,2048]{1,0:T(8,128)(2,1)}, bf16[512,2048]{1,0:T(8,128)(2,1)S(1)}, u32[]{:S(2)}, u32[]{:S(2)}) collective-permute-start(bf16[512,2048]{1,0:T(8,128)(2,1)} %get-tuple-element.70), channel_id=1, source_target_pairs={{0,4},{1,3},{2,6},{3,1},{4,0},{5,7},{6,2},{7,5},{8,12},{9,11},{10,... | collective-permute-start | bytes 6291464 | tf_op jit(solution)/shard_map/ppermute | solution.py:98
  777.2 47.7 %collective-permute-start.2 = (bf16[512,2048]{1,0:T(8,128)(2,1)}, bf16[512,2048]{1,0:T(8,128)(2,1)S(1)}, u32[]{:S(2)}, u32[]{:S(2)}) collective-permute-start(bf16[512,2048]{1,0:T(8,128)(2,1)} %get-tuple-element.71), channel_id=1, source_target_pairs={{0,4},{1,3},{2,6},{3,1},{4,0},{5,7},{6,2},{7,5},{8,12},{9,11},{10,... | collective-permute-start | bytes 6291464 | tf_op jit(solution)/shard_map/ppermute | solution.py:98
  778.2 69.2 %collective-permute-start.3 = (bf16[512,2048]{1,0:T(8,128)(2,1)}, bf16[512,2048]{1,0:T(8,128)(2,1)S(1)}, u32[]{:S(2)}, u32[]{:S(2)}) collective-permute-start(bf16[512,2048]{1,0:T(8,128)(2,1)} %get-tuple-element.72), channel_id=1, source_target_pairs={{0,4},{1,3},{2,6},{3,1},{4,0},{5,7},{6,2},{7,5},{8,12},{9,11},{10,... | collective-permute-start | bytes 6291464 | tf_op jit(solution)/shard_map/ppermute | solution.py:98
  779.2 90.6 %collective-permute-start.4 = (bf16[512,2048]{1,0:T(8,128)(2,1)S(1)}, bf16[512,2048]{1,0:T(8,128)(2,1)S(1)}, u32[]{:S(2)}, u32[]{:S(2)}) collective-permute-start(bf16[512,2048]{1,0:T(8,128)(2,1)S(1)} %copy-done.104), channel_id=1, source_target_pairs={{0,4},{1,3},{2,6},{3,1},{4,0},{5,7},{6,2},{7,5},{8,12},{9,11},{10,... | collective-permute-start | bytes 6291464 | tf_op jit(solution)/shard_map/ppermute | solution.py:98
  802.4 67.4 %copy-start.47 = (bf16[512,2048]{1,0:T(8,128)(2,1)}, bf16[512,2048]{1,0:T(8,128)(2,1)S(1)}, u32[]{:S(2)}) copy-start(bf16[512,2048]{1,0:T(8,128)(2,1)S(1)} %collective-permute-done.1) | copy-start | bytes 6291460
  824.9 44.9 %copy-start.42 = (bf16[512,2048]{1,0:T(8,128)(2,1)}, bf16[512,2048]{1,0:T(8,128)(2,1)S(1)}, u32[]{:S(2)}) copy-start(bf16[512,2048]{1,0:T(8,128)(2,1)S(1)} %collective-permute-done.2) | copy-start | bytes 6291460
  876.7 40.6 %collective-permute-start.7 = (bf16[512,2048]{1,0:T(8,128)(2,1)}, bf16[512,2048]{1,0:T(8,128)(2,1)}, u32[]{:S(2)}, u32[]{:S(2)}) collective-permute-start(bf16[512,2048]{1,0:T(8,128)(2,1)} %add_convert_fusion.5), channel_id=1, source_target_pairs={{0,2},{1,5},{2,0},{3,7},{4,6},{5,1},{6,4},{7,3},{8,10},{9,13},{10,... | collective-permute-start | bytes 6291464 | tf_op jit(solution)/shard_map/ppermute | solution.py:98
  879.9 45.7 %collective-permute-start.6 = (bf16[512,2048]{1,0:T(8,128)(2,1)}, bf16[512,2048]{1,0:T(8,128)(2,1)}, u32[]{:S(2)}, u32[]{:S(2)}) collective-permute-start(bf16[512,2048]{1,0:T(8,128)(2,1)} %add_convert_fusion.6), channel_id=1, source_target_pairs={{0,2},{1,5},{2,0},{3,7},{4,6},{5,1},{6,4},{7,3},{8,10},{9,13},{10,... | collective-permute-start | bytes 6291464 | tf_op jit(solution)/shard_map/ppermute | solution.py:98
  962.0 37.8 %collective-permute-start.10 = (bf16[512,2048]{1,0:T(8,128)(2,1)}, bf16[512,2048]{1,0:T(8,128)(2,1)}, u32[]{:S(2)}, u32[]{:S(2)}) collective-permute-start(bf16[512,2048]{1,0:T(8,128)(2,1)} %add_convert_fusion.2), channel_id=1, source_target_pairs={{0,1},{1,0},{2,3},{3,2},{4,5},{5,4},{6,7},{7,6},{8,9},{9,8},{10,11... | collective-permute-start | bytes 6291464 | tf_op jit(solution)/shard_map/ppermute | solution.py:102
  966.5 201.2 %collective-permute-start.9 = (bf16[512,2048]{1,0:T(8,128)(2,1)}, bf16[512,2048]{1,0:T(8,128)(2,1)}, u32[]{:S(2)}, u32[]{:S(2)}) collective-permute-start(bf16[512,2048]{1,0:T(8,128)(2,1)} %add_convert_fusion.3), channel_id=1, source_target_pairs={{0,0},{1,9},{2,2},{3,11},{4,4},{5,13},{6,6},{7,15},{8,8},{9,1},{10... | collective-permute-start | bytes 6291464 | tf_op jit(solution)/shard_map/ppermute | solution.py:98
  988.3 179.5 %collective-permute-start.8 = (bf16[512,2048]{1,0:T(8,128)(2,1)}, bf16[512,2048]{1,0:T(8,128)(2,1)}, u32[]{:S(2)}, u32[]{:S(2)}) collective-permute-start(bf16[512,2048]{1,0:T(8,128)(2,1)} %add_convert_fusion.4), channel_id=1, source_target_pairs={{0,24},{1,17},{2,26},{3,19},{4,28},{5,21},{6,30},{7,23},{8,16},{9,... | collective-permute-start | bytes 6291464 | tf_op jit(solution)/shard_map/ppermute | solution.py:98
  1181.4 13.9 %collective-permute-start.11 = (bf16[512,2048]{1,0:T(8,128)(2,1)S(1)}, bf16[512,2048]{1,0:T(8,128)(2,1)}, u32[]{:S(2)}, u32[]{:S(2)}) collective-permute-start(bf16[512,2048]{1,0:T(8,128)(2,1)S(1)} %add_convert_fusion.1), channel_id=1, source_target_pairs={{0,1},{1,0},{2,3},{3,2},{4,5},{5,4},{6,7},{7,6},{8,9},{9,8},{10,11... | collective-permute-start | bytes 6291464 | tf_op jit(solution)/shard_map/ppermute | solution.py:102
  (107 other events, 564.4 us)

commit v5 on v4

--- a/solution.py
+++ b/solution.py
@@ -719,7 +719,7 @@
     *refs,
 ):
     weights, grads, refs = refs[:6], refs[6], refs[7:]
-    parts, refs = refs[:8], refs[8:]
+    parts, outs, refs = refs[:8], refs[8:12], refs[12:]
     (
     blocks,
     far_sums,
@@ -756,6 +756,8 @@
     back_recv,
     piece_send,
     piece_recv,
+    out_send,
+    out_recv,
     ) = refs
     me = lax.axis_index("expert")
     core = lax.axis_index("tensor")
@@ -877,6 +879,16 @@
 
     def plane_piece(piece):
         return give_piece(stage.at[4], plane_sums.at[1], 3, piece, far_plane)
+
+    def send_out(index):
+        return pltpu.make_async_remote_copy(
+            src_ref=parts[(2, 3, 6, 7)[index]],
+            dst_ref=outs[index],
+            send_sem=out_send.at[index],
+            recv_sem=out_recv.at[index],
+            device_id=(second, core),
+            device_id_type=mesh,
+        )
 
     def first_sum(turn):
         give(far_sums.at[2 * turn + 1], far_sums.at[2 * turn + 1], 2 * turn + 1, second).wait_recv()
@@ -971,9 +983,17 @@
         for copy in saves:
             copy.start()
 
-        @pl.when(k > 0)
-        def _():
-            pltpu.make_async_copy(part_v, parts[0], save_sem.at[5]).wait()
+        for index in range(8):
+
+            @pl.when(k == index + 1)
+            def _():
+                pltpu.make_async_copy(part_v, parts[index], save_sem.at[5]).wait()
+
+        for index in range(2):
+
+            @pl.when(k == 3 + index)
+            def _():
+                send_out(index).start()
 
         for at in range(0, width, 512):
             span = slice(at, at + 512)
@@ -1027,6 +1047,9 @@
         return carry
 
     lax.fori_loop(0, 8, block_step, 0)
+    pltpu.make_async_copy(part_v, parts[7], save_sem.at[5]).wait()
+    send_out(2).start()
+    send_out(3).start()
     for piece in range(pieces):
         far_piece(1, piece).wait_recv()
         add_block(5, [far_sums.at[3]], piece * size, size)
@@ -1048,7 +1071,8 @@
         add_block(0, [plane_sums.at[1]], piece * size, size)
     final = pltpu.make_async_copy(stage.at[0], result, load_sem.at[0])
     final.start()
-    pltpu.make_async_copy(part_v, parts[7], save_sem.at[5]).wait()
+    for index in range(4):
+        send_out(index).wait()
     for k in range(8):
         if k > 0:
             pass_on(blocks.at[k], k, first).wait_send()
@@ -1079,8 +1103,8 @@
     return pl.pallas_call(
         functools.partial(moe_kernel, capacity, experts),
         in_specs=[hbm] * 8,
-        out_specs=[hbm] * 18,
-        out_shape=[shape(SEQ, width)] * 8
+        out_specs=[hbm] * 22,
+        out_shape=[shape(SEQ, width)] * 12
         + [
             shape(8, rows, width),
             shape(4, rows, width),
@@ -1119,6 +1143,8 @@
             pltpu.SemaphoreType.DMA((8,)),
             pltpu.SemaphoreType.DMA((4, 3)),
             pltpu.SemaphoreType.DMA((4, 3)),
+            pltpu.SemaphoreType.DMA((4,)),
+            pltpu.SemaphoreType.DMA((4,)),
         ],
         compiler_params=pltpu.CompilerParams(
             collective_id=0, has_side_effects=True, vmem_limit_bytes=67043328
@@ -1249,9 +1275,13 @@
     token_block = jnp.concatenate([ffn_in, gate_rows], axis=0)
     if grid.side == 2:
         done = moe_layer(token_block, grad_blocks, halves + others, capacity)
-        saved = [tuple(done[12:17])]
-        far = [grid.send(done[at], grid.second(1)) for at in (6, 7, 2, 3)]
-        back_sum = both_cores(done[17])
+        saved = [tuple(done[16:21])]
+        sums_kept = [
+            done[at].astype(jnp.float32) + done[part].astype(jnp.float32)
+            for at, part in zip((4, 5, 0, 1), (10, 11, 8, 9))
+        ]
+        near = [grid.send(sums_kept[at].astype(low), grid.first(1)) for at in (1, 3)]
+        back_sum = both_cores(done[21])
     else:
         wg, wu, wd = (
             jnp.concatenate([half, swap(half)], axis=axis) for half, axis in zip(halves, (1, 1, 0))
@@ -1297,12 +1327,11 @@
         .reshape(SEQ, heads_here, HD)
     )
     if grid.side == 2:
-        far, grad_mixed = lax.optimization_barrier((far, grad_mixed))
-        sums_kept = [
-            done[at].astype(jnp.float32) + part.astype(jnp.float32)
-            for at, part in zip((4, 5, 0, 1), far)
+        near, grad_mixed = lax.optimization_barrier((near, grad_mixed))
+        crossing = [
+            grid.send((kept + part.astype(jnp.float32)).astype(low), grid.planes_of(turn))
+            for kept, part, turn in zip(sums_kept[::2], near, (1, 0))
         ]
-        near = [grid.send(sums_kept[at].astype(low), grid.first(1)) for at in (1, 3)]
     masked = masked_scores()
     attn_probs = jnp.exp(masked - log_total)
     probs_again = attn_probs.astype(low)
@@ -1317,12 +1346,6 @@
     grad_scores = (
         attn_probs * (grad_probs - jnp.sum(attn_probs * grad_probs, axis=-1, keepdims=True))
     ).astype(low)
-    if grid.side == 2:
-        near, grad_scores = lax.optimization_barrier((near, grad_scores))
-        crossing = [
-            grid.send((kept + part.astype(jnp.float32)).astype(low), grid.planes_of(turn))
-            for kept, part, turn in zip(sums_kept[::2], near, (1, 0))
-        ]
     grad_queries = (
         jnp.einsum("hqk,khd->qhd", grad_scores, keys_rot, preferred_element_type=jnp.float32)
         * scale

time: 1210 us -> 1190 us (0.983)
  waiting for transfers between devices: 79.5 us -> 25.4 us
  Pallas kernels: 785 us -> 824 us
  matrix products: 134 us -> 112 us
    ppermute x8 -> x4, waiting for transfers between devices: 75.8 us -> 21.7 us  [send(): return lax.ppermute(value, ('expert', 'tensor'), pairs)]
    pallas_call x1, Pallas kernels: 324 us -> 364 us  [moe_layer(): pl.pallas_call(functools.partial(moe_kernel, capacity, experts), in_specs...]
    sub x1 -> x0, matrix products: 16.2 us -> none  [local(): grad_probs - jnp.sum(attn_probs * grad_probs, axis=-1, keepdims=True)]
    ppermute x8 -> x4, starting transfers between devices: 25.3 us -> 21.3 us  [send(): return lax.ppermute(value, ('expert', 'tensor'), pairs)]
  transfers between devices with their start and end apart: 12 -> 8, of which waited for: 6 -> 2; matrix products, arithmetic and copies ran while one was open for 10% -> 6% of each run, Pallas kernels for 14% -> 14%
where the time goes in v5:
time: 1190 us; the launch traced here: 1180 us
  Pallas kernels  824 us (69%)
  matrix products  112 us (9%)
  other arithmetic  93.2 us (8%)
  starting transfers between devices  85.5 us (7%)
  local copies, waits for them, and re-layouts  32.9 us (3%)
  waiting for transfers between devices  25.4 us (2%)
    pallas_call x1, Pallas kernels, moe_layer(): pl.pallas_call(functools.partial(moe_kernel, capacity, experts), in_specs...  364 us
    pallas_call x1, Pallas kernels, gather_all(): pl.pallas_call(functools.partial(gather_kernel, rows), in_specs=[hbm] * 9...  297 us
    pallas_call x1, Pallas kernels, reduce_all(): pl.pallas_call(functools.partial(reduce_kernel, rows), in_specs=[hbm] * 8...  163 us
    ppermute x4, starting transfers between devices, swap(): return lax.ppermute(value, 'tensor', [(0, 1), (1, 0)])  64.2 us
    dot_general x8, matrix products, contract_rows(): lax.dot_general(left_mat, right_mat, (((0,), (0,)), ((), ())), preferred_...  62.5 us
  transfers between devices with their start and end apart: 8, of which 2 were waited for; matrix products, arithmetic and copies ran while one was open for 6% of the time, Pallas kernels for 14%

profile of v5, /device:TPU:0, one launch (start us, length us, event | category | flops | bytes accessed | tf_op | source)
XLA Modules:
  0.0 1176.4 jit_solution(4444159406414155164)
XLA Ops:
  17.3 297.0 %gather_all.1 = (bf16[2048,1024]{1,0:T(8,128)(2,1)}, bf16[2048,1024]{1,0:T(8,128)(2,1)}, bf16[2048,1024]{1,0:T(8,128)(2,1)}, bf16[2048,1024]{1,0:T(8,128)(2,1)},...) custom-call(bf16[128,1024]{1,0:T(8,128)(2,1)} %convert_element_type., ...), custom_call_target="tpu_custom_call" | custom-call | tf_op jit(solution)/shard_map/gather_all/pallas_call | solution.py:378
  316.6 4.6 fusion.75
  323.8 4.6 fusion.77
  331.0 4.7 fusion.33
  349.2 4.4 fusion.81
  361.3 4.2 multiply_reduce_fusion.3
  370.7 364.3 %moe_layer.1 = (bf16[512,2048]{1,0:T(8,128)(2,1)}, bf16[512,2048]{1,0:T(8,128)(2,1)}, bf16[512,2048]{1,0:T(8,128)(2,1)}, bf16[512,2048]{1,0:T(8,128)(2,1)}, bf16...) custom-call(bf16[528,2048]{1,0:T(8,128)(2,1)} %pad_maximum_fusion.ow, ...), custom_call_target="tpu_custom_call" | custom-call | tf_op jit(solution)/shard_map/moe_layer/pallas_call | solution.py:1103
  735.1 16.3 %fusion.83.refs_6_ = f32[2048,1024]{1,0:T(8,128)} fusion(bf16[2304,2048]{1,0:T(8,128)(2,1)} %get-tuple-element.71, bf16[2304,1024]{1,0:T(8,128)(2,1)} %get-tuple-element.73), kind=kOutput, calls=%fused_computation.192 | convolution fusion | flops 9663676416 | bytes 22544384 | tf_op jit(solution)/shard_map/dot_general | solution.py:61
  751.4 15.0 %fusion.82.refs_5_ = f32[2048,1024]{1,0:T(8,128)} fusion(bf16[2304,2048]{1,0:T(8,128)(2,1)} %get-tuple-element.71, bf16[2304,1024]{1,0:T(8,128)(2,1)S(1)} %copy-done.97), kind=kOutput, calls=%fused_computation.191 | convolution fusion | flops 9663676416 | bytes 22544384 | tf_op jit(solution)/shard_map/dot_general | solution.py:61
  766.4 63.3 %collective-permute-start.3 = (bf16[528,2048]{1,0:T(8,128)(2,1)S(1)}, bf16[528,2048]{1,0:T(8,128)(2,1)S(1)}, u32[]{:S(2)}, u32[]{:S(2)}) collective-permute-start(bf16[528,2048]{1,0:T(8,128)(2,1)S(1)} %copy-done.39), channel_id=1, source_target_pairs={{0,1},{1,0},{2,3},{3,2},{4,5},{5,4},{6,7},{7,6},{8,9},{9,8},{10,11... | collective-permute-start | bytes 6488072 | tf_op jit(solution)/shard_map/ppermute | solution.py:102
  833.6 12.8 %fusion.84.refs_7_ = f32[1024,2048]{1,0:T(8,128)} fusion(bf16[2304,1024]{1,0:T(8,128)(2,1)S(1)} %bitcast.250, bf16[2304,2048]{1,0:T(8,128)(2,1)S(1)} %bitcast.248), kind=kOutput, calls=%fused_computation.193 | convolution fusion | flops 9663676416 | bytes 22544384 | tf_op jit(solution)/shard_map/dot_general | solution.py:61
  857.4 21.7 %collective-permute-done.1 = bf16[512,2048]{1,0:T(8,128)(2,1)S(1)} collective-permute-done((bf16[512,2048]{1,0:T(8,128)(2,1)S(1)}, bf16[512,2048]{1,0:T(8,128)(2,1)S(1)}, u32[]{:S(2)}, u32[]{:S(2)}) %collective-permute-start.1) | collective-permute-done | bytes 2097184 | tf_op jit(solution)/shard_map/ppermute | solution.py:98
  881.2 4.4 multiply_reduce_fusion
  885.6 5.0 multiply_convert_fusion
  908.1 4.4 fusion.86
  928.3 5.0 add_convert_fusion.3
  933.3 17.3 %collective-permute-start.5 = (bf16[512,2048]{1,0:T(8,128)(2,1)}, bf16[512,2048]{1,0:T(8,128)(2,1)}, u32[]{:S(2)}, u32[]{:S(2)}) collective-permute-start(bf16[512,2048]{1,0:T(8,128)(2,1)} %add_convert_fusion.3), channel_id=1, source_target_pairs={{0,0},{1,9},{2,2},{3,11},{4,4},{5,13},{6,6},{7,15},{8,8},{9,1},{10... | collective-permute-start | bytes 6291464 | tf_op jit(solution)/shard_map/ppermute | solution.py:98
  955.3 4.5 convolution_convert_fusion.2.refs_1_
  959.8 4.6 convolution_convert_fusion.1.refs_2_
  964.4 4.5 convolution_convert_fusion.3.refs_0_
  968.9 4.4 convolution_convert_fusion.refs_3_
  978.1 162.9 %reduce_all.1 = (f32[128,1024]{1,0:T(8,128)}, f32[128,1024]{1,0:T(8,128)}, f32[128,1024]{1,0:T(8,128)}, f32[128,1024]{1,0:T(8,128)}, f32[24,128]{1,0:T(8,128)}, ...) custom-call(bf16[2048,1024]{1,0:T(8,128)(2,1)} %convolution_convert_fusion.3.refs_0_, ...), custom_call_target="tpu_custom_call" | custom-call | tf_op jit(solution)/shard_map/reduce_all/pallas_call | solution.py:615
  1144.8 6.7 add_bitcast_fusion
  1163.4 5.2 fusion.12
  (362 shorter events, 131.3 us)
Async XLA Ops:
  3.4 337.8 %copy-start.93 = (pred[512]{0:T(512)(128)(4,1)}, pred[512]{0:T(512)(128)(4,1)S(1)}, u32[]{:S(2)}) copy-start(pred[512]{0:T(512)(128)(4,1)S(1)} %iota_compare_fusion.4) | copy-start | bytes 1540
  17.3 298.8 %copy-start.6 = (bf16[512,2048]{1,0:T(8,128)(2,1)S(1)}, bf16[512,2048]{1,0:T(8,128)(2,1)}, u32[]{:S(2)}) copy-start(bf16[512,2048]{1,0:T(8,128)(2,1)} %param.16) | copy-start | bytes 6291460
  315.2 50.4 %copy-start.73 = (f32[16,1,128]{2,1,0:T(1,128)}, f32[16,1,128]{2,1,0:T(1,128)S(1)}, u32[]{:S(2)}) copy-start(f32[16,1,128]{2,1,0:T(1,128)S(1)} %get-tuple-element.122) | copy-start | bytes 24580
  323.7 30.5 %copy-start.69 = (f32[512,8]{0,1:T(8,128)}, f32[512,8]{0,1:T(8,128)S(1)}, u32[]{:S(2)}) copy-start(f32[512,8]{0,1:T(8,128)S(1)} %add_rsqrt_fusion) | copy-start | bytes 49156
  323.8 32.1 %copy-start.91 = (f32[128]{0:T(128)}, f32[128]{0:T(128)S(1)}, u32[]{:S(2)}) copy-start(f32[128]{0:T(128)S(1)} %reshape.330) | copy-start | bytes 1540
  331.0 25.5 %copy-start.89 = (f32[128]{0:T(128)}, f32[128]{0:T(128)S(1)}, u32[]{:S(2)}) copy-start(f32[128]{0:T(128)S(1)} %reshape.329) | copy-start | bytes 1540
  353.6 7.8 collective-permute-start
  735.1 98.5 %slice-start.6 = ((s8[9437184]{0:T(1024)(128)(4,1)}), s8[4194304]{0:T(1024)(128)(4,1)S(1)}, s32[]{:S(2)}) async-start(s8[9437184]{0:T(1024)(128)(4,1)} %bitcast.247), calls=%async_computation.6 | async-start | bytes 8388608
  735.1 98.5 %slice-start.7 = ((s8[9437184]{0:T(1024)(128)(4,1)}), s8[4194304]{0:T(1024)(128)(4,1)S(1)}, s32[]{:S(2)}) async-start(s8[9437184]{0:T(1024)(128)(4,1)} %bitcast.247), calls=%async_computation.7 | async-start | bytes 8388608
  735.1 98.5 %slice-start.9 = ((s8[4718592]{0:T(1024)(128)(4,1)}), s8[4194304]{0:T(1024)(128)(4,1)S(1)}, s32[]{:S(2)}) async-start(s8[4718592]{0:T(1024)(128)(4,1)} %bitcast.249), calls=%async_computation.9 | async-start | bytes 8388608
  751.4 78.3 %copy-start.42 = (bf16[512,2048]{1,0:T(8,128)(2,1)S(1)}, bf16[512,2048]{1,0:T(8,128)(2,1)}, u32[]{:S(2)}) copy-start(bf16[512,2048]{1,0:T(8,128)(2,1)} %get-tuple-element.68) | copy-start | bytes 6291460
  751.4 78.3 %copy-start.43 = (bf16[512,2048]{1,0:T(8,128)(2,1)S(1)}, bf16[512,2048]{1,0:T(8,128)(2,1)}, u32[]{:S(2)}) copy-start(bf16[512,2048]{1,0:T(8,128)(2,1)} %get-tuple-element.69) | copy-start | bytes 6291460
  751.4 82.2 %slice-start.8 = ((s8[9437184]{0:T(1024)(128)(4,1)}), s8[1048576]{0:T(1024)(128)(4,1)S(1)}, s32[]{:S(2)}) async-start(s8[9437184]{0:T(1024)(128)(4,1)} %bitcast.247), calls=%async_computation.8 | async-start | bytes 2097152
  751.4 82.2 %slice-start.10 = ((s8[4718592]{0:T(1024)(128)(4,1)}), s8[524288]{0:T(1024)(128)(4,1)S(1)}, s32[]{:S(2)}) async-start(s8[4718592]{0:T(1024)(128)(4,1)} %bitcast.249), calls=%async_computation.10 | async-start | bytes 1048576
  766.4 65.3 %copy-start.40 = (bf16[512,2048]{1,0:T(8,128)(2,1)S(1)}, bf16[512,2048]{1,0:T(8,128)(2,1)}, u32[]{:S(2)}) copy-start(bf16[512,2048]{1,0:T(8,128)(2,1)} %get-tuple-element.66) | copy-start | bytes 6291460
  766.4 65.3 %copy-start.41 = (bf16[512,2048]{1,0:T(8,128)(2,1)S(1)}, bf16[512,2048]{1,0:T(8,128)(2,1)}, u32[]{:S(2)}) copy-start(bf16[512,2048]{1,0:T(8,128)(2,1)} %get-tuple-element.67) | copy-start | bytes 6291460
  766.4 80.1 %collective-permute-start.3 = (bf16[528,2048]{1,0:T(8,128)(2,1)S(1)}, bf16[528,2048]{1,0:T(8,128)(2,1)S(1)}, u32[]{:S(2)}, u32[]{:S(2)}) collective-permute-start(bf16[528,2048]{1,0:T(8,128)(2,1)S(1)} %copy-done.39), channel_id=1, source_target_pairs={{0,1},{1,0},{2,3},{3,2},{4,5},{5,4},{6,7},{7,6},{8,9},{9,8},{10,11... | collective-permute-start | bytes 6488072 | tf_op jit(solution)/shard_map/ppermute | solution.py:102
  830.6 26.8 %collective-permute-start.2 = (bf16[512,2048]{1,0:T(8,128)(2,1)S(1)}, bf16[512,2048]{1,0:T(8,128)(2,1)S(1)}, u32[]{:S(2)}, u32[]{:S(2)}) collective-permute-start(bf16[512,2048]{1,0:T(8,128)(2,1)S(1)} %add_convert_fusion.5), channel_id=1, source_target_pairs={{0,2},{1,5},{2,0},{3,7},{4,6},{5,1},{6,4},{7,3},{8,10},{9,13},{10,... | collective-permute-start | bytes 6291464 | tf_op jit(solution)/shard_map/ppermute | solution.py:98
  832.5 46.7 %collective-permute-start.1 = (bf16[512,2048]{1,0:T(8,128)(2,1)S(1)}, bf16[512,2048]{1,0:T(8,128)(2,1)S(1)}, u32[]{:S(2)}, u32[]{:S(2)}) collective-permute-start(bf16[512,2048]{1,0:T(8,128)(2,1)S(1)} %add_convert_fusion.6), channel_id=1, source_target_pairs={{0,2},{1,5},{2,0},{3,7},{4,6},{5,1},{6,4},{7,3},{8,10},{9,13},{10,... | collective-permute-start | bytes 6291464 | tf_op jit(solution)/shard_map/ppermute | solution.py:98
  856.3 24.9 %copy-start.51 = (bf16[64,8,8,128]{3,2,1,0:T(8,128)(2,1)S(1)}, bf16[64,8,8,128]{3,2,1,0:T(8,128)(2,1)}, u32[]{:S(2)}) copy-start(bf16[64,8,8,128]{3,2,1,0:T(8,128)(2,1)} %copy-done.50) | copy-start | bytes 3145732
  928.1 45.3 %collective-permute-start.6 = (bf16[512,2048]{1,0:T(8,128)(2,1)}, bf16[512,2048]{1,0:T(8,128)(2,1)}, u32[]{:S(2)}, u32[]{:S(2)}) collective-permute-start(bf16[512,2048]{1,0:T(8,128)(2,1)} %add_convert_fusion.2), channel_id=1, source_target_pairs={{0,1},{1,0},{2,3},{3,2},{4,5},{5,4},{6,7},{7,6},{8,9},{9,8},{10,11... | collective-permute-start | bytes 6291464 | tf_op jit(solution)/shard_map/ppermute | solution.py:102
  933.3 207.6 %collective-permute-start.5 = (bf16[512,2048]{1,0:T(8,128)(2,1)}, bf16[512,2048]{1,0:T(8,128)(2,1)}, u32[]{:S(2)}, u32[]{:S(2)}) collective-permute-start(bf16[512,2048]{1,0:T(8,128)(2,1)} %add_convert_fusion.3), channel_id=1, source_target_pairs={{0,0},{1,9},{2,2},{3,11},{4,4},{5,13},{6,6},{7,15},{8,8},{9,1},{10... | collective-permute-start | bytes 6291464 | tf_op jit(solution)/shard_map/ppermute | solution.py:98
  953.3 187.6 %collective-permute-start.4 = (bf16[512,2048]{1,0:T(8,128)(2,1)}, bf16[512,2048]{1,0:T(8,128)(2,1)}, u32[]{:S(2)}, u32[]{:S(2)}) collective-permute-start(bf16[512,2048]{1,0:T(8,128)(2,1)} %add_convert_fusion.4), channel_id=1, source_target_pairs={{0,24},{1,17},{2,26},{3,19},{4,28},{5,21},{6,30},{7,23},{8,16},{9,... | collective-permute-start | bytes 6291464 | tf_op jit(solution)/shard_map/ppermute | solution.py:98
  1154.8 13.8 %collective-permute-start.7 = (bf16[512,2048]{1,0:T(8,128)(2,1)S(1)}, bf16[512,2048]{1,0:T(8,128)(2,1)}, u32[]{:S(2)}, u32[]{:S(2)}) collective-permute-start(bf16[512,2048]{1,0:T(8,128)(2,1)S(1)} %add_convert_fusion.1), channel_id=1, source_target_pairs={{0,1},{1,0},{2,3},{3,2},{4,5},{5,4},{6,7},{7,6},{8,9},{9,8},{10,11... | collective-permute-start | bytes 6291464 | tf_op jit(solution)/shard_map/ppermute | solution.py:102
  (101 other events, 541.5 us)

commit v6 on v5

--- a/solution.py
+++ b/solution.py
@@ -1326,12 +1326,6 @@
         .astype(low)
         .reshape(SEQ, heads_here, HD)
     )
-    if grid.side == 2:
-        near, grad_mixed = lax.optimization_barrier((near, grad_mixed))
-        crossing = [
-            grid.send((kept + part.astype(jnp.float32)).astype(low), grid.planes_of(turn))
-            for kept, part, turn in zip(sums_kept[::2], near, (1, 0))
-        ]
     masked = masked_scores()
     attn_probs = jnp.exp(masked - log_total)
     probs_again = attn_probs.astype(low)
@@ -1346,6 +1340,12 @@
     grad_scores = (
         attn_probs * (grad_probs - jnp.sum(attn_probs * grad_probs, axis=-1, keepdims=True))
     ).astype(low)
+    if grid.side == 2:
+        near, grad_scores = lax.optimization_barrier((near, grad_scores))
+        crossing = [
+            grid.send((kept + part.astype(jnp.float32)).astype(low), grid.planes_of(turn))
+            for kept, part, turn in zip(sums_kept[::2], near, (1, 0))
+        ]
     grad_queries = (
         jnp.einsum("hqk,khd->qhd", grad_scores, keys_rot, preferred_element_type=jnp.float32)
         * scale

time: 1190 us -> 1180 us (level)
  waiting for transfers between devices: 25.4 us -> 3.67 us
  matrix products: 112 us -> 131 us
    ppermute x4, waiting for transfers between devices: 21.7 us -> 0.01 us  [send(): return lax.ppermute(value, ('expert', 'tensor'), pairs)]
    sub x0 -> x1, matrix products: none -> 14.8 us  [local(): grad_probs - jnp.sum(attn_probs * grad_probs, axis=-1, keepdims=True)]
  transfers between devices with their start and end apart: 8 -> 8, of which waited for: 2 -> 1; matrix products, arithmetic and copies ran while one was open for 6% -> 8% of each run, Pallas kernels for 14% -> 14%
where the time goes in v6:
time: 1180 us; the launch traced here: 1170 us
  Pallas kernels  824 us (70%)
  matrix products  131 us (11%)
  other arithmetic  90.4 us (8%)
  starting transfers between devices  85.5 us (7%)
  local copies, waits for them, and re-layouts  29.2 us (2%)
    pallas_call x1, Pallas kernels, moe_layer(): pl.pallas_call(functools.partial(moe_kernel, capacity, experts), in_specs...  364 us
    pallas_call x1, Pallas kernels, gather_all(): pl.pallas_call(functools.partial(gather_kernel, rows), in_specs=[hbm] * 9...  297 us
    pallas_call x1, Pallas kernels, reduce_all(): pl.pallas_call(functools.partial(reduce_kernel, rows), in_specs=[hbm] * 8...  163 us
    ppermute x4, starting transfers between devices, swap(): return lax.ppermute(value, 'tensor', [(0, 1), (1, 0)])  64.2 us
    dot_general x8, matrix products, contract_rows(): lax.dot_general(left_mat, right_mat, (((0,), (0,)), ((), ())), preferred_...  61.3 us
  transfers between devices with their start and end apart: 8, of which 1 were waited for; matrix products, arithmetic and copies ran while one was open for 8% of the time, Pallas kernels for 14%

profile of v6, /device:TPU:0, one launch (start us, length us, event | category | flops | bytes accessed | tf_op | source)
XLA Modules:
  0.0 1167.4 jit_solution(4431207435507298770)
XLA Ops:
  15.2 297.0 %gather_all.1 = (bf16[2048,1024]{1,0:T(8,128)(2,1)}, bf16[2048,1024]{1,0:T(8,128)(2,1)}, bf16[2048,1024]{1,0:T(8,128)(2,1)}, bf16[2048,1024]{1,0:T(8,128)(2,1)},...) custom-call(bf16[128,1024]{1,0:T(8,128)(2,1)} %convert_element_type., ...), custom_call_target="tpu_custom_call" | custom-call | tf_op jit(solution)/shard_map/gather_all/pallas_call | solution.py:378
  314.5 4.6 fusion.92
  321.7 4.6 fusion.94
  328.9 4.7 fusion.45
  347.0 4.4 fusion.97
  368.2 364.3 %moe_layer.1 = (bf16[512,2048]{1,0:T(8,128)(2,1)}, bf16[512,2048]{1,0:T(8,128)(2,1)}, bf16[512,2048]{1,0:T(8,128)(2,1)}, bf16[512,2048]{1,0:T(8,128)(2,1)}, bf16...) custom-call(bf16[528,2048]{1,0:T(8,128)(2,1)} %pad_maximum_fusion.ow, ...), custom_call_target="tpu_custom_call" | custom-call | tf_op jit(solution)/shard_map/moe_layer/pallas_call | solution.py:1103
  732.6 16.3 %fusion.99.refs_6_ = f32[2048,1024]{1,0:T(8,128)} fusion(bf16[2304,2048]{1,0:T(8,128)(2,1)} %get-tuple-element.71, bf16[2304,1024]{1,0:T(8,128)(2,1)} %get-tuple-element.73), kind=kOutput, calls=%fused_computation.205 | convolution fusion | flops 9663676416 | bytes 22544384 | tf_op jit(solution)/shard_map/dot_general | solution.py:61
  748.9 14.0 %fusion.98.refs_5_ = f32[2048,1024]{1,0:T(8,128)} fusion(bf16[2304,2048]{1,0:T(8,128)(2,1)S(1)} %copy-done.92, bf16[2304,1024]{1,0:T(8,128)(2,1)} %get-tuple-element.72), kind=kOutput, calls=%fused_computation.204 | convolution fusion | flops 9663676416 | bytes 22544384 | tf_op jit(solution)/shard_map/dot_general | solution.py:61
  762.9 63.3 %collective-permute-start.3 = (bf16[528,2048]{1,0:T(8,128)(2,1)S(1)}, bf16[528,2048]{1,0:T(8,128)(2,1)S(1)}, u32[]{:S(2)}, u32[]{:S(2)}) collective-permute-start(bf16[528,2048]{1,0:T(8,128)(2,1)S(1)} %copy-done.40), channel_id=1, source_target_pairs={{0,1},{1,0},{2,3},{3,2},{4,5},{5,4},{6,7},{7,6},{8,9},{9,8},{10,11... | collective-permute-start | bytes 6488072 | tf_op jit(solution)/shard_map/ppermute | solution.py:102
  832.5 12.6 %fusion.100.refs_7_ = f32[1024,2048]{1,0:T(8,128)} fusion(bf16[2304,1024]{1,0:T(8,128)(2,1)S(1)} %copy-done.93, bf16[2304,2048]{1,0:T(8,128)(2,1)S(1)} %bitcast.243), kind=kOutput, calls=%fused_computation.206 | convolution fusion | flops 9663676416 | bytes 22544384 | tf_op jit(solution)/shard_map/dot_general | solution.py:61
  857.3 6.2 fusion.47
  863.5 14.8 %multiply_convert_fusion = bf16[8,512,512]{1,2,0:T(8,128)(2,1)} fusion(f32[8,512,512]{1,2,0:T(8,128)} %fusion.47, f32[8,512]{1,0:T(8,128)S(1)} %copy-done.83, pred[512]{0:T(512)(128)(4,1)S(1)} %copy-done.85, bf16[512,8,64]{2,0,1:T(8,128)(2,1)S(1)} %copy-done.23, bf16[512,8,64]{2,0,1:T(8,128)(2,1)} %copy-done.24, bf16[512,8,64]{2,0,1:T(8,128)(2,1)S(1)} %copy-done.21, ...), kind=kOutput, calls=%fused_computation.1 | convolution fusion | flops 1103106560 | bytes 14696960 | tf_op jit(solution)/shard_map/sub | solution.py:1341
  878.3 4.4 multiply_bitcast_fusion.1
  898.8 4.4 fusion.102
  917.7 4.9 add_convert_fusion.3
  922.7 17.4 %collective-permute-start.5 = (bf16[512,2048]{1,0:T(8,128)(2,1)}, bf16[512,2048]{1,0:T(8,128)(2,1)}, u32[]{:S(2)}, u32[]{:S(2)}) collective-permute-start(bf16[512,2048]{1,0:T(8,128)(2,1)} %add_convert_fusion.3), channel_id=1, source_target_pairs={{0,0},{1,9},{2,2},{3,11},{4,4},{5,13},{6,6},{7,15},{8,8},{9,1},{10... | collective-permute-start | bytes 6291464 | tf_op jit(solution)/shard_map/ppermute | solution.py:98
  940.2 4.3 add_convert_fusion.4
  946.4 4.5 convolution_convert_fusion.2.refs_1_
  950.9 4.6 convolution_convert_fusion.1.refs_2_
  955.5 4.5 convolution_convert_fusion.3.refs_0_
  960.0 4.4 convolution_convert_fusion.refs_3_
  969.1 162.8 %reduce_all.1 = (f32[128,1024]{1,0:T(8,128)}, f32[128,1024]{1,0:T(8,128)}, f32[128,1024]{1,0:T(8,128)}, f32[128,1024]{1,0:T(8,128)}, f32[24,128]{1,0:T(8,128)}, ...) custom-call(bf16[2048,1024]{1,0:T(8,128)(2,1)} %convolution_convert_fusion.3.refs_0_, ...), custom_call_target="tpu_custom_call" | custom-call | tf_op jit(solution)/shard_map/reduce_all/pallas_call | solution.py:615
  1135.8 6.7 add_bitcast_fusion
  1154.4 5.2 fusion.19
  (352 shorter events, 129.2 us)
Async XLA Ops:
  1.4 342.3 %copy-start.84 = (pred[512]{0:T(512)(128)(4,1)}, pred[512]{0:T(512)(128)(4,1)S(1)}, u32[]{:S(2)}) copy-start(pred[512]{0:T(512)(128)(4,1)S(1)} %iota_compare_fusion.4) | copy-start | bytes 1540
  15.2 298.8 %copy-start.6 = (bf16[512,2048]{1,0:T(8,128)(2,1)S(1)}, bf16[512,2048]{1,0:T(8,128)(2,1)}, u32[]{:S(2)}) copy-start(bf16[512,2048]{1,0:T(8,128)(2,1)} %param.16) | copy-start | bytes 6291460
  313.1 50.4 %copy-start.69 = (f32[16,1,128]{2,1,0:T(1,128)}, f32[16,1,128]{2,1,0:T(1,128)S(1)}, u32[]{:S(2)}) copy-start(f32[16,1,128]{2,1,0:T(1,128)S(1)} %get-tuple-element.122) | copy-start | bytes 24580
  321.6 30.5 %copy-start.65 = (f32[512,8]{0,1:T(8,128)}, f32[512,8]{0,1:T(8,128)S(1)}, u32[]{:S(2)}) copy-start(f32[512,8]{0,1:T(8,128)S(1)} %add_rsqrt_fusion) | copy-start | bytes 49156
  321.7 32.0 %copy-start.88 = (f32[128]{0:T(128)}, f32[128]{0:T(128)S(1)}, u32[]{:S(2)}) copy-start(f32[128]{0:T(128)S(1)} %reshape.330) | copy-start | bytes 1540
  328.8 24.1 %copy-start.63 = (f32[512,8]{0,1:T(8,128)}, f32[512,8]{0,1:T(8,128)S(1)}, u32[]{:S(2)}) copy-start(f32[512,8]{0,1:T(8,128)S(1)} %add_rsqrt_fusion.1) | copy-start | bytes 49156
  328.9 25.5 %copy-start.86 = (f32[128]{0:T(128)}, f32[128]{0:T(128)S(1)}, u32[]{:S(2)}) copy-start(f32[128]{0:T(128)S(1)} %reshape.329) | copy-start | bytes 1540
  351.4 7.8 collective-permute-start
  732.5 99.9 %slice-start.6 = ((s8[9437184]{0:T(1024)(128)(4,1)}), s8[4194304]{0:T(1024)(128)(4,1)S(1)}, s32[]{:S(2)}) async-start(s8[9437184]{0:T(1024)(128)(4,1)} %bitcast.242), calls=%async_computation.6 | async-start | bytes 8388608
  732.5 99.9 %slice-start.7 = ((s8[9437184]{0:T(1024)(128)(4,1)}), s8[4194304]{0:T(1024)(128)(4,1)S(1)}, s32[]{:S(2)}) async-start(s8[9437184]{0:T(1024)(128)(4,1)} %bitcast.242), calls=%async_computation.7 | async-start | bytes 8388608
  748.8 77.4 %copy-start.43 = (bf16[512,2048]{1,0:T(8,128)(2,1)S(1)}, bf16[512,2048]{1,0:T(8,128)(2,1)}, u32[]{:S(2)}) copy-start(bf16[512,2048]{1,0:T(8,128)(2,1)} %get-tuple-element.68) | copy-start | bytes 6291460
  748.8 77.4 %copy-start.44 = (bf16[512,2048]{1,0:T(8,128)(2,1)S(1)}, bf16[512,2048]{1,0:T(8,128)(2,1)}, u32[]{:S(2)}) copy-start(bf16[512,2048]{1,0:T(8,128)(2,1)} %get-tuple-element.69) | copy-start | bytes 6291460
  748.8 83.6 %slice-start.8 = ((s8[9437184]{0:T(1024)(128)(4,1)}), s8[1048576]{0:T(1024)(128)(4,1)S(1)}, s32[]{:S(2)}) async-start(s8[9437184]{0:T(1024)(128)(4,1)} %bitcast.242), calls=%async_computation.8 | async-start | bytes 2097152
  762.9 66.4 %copy-start.41 = (bf16[512,2048]{1,0:T(8,128)(2,1)S(1)}, bf16[512,2048]{1,0:T(8,128)(2,1)}, u32[]{:S(2)}) copy-start(bf16[512,2048]{1,0:T(8,128)(2,1)} %get-tuple-element.66) | copy-start | bytes 6291460
  762.9 66.4 %copy-start.42 = (bf16[512,2048]{1,0:T(8,128)(2,1)S(1)}, bf16[512,2048]{1,0:T(8,128)(2,1)}, u32[]{:S(2)}) copy-start(bf16[512,2048]{1,0:T(8,128)(2,1)} %get-tuple-element.67) | copy-start | bytes 6291460
  762.9 82.2 %collective-permute-start.3 = (bf16[528,2048]{1,0:T(8,128)(2,1)S(1)}, bf16[528,2048]{1,0:T(8,128)(2,1)S(1)}, u32[]{:S(2)}, u32[]{:S(2)}) collective-permute-start(bf16[528,2048]{1,0:T(8,128)(2,1)S(1)} %copy-done.40), channel_id=1, source_target_pairs={{0,1},{1,0},{2,3},{3,2},{4,5},{5,4},{6,7},{7,6},{8,9},{9,8},{10,11... | collective-permute-start | bytes 6488072 | tf_op jit(solution)/shard_map/ppermute | solution.py:102
  828.3 50.0 %collective-permute-start.2 = (bf16[512,2048]{1,0:T(8,128)(2,1)}, bf16[512,2048]{1,0:T(8,128)(2,1)}, u32[]{:S(2)}, u32[]{:S(2)}) collective-permute-start(bf16[512,2048]{1,0:T(8,128)(2,1)} %add_convert_fusion.5), channel_id=1, source_target_pairs={{0,2},{1,5},{2,0},{3,7},{4,6},{5,1},{6,4},{7,3},{8,10},{9,13},{10,... | collective-permute-start | bytes 6291464 | tf_op jit(solution)/shard_map/ppermute | solution.py:98
  831.5 46.8 %collective-permute-start.1 = (bf16[512,2048]{1,0:T(8,128)(2,1)}, bf16[512,2048]{1,0:T(8,128)(2,1)}, u32[]{:S(2)}, u32[]{:S(2)}) collective-permute-start(bf16[512,2048]{1,0:T(8,128)(2,1)} %add_convert_fusion.6), channel_id=1, source_target_pairs={{0,2},{1,5},{2,0},{3,7},{4,6},{5,1},{6,4},{7,3},{8,10},{9,13},{10,... | collective-permute-start | bytes 6291464 | tf_op jit(solution)/shard_map/ppermute | solution.py:98
  917.5 46.9 %collective-permute-start.6 = (bf16[512,2048]{1,0:T(8,128)(2,1)}, bf16[512,2048]{1,0:T(8,128)(2,1)}, u32[]{:S(2)}, u32[]{:S(2)}) collective-permute-start(bf16[512,2048]{1,0:T(8,128)(2,1)} %add_convert_fusion.2), channel_id=1, source_target_pairs={{0,1},{1,0},{2,3},{3,2},{4,5},{5,4},{6,7},{7,6},{8,9},{9,8},{10,11... | collective-permute-start | bytes 6291464 | tf_op jit(solution)/shard_map/ppermute | solution.py:102
  917.7 22.4 %copy-start.45 = (bf16[512,2048]{1,0:T(8,128)(2,1)S(1)}, bf16[512,2048]{1,0:T(8,128)(2,1)}, u32[]{:S(2)}) copy-start(bf16[512,2048]{1,0:T(8,128)(2,1)} %get-tuple-element.64) | copy-start | bytes 6291460
  917.7 22.4 %copy-start.46 = (bf16[512,2048]{1,0:T(8,128)(2,1)S(1)}, bf16[512,2048]{1,0:T(8,128)(2,1)}, u32[]{:S(2)}) copy-start(bf16[512,2048]{1,0:T(8,128)(2,1)} %get-tuple-element.65) | copy-start | bytes 6291460
  922.7 209.2 %collective-permute-start.5 = (bf16[512,2048]{1,0:T(8,128)(2,1)}, bf16[512,2048]{1,0:T(8,128)(2,1)}, u32[]{:S(2)}, u32[]{:S(2)}) collective-permute-start(bf16[512,2048]{1,0:T(8,128)(2,1)} %add_convert_fusion.3), channel_id=1, source_target_pairs={{0,0},{1,9},{2,2},{3,11},{4,4},{5,13},{6,6},{7,15},{8,8},{9,1},{10... | collective-permute-start | bytes 6291464 | tf_op jit(solution)/shard_map/ppermute | solution.py:98
  944.5 187.5 %collective-permute-start.4 = (bf16[512,2048]{1,0:T(8,128)(2,1)}, bf16[512,2048]{1,0:T(8,128)(2,1)}, u32[]{:S(2)}, u32[]{:S(2)}) collective-permute-start(bf16[512,2048]{1,0:T(8,128)(2,1)} %add_convert_fusion.4), channel_id=1, source_target_pairs={{0,24},{1,17},{2,26},{3,19},{4,28},{5,21},{6,30},{7,23},{8,16},{9,... | collective-permute-start | bytes 6291464 | tf_op jit(solution)/shard_map/ppermute | solution.py:98
  1145.8 13.8 %collective-permute-start.7 = (bf16[512,2048]{1,0:T(8,128)(2,1)S(1)}, bf16[512,2048]{1,0:T(8,128)(2,1)}, u32[]{:S(2)}, u32[]{:S(2)}) collective-permute-start(bf16[512,2048]{1,0:T(8,128)(2,1)S(1)} %add_convert_fusion.1), channel_id=1, source_target_pairs={{0,1},{1,0},{2,3},{3,2},{4,5},{5,4},{6,7},{7,6},{8,9},{9,8},{10,11... | collective-permute-start | bytes 6291464 | tf_op jit(solution)/shard_map/ppermute | solution.py:102
  (97 other events, 425.7 us)
